TPU v7x, 128 devices: a whole 4x4x4 slice. The times are simulated.
128 devices in a mesh: req: 32 (over z, x, core), tp: 4 (over y).
Axes of the slice: x: 4, y: 4, z: 4, core: 2. Of those that a mesh axis runs over, the one named last changes fastest.
Arguments:
- tokens: bfloat16 [32768, 1280], P('req'), may hold values from -14 to 14
- segments: int32 [32768], P('req'), may hold values from 0 to 30, never falling along the last dimension, each value on 1 to 2048 neighbouring positions
- attend_gain: bfloat16 [1280], replicated, may hold values from 0.25 to 1.75
- attend_weight: bfloat16 [1280, 3, 1280], P(None, None, 'tp'), may hold values from -1 to 1
- output_weight: bfloat16 [1280, 1280], P('tp'), may hold values from -0.15625 to 0.15625
- mixer_gain: bfloat16 [1280], replicated, may hold values from 0.25 to 1.75
- expand_weight: bfloat16 [1280, 5120], P(None, 'tp'), may hold values from -0.15625 to 0.15625
- reduce_weight: bfloat16 [5120, 1280], P('tp'), may hold values from -0.078125 to 0.078125
- output_gain: bfloat16 [1280], replicated, may hold values from 0.25 to 1.75
- merge_weight: bfloat16 [5120, 1280], P(None, 'tp'), may hold values from -0.078125 to 0.078125
- merge_index: int32 [8192, 4], P('req'), may hold values from 0 to 32767, as said below
- owners: int32 [8192, 1], P('req'), may hold values from 0 to 31; in each aligned block of 256 rows (0 to 255, 256 to 511, ...) at most 16 rows name the same one
Outputs:
- owned: bfloat16 [32, 32, 16, 1280], P('req', None, None, 'tp')
Inputs may be any that keep to these rules, and one draw needn't show every extreme that they name: segments never fall along the tokens; every image has at most 2048 tokens. `merge_index`: merged rows 256 * j to 256 * (j + 1) - 1 name the tokens 1024 * j to 1024 * (j + 1) - 1, each exactly once. `owners`: within the rows of one index of req each owner is named at most 16 times.
All inputs are finite; a program needn't handle non-finite values.
Results may differ from a plain program's by a relative error of at most 0.014.
Values may be sent and summed in bfloat16 or wider, within the bound.
A program may use at most 128 MiB of HBM per device.

v0:
```python
import functools
import math

import jax
import jax.numpy as jnp
from jax import lax
from jax.experimental import pallas as pl
from jax.experimental.pallas import tpu as pltpu
from jax.sharding import PartitionSpec as P

HD = 80
TILE = 256
MESH_IDS = pl.DeviceIdType.MESH


def project_kernel(order, ctx_ref, weight_ref, tokens_ref, out_ref, slots, send_sem, recv_sem):
    n = slots.shape[0]
    rows, width = ctx_ref.shape
    cols = out_ref.shape[1]
    me = lax.axis_index("tp")
    place = {"tp": me, "req": lax.axis_index("req")}

    def peer(k):
        where = dict(place, tp=lax.rem(me + k, n))
        return tuple(where[a] for a in order)

    barrier = pltpu.get_barrier_semaphore()
    for k in range(1, n):
        pl.semaphore_signal(barrier, inc=1, device_id=peer(k), device_id_type=MESH_IDS)
    pl.semaphore_wait(barrier, n - 1)
    copies = []
    for k in range(1, n):
        copy = pltpu.make_async_remote_copy(
            src_ref=ctx_ref,
            dst_ref=slots.at[k],
            send_sem=send_sem.at[k],
            recv_sem=recv_sem.at[k],
            device_id=peer(k),
            device_id_type=MESH_IDS,
        )
        copy.start()
        copies.append(copy)
    tile = 256

    def add_term(block, source, first):
        base = pl.multiple_of(source * width, 8)

        @pl.loop(0, rows // tile)
        def _(i):
            r = pl.ds(pl.multiple_of(i * tile, tile), tile)

            @pl.loop(0, cols // tile)
            def _(j):
                c = pl.ds(pl.multiple_of(j * tile, tile), tile)
                term = jnp.dot(
                    block[r, :], weight_ref[pl.ds(base, width), c], preferred_element_type=jnp.float32
                )
                term = term.astype(jnp.bfloat16).astype(jnp.float32)
                if first:
                    out_ref[r, c] = term
                else:
                    out_ref[r, c] = out_ref[r, c] + term

    add_term(ctx_ref, me, True)
    for k in range(1, n):
        copies[k - 1].wait_recv()
        add_term(slots.at[k], lax.rem(me - k + n, n), False)

    @pl.loop(0, rows // tile)
    def _(i):
        r = pl.ds(pl.multiple_of(i * tile, tile), tile)
        out_ref[r, :] = out_ref[r, :] + tokens_ref[r, :].astype(jnp.float32)

    for copy in copies:
        copy.wait_send()


def project(context, weight, tokens, order):
    n = weight.shape[0] // context.shape[1]
    rows, cols = tokens.shape
    return pl.pallas_call(
        functools.partial(project_kernel, order),
        out_shape=jax.ShapeDtypeStruct((rows, cols), jnp.float32),
        in_specs=[pl.BlockSpec(memory_space=pltpu.VMEM)] * 3,
        out_specs=pl.BlockSpec(memory_space=pltpu.VMEM),
        scratch_shapes=[
            pltpu.VMEM((n,) + context.shape, context.dtype),
            pltpu.SemaphoreType.DMA((n,)),
            pltpu.SemaphoreType.DMA((n,)),
        ],
        compiler_params=pltpu.CompilerParams(
            collective_id=0, has_side_effects=True, vmem_limit_bytes=48 * 1024 * 1024
        ),
        cost_estimate=pl.CostEstimate(
            flops=2 * rows * cols * weight.shape[0],
            bytes_accessed=4 * rows * cols + 2 * weight.size + 2 * rows * cols + 2 * n * context.size,
            transcendentals=0,
        ),
    )(context, weight, tokens)


def shifted_2(block, axis, distance):
    devices = range(lax.axis_size(axis))
    route = [(i - distance, i) for i in devices if i - distance in devices]
    return lax.ppermute(block, axis, route)


def layer_norm(stream, gain):
    center = jnp.mean(stream, axis=-1, keepdims=True)
    shifted = stream - center
    spread = jnp.mean(shifted * shifted, axis=-1, keepdims=True)
    return shifted * lax.rsqrt(spread + 1e-06) * gain.astype(jnp.float32)


def flash_kernel(bounds, q_ref, qm_ref, k_ref, v_ref, km_ref, o_ref):
    i = pl.program_id(1)
    tile = TILE
    factor = 1.0 / math.sqrt(HD)
    q = q_ref[0]
    qm = qm_ref[...]

    def step(j, carry):
        running_max, running_sum, weighted = carry
        start = pl.multiple_of(j * tile, tile)
        keys = k_ref[0, pl.ds(start, tile), :]
        values = v_ref[0, pl.ds(start, tile), :]
        km = km_ref[:, pl.ds(start, tile)]
        scores = lax.dot_general(
            q, keys, (((1,), (1,)), ((), ())), preferred_element_type=jnp.float32
        ) * factor
        matches = qm == km
        new_max = jnp.maximum(
            running_max, jnp.max(jnp.where(matches, scores, -1e30), axis=1, keepdims=True)
        )
        probs = jnp.where(matches, jnp.exp(scores - new_max), 0.0)
        shrink = jnp.exp(running_max - new_max)
        new_sum = running_sum * shrink + jnp.sum(probs, axis=1, keepdims=True)
        new_weighted = weighted * shrink + jnp.dot(
            probs.astype(jnp.bfloat16), values, preferred_element_type=jnp.float32
        )
        return new_max, new_sum, new_weighted

    rows = q.shape[0]
    init = (
        jnp.full((rows, 1), -1e30, jnp.float32),
        jnp.zeros((rows, 1), jnp.float32),
        jnp.zeros((rows, q.shape[1]), jnp.float32),
    )
    _, total, weighted = lax.fori_loop(bounds[0, i], bounds[1, i], step, init)
    o_ref[0] = (weighted / total).astype(o_ref.dtype)


def attention(queries, query_marks, keys, values, key_marks):
    heads, rows, width = queries.shape
    key_rows = keys.shape[1]
    tiles = rows // TILE
    low = query_marks.reshape(tiles, TILE).min(axis=1)
    high = query_marks.reshape(tiles, TILE).max(axis=1)
    valid = (key_marks[None, :] >= low[:, None]) & (key_marks[None, :] <= high[:, None])
    first = jnp.argmax(valid, axis=1)
    last = key_rows - 1 - jnp.argmax(valid[:, ::-1], axis=1)
    bounds = jnp.stack([first // TILE, last // TILE + 1]).astype(jnp.int32)
    return pl.pallas_call(
        flash_kernel,
        out_shape=jax.ShapeDtypeStruct(queries.shape, queries.dtype),
        grid_spec=pltpu.PrefetchScalarGridSpec(
            num_scalar_prefetch=1,
            grid=(heads, tiles),
            in_specs=[
                pl.BlockSpec((1, TILE, width), lambda h, i, b: (h, i, 0)),
                pl.BlockSpec((TILE, 1), lambda h, i, b: (i, 0)),
                pl.BlockSpec((1, key_rows, width), lambda h, i, b: (h, 0, 0)),
                pl.BlockSpec((1, key_rows, width), lambda h, i, b: (h, 0, 0)),
                pl.BlockSpec((1, key_rows), lambda h, i, b: (0, 0)),
            ],
            out_specs=pl.BlockSpec((1, TILE, width), lambda h, i, b: (h, i, 0)),
        ),
        compiler_params=pltpu.CompilerParams(vmem_limit_bytes=48 * 1024 * 1024),
        cost_estimate=pl.CostEstimate(
            flops=4 * heads * rows * 2048 * width,
            bytes_accessed=2 * (queries.size * 2 + keys.size + values.size),
            transcendentals=heads * rows * 2048,
        ),
    )(bounds, queries, query_marks.reshape(rows, 1), keys, values, key_marks.reshape(1, key_rows))


def body(
    order,
    tokens,
    segments,
    attend_gain,
    attend_weight,
    output_weight,
    mixer_gain,
    expand_weight,
    reduce_weight,
    output_gain,
    merge_weight,
    merge_index,
    owners,
):
    token_rows = tokens.shape[0]
    head_width = attend_weight.shape[2]
    head_count = head_width // HD
    full_weight = lax.all_gather(output_weight, "tp", axis=0, tiled=True)
    stream = tokens.astype(jnp.float32)
    attend_in = layer_norm(stream, attend_gain).astype(jnp.bfloat16)
    projected = jnp.dot(
        attend_in,
        attend_weight.reshape(attend_weight.shape[0], 3 * head_width),
        preferred_element_type=jnp.float32,
    ).astype(jnp.bfloat16)
    key_value = projected[:, head_width:]
    marks = segments + 1
    near = {0: (key_value, marks)}
    for distance in (1, -1, 2, -2):
        near[distance] = shifted_2((key_value, marks), "req", distance)
    ordered = [near[d] for d in (2, 1, 0, -1, -2)]
    all_kv = jnp.concatenate([p for p, _ in ordered], axis=0)
    key_marks = jnp.concatenate([m for _, m in ordered], axis=0)

    def by_head(block):
        return jnp.transpose(block.reshape(block.shape[0], head_count, HD), (1, 0, 2))

    context = attention(
        by_head(projected[:, :head_width]),
        marks,
        by_head(all_kv[:, :head_width]),
        by_head(all_kv[:, head_width:]),
        key_marks,
    )
    context = jnp.transpose(context, (1, 0, 2)).reshape(token_rows, head_width)
    middle = project(context, full_weight, tokens, order)
    mixer_in = layer_norm(middle, mixer_gain).astype(jnp.bfloat16)
    expanded = jax.nn.gelu(
        jnp.dot(mixer_in, expand_weight, preferred_element_type=jnp.float32), approximate=False
    ).astype(jnp.bfloat16)
    hidden_terms = jnp.dot(expanded, reduce_weight, preferred_element_type=jnp.float32)
    final_stream = middle + lax.psum(hidden_terms.astype(jnp.bfloat16), "tp").astype(jnp.float32)
    final_normed = layer_norm(final_stream, output_gain).astype(jnp.bfloat16)
    merged_rows = merge_index.shape[0]
    local_index = merge_index - lax.axis_index("req") * token_rows
    merged = jnp.take(final_normed, local_index.reshape(-1), axis=0).reshape(
        merged_rows, 4 * final_normed.shape[1]
    )
    feature = jnp.dot(merged, merge_weight, preferred_element_type=jnp.float32).astype(jnp.bfloat16)
    peers = lax.axis_size("req")
    capacity = 2 * merged_rows // peers
    target = owners[:, 0]
    choose = (target[:, None] == jnp.arange(peers, dtype=jnp.int32)[None, :]).astype(jnp.int32)
    slot = jnp.sum((jnp.cumsum(choose, axis=0) - 1) * choose, axis=1)
    position = target * capacity + slot
    placement = (
        position[:, None] == jnp.arange(peers * capacity, dtype=jnp.int32)[None, :]
    ).astype(jnp.bfloat16)
    outgoing = jnp.einsum(
        "ms,mc->sc", placement, feature, preferred_element_type=jnp.float32
    ).astype(jnp.bfloat16)
    outgoing = outgoing.reshape(peers, capacity, feature.shape[1])
    received = lax.all_to_all(outgoing, "req", split_axis=0, concat_axis=0, tiled=True)
    return received.reshape(1, peers, capacity, feature.shape[1])


def solution(mesh):
    placed = (
        P("req", None),
        P("req"),
        P(),
        P(None, None, "tp"),
        P("tp", None),
        P(),
        P(None, "tp"),
        P("tp", None),
        P(),
        P(None, "tp"),
        P("req", None),
        P("req", None),
    )
    return jax.shard_map(
        functools.partial(body, tuple(mesh.axis_names)), mesh=mesh, in_specs=placed, out_specs=P("req", None, None, "tp"), check_vma=False
    )
```

profile of v0, /device:TPU:1, one launch (start us, length us, event | category | flops | bytes accessed | tf_op | source)
XLA Modules:
  0.0 396.0 jit_solution(4133756953164311484)
XLA Ops:
  7.4 4.2 %collective-permute-start = (s32[1024]{0:T(1024)S(1)}, s32[1024]{0:T(1024)S(1)}, u32[]{:S(2)}, u32[]{:S(2)}) collective-permute-start(s32[1024]{0:T(1024)S(1)} %broadcast_add_fusion), channel_id=1, source_target_pairs={{0,8},{4,12},{8,16},{12,20},{16,24},{20,28},{24,32},{28,36},{32,40... | collective-permute-start | bytes 12296 | tf_op jit(solution)/shard_map/ppermute | solution.py:105
  11.6 4.0 %collective-permute-start.1 = (s32[1024]{0:T(1024)S(1)}, s32[1024]{0:T(1024)S(1)}, u32[]{:S(2)}, u32[]{:S(2)}) collective-permute-start(s32[1024]{0:T(1024)S(1)} %broadcast_add_fusion), channel_id=1, source_target_pairs={{0,4},{4,8},{8,12},{12,16},{16,20},{20,24},{24,28},{28,32},{32,36}... | collective-permute-start | bytes 12296 | tf_op jit(solution)/shard_map/ppermute | solution.py:105
  15.6 1.9 collective-permute-start.2
  18.8 2.2 convert_reduce_fusion
  21.0 2.6 fusion.2
  23.6 2.9 fusion.27
  29.0 5.0 %collective-permute-start.4 = (bf16[1024,640]{0,1:T(8,128)(2,1)}, bf16[1024,640]{0,1:T(8,128)(2,1)}, u32[]{:S(2)}, u32[]{:S(2)}) collective-permute-start(bf16[1024,640]{0,1:T(8,128)(2,1)} %slice.28), channel_id=1, source_target_pairs={{0,8},{4,12},{8,16},{12,20},{16,24},{20,28},{24,32},{28,36},{32,40... | collective-permute-start | bytes 3932168 | tf_op jit(solution)/shard_map/ppermute | solution.py:105
  34.3 2.0 slice.27
  37.3 2.2 copy.28
  39.5 3.1 collective-permute-start.5
  42.7 2.2 collective-permute-start.6
  46.4 3.6 rev.3
  51.5 9.5 %collective-permute-done.4 = bf16[1024,640]{0,1:T(8,128)(2,1)} collective-permute-done((bf16[1024,640]{0,1:T(8,128)(2,1)}, bf16[1024,640]{0,1:T(8,128)(2,1)}, u32[]{:S(2)}, u32[]{:S(2)}) %collective-permute-start.4) | collective-permute-done | bytes 1310752 | tf_op jit(solution)/shard_map/ppermute | solution.py:105
  62.5 13.4 %collective-permute-done.5 = bf16[1024,640]{0,1:T(8,128)(2,1)} collective-permute-done((bf16[1024,640]{0,1:T(8,128)(2,1)}, bf16[1024,640]{0,1:T(8,128)(2,1)}, u32[]{:S(2)}, u32[]{:S(2)}) %collective-permute-start.5) | collective-permute-done | bytes 1310752 | tf_op jit(solution)/shard_map/ppermute | solution.py:105
  80.3 3.1 fusion.74
  83.4 6.4 %copy.29 = bf16[5120,4,80]{2,0,1:T(8,128)(2,1)} copy(bf16[5120,4,80]{0,2,1:T(8,128)(2,1)} %bitcast.49) | data formatting | bytes 6553600 | tf_op jit(solution)/shard_map/reshape | solution.py:223
  89.8 6.3 %copy.30 = bf16[5120,4,80]{2,0,1:T(8,128)(2,1)} copy(bf16[5120,4,80]{0,2,1:T(8,128)(2,1)} %bitcast.48) | data formatting | bytes 6553600 | tf_op jit(solution)/shard_map/reshape | solution.py:223
  98.4 61.3 %shard_map.118 = bf16[4,1024,80]{2,1,0:T(8,128)(2,1)S(1)} custom-call(s32[2,4]{1,0:T(2,128)S(1)} %pad_add_fusion.bounds, bf16[4,1024,80]{2,1,0:T(8,128)(2,1)S(1)} %bitcast.43, s32[1024,1]{1,0:T(8,128)S(1)} %copy-done.7, bf16[4,5120,80]{2,1,0:T(8,128)(2,1)} %bitcast.51, bf16[4,5120,80]{2,1,0:T(8,128)(2,1)} %bitcast.52, s32[1,5120]{1,0:T(1,128)S(1)} %bitcast.45), custom_call_target="tpu_custom_call" | custom-call | flops 2684354560 | bytes 7864320 | tf_op jit(solution)/shard_map/pallas_call | solution.py:163
  160.7 2.2 copy.32
  162.8 2.2 copy.33.ctx_ref
  167.9 37.0 %shard_map.119 = f32[1024,1280]{1,0:T(8,128)} custom-call(bf16[1024,320]{1,0:T(8,128)(2,1)S(1)} %copy-done.6, bf16[1280,1280]{1,0:T(8,128)(2,1)} %all-gather.2.cloned.1.call-done.weight_ref, bf16[1024,1280]{1,0:T(8,128)(2,1)S(1)} %copy-done.3), custom_call_target="tpu_custom_call" | custom-call | flops 3355443200 | bytes 13762560 | tf_op jit(solution)/shard_map/pallas_call | solution.py:81
  205.0 2.8 reduce_sum.69
  207.8 3.1 multiply_reduce_fusion.1
  211.0 20.9 %convolution_convert_fusion = bf16[1024,1280]{1,0:T(8,128)(2,1)} fusion(bf16[1280,1280]{1,0:T(8,128)(2,1)S(1)} %copy-done, bf16[1280,1280]{1,0:T(8,128)(2,1)} %param.18, f32[1024,1280]{1,0:T(8,128)} %shard_map.119, f32[1280]{0:T(1024)S(1)} %convert_element_type.50, f32[1024]{0:T(1024)S(1)} %add_rsqrt_fusion.1, f32[1024]{0:T(1024)S(1)} %broadcast_multiply_fusion.1), kind=kOutput, calls=%fused_computation.32 | convolution fusion | flops 6802636800 | bytes 14431232 | tf_op jit(solution)/shard_map/dot_general | solution.py:238
  235.9 107.4 %all-reduce.2.cloned.1.call-done = bf16[1024,1280]{1,0:T(8,128)(2,1)} async-done(((bf16[1024,1280]{1,0:T(8,128)(2,1)}), bf16[1024,1280]{1,0:T(8,128)(2,1)}) %all-reduce.2.cloned.1.call-update) | async-done | bytes 2621456 | tf_op jit(solution)/shard_map/psum | solution.py:239
  343.3 4.0 %fusion.26 = f32[1024]{0:T(1024)S(1)} fusion(f32[1024,1280]{1,0:T(8,128)} %shard_map.119, bf16[1024,1280]{1,0:T(8,128)(2,1)} %all-reduce.2.cloned.1.call-done), kind=kLoop, calls=%fused_computation.43 | loop fusion | flops 3931136 | bytes 7868416 | tf_op jit(solution)/shard_map/reduce_sum | solution.py:109
  347.4 3.7 multiply_reduce_fusion
  352.7 5.5 %gather_fusion = bf16[1024,1280]{1,0:T(8,128)(2,1)} fusion(bf16[1024,1280]{1,0:T(8,128)(2,1)S(1)} %multiply_convert_fusion, s32[1024]{0:T(1024)S(1)} %broadcast_clamp_fusion), kind=kCustom, calls=%fused_computation | custom fusion | bytes 5246976 | tf_op jit(solution)/shard_map/jit(_take)/gather | solution.py:243
  358.1 5.2 %gather.7 = bf16[256,5120]{1,0:T(8,128)(2,1)} reshape(bf16[1024,1280]{1,0:T(8,128)(2,1)} %gather_fusion) | data formatting | bytes 5242880 | tf_op jit(solution)/shard_map/jit(_take)/gather | solution.py:243
  363.4 5.3 %convolution_convert_fusion.1 = bf16[512,320]{0,1:T(8,128)(2,1)} fusion(bf16[5120,320]{0,1:T(8,128)(2,1)} %param.21, pred[256,5120]{1,0:T(8,128)(4,1)} %bitcast.57, bf16[256,5120]{1,0:T(8,128)(2,1)} %gather.7, s32[256]{0:T(256)S(1)} %bitcast.63), kind=kOutput, calls=%fused_computation.46 | convolution fusion | flops 924434432 | bytes 7537664 | tf_op jit(solution)/shard_map/ms,mc->sc/dot_general | solution.py:256
  368.7 1.9 copy.35
  370.6 17.8 %all_to_all.5 = bf16[32,16,320]{2,1,0:T(8,128)(2,1)S(1)} all-to-all(bf16[32,16,320]{2,1,0:T(8,128)(2,1)} %bitcast.56), channel_id=1, replica_groups=mesh['req'=32,'tp'=4] {'req'}, dimensions={0} | all-to-all | bytes 655360 | tf_op jit(solution)/shard_map/all_to_all | solution.py:260
  (100 shorter events, 26.8 us)
Async XLA Ops:
  6.5 204.4 %copy-start = (bf16[1280,1280]{1,0:T(8,128)(2,1)S(1)}, bf16[1280,1280]{1,0:T(8,128)(2,1)}, u32[]{:S(2)}) copy-start(bf16[1280,1280]{1,0:T(8,128)(2,1)} %param.19) | copy-start | bytes 9830404
  6.5 17.0 %copy-start.13 = (bf16[1280]{0:T(1024)(128)(2,1)S(1)}, bf16[1280]{0:T(1024)(128)(2,1)}, u32[]{:S(2)}) copy-start(bf16[1280]{0:T(1024)(128)(2,1)} %param.14) | copy-start | bytes 7684
  6.5 158.5 %all-gather.2.cloned.1.call-start = ((), (), s32[]{:S(2)}) async-start(), calls=%async_computation.1 | async-start | bytes 4096000 | tf_op jit(solution)/shard_map/all_gather | solution.py:205
  6.5 17.0 %copy-start.2 = (bf16[1024,1280]{1,0:T(8,128)(2,1)S(1)}, bf16[1024,1280]{1,0:T(8,128)(2,1)}, u32[]{:S(2)}) copy-start(bf16[1024,1280]{1,0:T(8,128)(2,1)} %tokens_ref.1) | copy-start | bytes 7864324
  6.5 17.0 %copy-start.17 = (bf16[1280,3,320]{0,2,1:T(8,128)(2,1)S(1)}, bf16[1280,3,320]{0,2,1:T(8,128)(2,1)}, u32[]{:S(2)}) copy-start(bf16[1280,3,320]{0,2,1:T(8,128)(2,1)} %param.15) | copy-start | bytes 7372804
  7.4 32.1 %collective-permute-start = (s32[1024]{0:T(1024)S(1)}, s32[1024]{0:T(1024)S(1)}, u32[]{:S(2)}, u32[]{:S(2)}) collective-permute-start(s32[1024]{0:T(1024)S(1)} %broadcast_add_fusion), channel_id=1, source_target_pairs={{0,8},{4,12},{8,16},{12,20},{16,24},{20,28},{24,32},{28,36},{32,40... | collective-permute-start | bytes 12296 | tf_op jit(solution)/shard_map/ppermute | solution.py:105
  11.6 31.1 %collective-permute-start.1 = (s32[1024]{0:T(1024)S(1)}, s32[1024]{0:T(1024)S(1)}, u32[]{:S(2)}, u32[]{:S(2)}) collective-permute-start(s32[1024]{0:T(1024)S(1)} %broadcast_add_fusion), channel_id=1, source_target_pairs={{0,4},{4,8},{8,12},{12,16},{16,20},{20,24},{24,28},{28,32},{32,36}... | collective-permute-start | bytes 12296 | tf_op jit(solution)/shard_map/ppermute | solution.py:105
  15.6 29.4 %collective-permute-start.2 = (s32[1024]{0:T(1024)S(1)}, s32[1024]{0:T(1024)S(1)}, u32[]{:S(2)}, u32[]{:S(2)}) collective-permute-start(s32[1024]{0:T(1024)S(1)} %broadcast_add_fusion), channel_id=1, source_target_pairs={{4,0},{8,4},{12,8},{16,12},{20,16},{24,20},{28,24},{32,28},{36,32}... | collective-permute-start | bytes 12296 | tf_op jit(solution)/shard_map/ppermute | solution.py:105
  17.5 28.8 %collective-permute-start.3 = (s32[1024]{0:T(1024)S(1)}, s32[1024]{0:T(1024)S(1)}, u32[]{:S(2)}, u32[]{:S(2)}) collective-permute-start(s32[1024]{0:T(1024)S(1)} %broadcast_add_fusion), channel_id=1, source_target_pairs={{8,0},{12,4},{16,8},{20,12},{24,16},{28,20},{32,24},{36,28},{40,32... | collective-permute-start | bytes 12296 | tf_op jit(solution)/shard_map/ppermute | solution.py:105
  26.5 1.3 copy-start.9
  27.8 11.7 %copy-start.14 = (bf16[1280]{0:T(1024)(128)(2,1)S(1)}, bf16[1280]{0:T(1024)(128)(2,1)}, u32[]{:S(2)}) copy-start(bf16[1280]{0:T(1024)(128)(2,1)} %param.17) | copy-start | bytes 7684
  27.8 17.1 %copy-start.11 = (s32[1024]{0:T(1024)S(1)}, s32[1024]{0:T(1024)}, u32[]{:S(2)}) copy-start(s32[1024]{0:T(1024)} %param.13) | copy-start | bytes 12292
  29.0 32.0 %collective-permute-start.4 = (bf16[1024,640]{0,1:T(8,128)(2,1)}, bf16[1024,640]{0,1:T(8,128)(2,1)}, u32[]{:S(2)}, u32[]{:S(2)}) collective-permute-start(bf16[1024,640]{0,1:T(8,128)(2,1)} %slice.28), channel_id=1, source_target_pairs={{0,8},{4,12},{8,16},{12,20},{16,24},{20,28},{24,32},{28,36},{32,40... | collective-permute-start | bytes 3932168 | tf_op jit(solution)/shard_map/ppermute | solution.py:105
  34.1 309.3 %all-reduce.2.cloned.1.call-start = ((), (), s32[]{:S(2)}) async-start(), calls=%async_computation.2 | async-start | bytes 5242880 | tf_op jit(solution)/shard_map/psum | solution.py:239
  39.5 36.4 %collective-permute-start.5 = (bf16[1024,640]{0,1:T(8,128)(2,1)}, bf16[1024,640]{0,1:T(8,128)(2,1)}, u32[]{:S(2)}, u32[]{:S(2)}) collective-permute-start(bf16[1024,640]{0,1:T(8,128)(2,1)} %slice.28), channel_id=1, source_target_pairs={{0,4},{4,8},{8,12},{12,16},{16,20},{20,24},{24,28},{28,32},{32,36}... | collective-permute-start | bytes 3932168 | tf_op jit(solution)/shard_map/ppermute | solution.py:105
  42.7 34.7 %collective-permute-start.6 = (bf16[1024,640]{0,1:T(8,128)(2,1)}, bf16[1024,640]{0,1:T(8,128)(2,1)}, u32[]{:S(2)}, u32[]{:S(2)}) collective-permute-start(bf16[1024,640]{0,1:T(8,128)(2,1)} %slice.28), channel_id=1, source_target_pairs={{4,0},{8,4},{12,8},{16,12},{20,16},{24,20},{28,24},{32,28},{36,32}... | collective-permute-start | bytes 3932168 | tf_op jit(solution)/shard_map/ppermute | solution.py:105
  45.0 33.9 %collective-permute-start.7 = (bf16[1024,640]{0,1:T(8,128)(2,1)}, bf16[1024,640]{0,1:T(8,128)(2,1)}, u32[]{:S(2)}, u32[]{:S(2)}) collective-permute-start(bf16[1024,640]{0,1:T(8,128)(2,1)} %slice.28), channel_id=1, source_target_pairs={{8,0},{12,4},{16,8},{20,12},{24,16},{28,20},{32,24},{36,28},{40,32... | collective-permute-start | bytes 3932168 | tf_op jit(solution)/shard_map/ppermute | solution.py:105
  50.1 27.2 %copy-start.10 = (bf16[1024,960]{0,1:T(8,128)(2,1)S(1)}, bf16[1024,960]{0,1:T(8,128)(2,1)}, u32[]{:S(2)}) copy-start(bf16[1024,960]{0,1:T(8,128)(2,1)} %copy-done.9) | copy-start | bytes 5898244
  96.1 1.2 copy-start.4
  97.4 1.0 copy-start.7
  159.7 1.0 copy-start.5
  165.1 1.7 copy-start.3
  166.8 1.1 copy-start.6
  210.9 21.0 %copy-start.15 = (bf16[1280]{0:T(1024)(128)(2,1)S(1)}, bf16[1280]{0:T(1024)(128)(2,1)}, u32[]{:S(2)}) copy-start(bf16[1280]{0:T(1024)(128)(2,1)} %param.20) | copy-start | bytes 7684
  210.9 21.0 %copy-start.16 = (s32[256,4]{0,1:T(4,128)S(1)}, s32[256,4]{0,1:T(4,128)}, u32[]{:S(2)}) copy-start(s32[256,4]{0,1:T(4,128)} %param.22) | copy-start | bytes 12292
  210.9 21.3 %copy-start.12 = (s32[256,1]{0,1:T(1,128)S(1)}, s32[256,1]{0,1:T(1,128)}, u32[]{:S(2)}) copy-start(s32[256,1]{0,1:T(1,128)} %param.23) | copy-start | bytes 3076
  343.3 4.0 %copy-start.8 = (bf16[1024,1280]{1,0:T(8,128)(2,1)S(1)}, bf16[1024,1280]{1,0:T(8,128)(2,1)}, u32[]{:S(2)}) copy-start(bf16[1024,1280]{1,0:T(8,128)(2,1)} %all-reduce.2.cloned.1.call-done) | copy-start | bytes 7864324
  343.3 7.8 %slice-start = ((s8[5242880]{0:T(1024)(128)(4,1)}), s8[4194304]{0:T(1024)(128)(4,1)S(1)}, s32[]{:S(2)}) async-start(s8[5242880]{0:T(1024)(128)(4,1)} %bitcast.46), calls=%async_computation.3 | async-start | bytes 8388608
  347.4 3.8 slice-start.1
  363.4 25.8 %copy-start.1 = (bf16[1280,1280]{1,0:T(8,128)(2,1)S(1)}, bf16[1280,1280]{1,0:T(8,128)(2,1)}, u32[]{:S(2)}) copy-start(bf16[1280,1280]{1,0:T(8,128)(2,1)} %param.19) | copy-start | bytes 9830404
Sparse Core Ops, SparseCore 0:
  34.2 44.2 all-gather.1
  232.1 111.2 all-reduce.1
where the time goes:
time: 397 us; the launch traced here: 396 us
  waiting for transfers between devices  130 us (33%)
  Pallas kernels  98.3 us (25%)
  local copies, waits for them, and re-layouts  60 us (15%)
  matrix products  29.2 us (7%)
  other arithmetic  23.2 us (6%)
  starting transfers between devices  23.1 us (6%)
  blocking collectives  17.8 us (4%)
  between operations  13.9 us (4%)
    psum x1, waiting for transfers between devices, body(): lax.psum(hidden_terms.astype(jnp.bfloat16), 'tp').astype(jnp.float32)  107 us
    pallas_call x1, Pallas kernels, attention(): pl.pallas_call(flash_kernel, out_shape=jax.ShapeDtypeStruct(queries.shape...  61.3 us
    pallas_call x1, Pallas kernels, project(): pl.pallas_call(functools.partial(project_kernel, order), out_shape=jax.Sh...  37 us
    ppermute x8, starting transfers between devices, shifted_2(): return lax.ppermute(block, axis, route)  23.1 us
    ppermute x8, waiting for transfers between devices, shifted_2(): return lax.ppermute(block, axis, route)  23 us
    dot_general x1, matrix products, body(): jnp.dot(expanded, reduce_weight, preferred_element_type=jnp.float32)  20.9 us
    all_to_all x1, blocking collectives, body(): lax.all_to_all(outgoing, 'req', split_axis=0, concat_axis=0, tiled=True)  17.8 us
    reshape x3, local copies, waits for them, and re-layouts, by_head(): block.reshape(block.shape[0], head_count, HD)  14.9 us
  transfers between devices with their start and end apart: 10, of which 3 were waited for; matrix products, arithmetic and copies ran while one was open for 12% of the time, Pallas kernels for 15%

commit v1 on v0

--- a/solution.py
+++ b/solution.py
@@ -113,46 +113,47 @@
 
 
 def flash_kernel(bounds, q_ref, qm_ref, k_ref, v_ref, km_ref, o_ref):
-    i = pl.program_id(1)
+    i = pl.program_id(0)
     tile = TILE
     factor = 1.0 / math.sqrt(HD)
-    q = q_ref[0]
+    q = q_ref[...]
     qm = qm_ref[...]
 
     def step(j, carry):
         running_max, running_sum, weighted = carry
         start = pl.multiple_of(j * tile, tile)
-        keys = k_ref[0, pl.ds(start, tile), :]
-        values = v_ref[0, pl.ds(start, tile), :]
+        keys = k_ref[:, :, pl.ds(start, tile)]
+        values = v_ref[:, pl.ds(start, tile), :]
         km = km_ref[:, pl.ds(start, tile)]
         scores = lax.dot_general(
-            q, keys, (((1,), (1,)), ((), ())), preferred_element_type=jnp.float32
+            q, keys, (((2,), (1,)), ((0,), (0,))), preferred_element_type=jnp.float32
         ) * factor
-        matches = qm == km
+        matches = (qm == km)[None]
         new_max = jnp.maximum(
-            running_max, jnp.max(jnp.where(matches, scores, -1e30), axis=1, keepdims=True)
+            running_max, jnp.max(jnp.where(matches, scores, -1e30), axis=2, keepdims=True)
         )
         probs = jnp.where(matches, jnp.exp(scores - new_max), 0.0)
         shrink = jnp.exp(running_max - new_max)
-        new_sum = running_sum * shrink + jnp.sum(probs, axis=1, keepdims=True)
-        new_weighted = weighted * shrink + jnp.dot(
-            probs.astype(jnp.bfloat16), values, preferred_element_type=jnp.float32
+        new_sum = running_sum * shrink + jnp.sum(probs, axis=2, keepdims=True)
+        update = lax.dot_general(
+            probs.astype(jnp.bfloat16), values, (((2,), (1,)), ((0,), (0,))),
+            preferred_element_type=jnp.float32,
         )
-        return new_max, new_sum, new_weighted
-
-    rows = q.shape[0]
+        return new_max, new_sum, weighted * shrink + update
+
+    heads, rows, width = q.shape
     init = (
-        jnp.full((rows, 1), -1e30, jnp.float32),
-        jnp.zeros((rows, 1), jnp.float32),
-        jnp.zeros((rows, q.shape[1]), jnp.float32),
+        jnp.full((heads, rows, 1), -1e30, jnp.float32),
+        jnp.zeros((heads, rows, 1), jnp.float32),
+        jnp.zeros((heads, rows, width), jnp.float32),
     )
     _, total, weighted = lax.fori_loop(bounds[0, i], bounds[1, i], step, init)
-    o_ref[0] = (weighted / total).astype(o_ref.dtype)
+    o_ref[...] = (weighted / total).astype(o_ref.dtype)
 
 
 def attention(queries, query_marks, keys, values, key_marks):
     heads, rows, width = queries.shape
-    key_rows = keys.shape[1]
+    key_rows = keys.shape[2]
     tiles = rows // TILE
     low = query_marks.reshape(tiles, TILE).min(axis=1)
     high = query_marks.reshape(tiles, TILE).max(axis=1)
@@ -165,15 +166,15 @@
         out_shape=jax.ShapeDtypeStruct(queries.shape, queries.dtype),
         grid_spec=pltpu.PrefetchScalarGridSpec(
             num_scalar_prefetch=1,
-            grid=(heads, tiles),
+            grid=(tiles,),
             in_specs=[
-                pl.BlockSpec((1, TILE, width), lambda h, i, b: (h, i, 0)),
-                pl.BlockSpec((TILE, 1), lambda h, i, b: (i, 0)),
-                pl.BlockSpec((1, key_rows, width), lambda h, i, b: (h, 0, 0)),
-                pl.BlockSpec((1, key_rows, width), lambda h, i, b: (h, 0, 0)),
-                pl.BlockSpec((1, key_rows), lambda h, i, b: (0, 0)),
+                pl.BlockSpec((heads, TILE, width), lambda i, b: (0, i, 0)),
+                pl.BlockSpec((TILE, 1), lambda i, b: (i, 0)),
+                pl.BlockSpec((heads, width, key_rows), lambda i, b: (0, 0, 0)),
+                pl.BlockSpec((heads, key_rows, width), lambda i, b: (0, 0, 0)),
+                pl.BlockSpec((1, key_rows), lambda i, b: (0, 0)),
             ],
-            out_specs=pl.BlockSpec((1, TILE, width), lambda h, i, b: (h, i, 0)),
+            out_specs=pl.BlockSpec((heads, TILE, width), lambda i, b: (0, i, 0)),
         ),
         compiler_params=pltpu.CompilerParams(vmem_limit_bytes=48 * 1024 * 1024),
         cost_estimate=pl.CostEstimate(
@@ -225,7 +226,7 @@
     context = attention(
         by_head(projected[:, :head_width]),
         marks,
-        by_head(all_kv[:, :head_width]),
+        jnp.transpose(all_kv[:, :head_width].reshape(-1, head_count, HD), (1, 2, 0)),
         by_head(all_kv[:, head_width:]),
         key_marks,
     )

time: 397 us -> 349 us (0.88)
  waiting for transfers between devices: 130 us -> 98.1 us
  Pallas kernels: 98.3 us -> 87 us
  local copies, waits for them, and re-layouts: 60 us -> 55.6 us
    psum x1, waiting for transfers between devices: 107 us -> 75.1 us  [body(): lax.psum(hidden_terms.astype(jnp.bfloat16), 'tp').astype(jnp.float32)]
    pallas_call x1, Pallas kernels: 61.3 us -> 39.8 us  [attention(): pl.pallas_call(flash_kernel, out_shape=jax.ShapeDtypeStruct(queries.shape...]
    pallas_call x1, Pallas kernels: 37 us -> 47.2 us  [project(): pl.pallas_call(functools.partial(project_kernel, order), out_shape=jax.Sh...]
    reshape x3 -> x2, local copies, waits for them, and re-layouts: 14.9 us -> 8.57 us  [by_head(): block.reshape(block.shape[0], head_count, HD)]
    unnamed x49 -> x51, local copies, waits for them, and re-layouts: 14.3 us -> 16.2 us
  transfers between devices with their start and end apart: 10 -> 10, of which waited for: 3 -> 3; matrix products, arithmetic and copies ran while one was open for 12% -> 12% of each run, Pallas kernels for 15% -> 11%
where the time goes in v1:
time: 349 us; the launch traced here: 348 us
  waiting for transfers between devices  98.1 us (28%)
  Pallas kernels  87 us (25%)
  local copies, waits for them, and re-layouts  55.6 us (16%)
  matrix products  29.2 us (8%)
  other arithmetic  23.2 us (7%)
  starting transfers between devices  23.1 us (7%)
  blocking collectives  17.8 us (5%)
  between operations  13.9 us (4%)
    psum x1, waiting for transfers between devices, body(): lax.psum(hidden_terms.astype(jnp.bfloat16), 'tp').astype(jnp.float32)  75.1 us
    pallas_call x1, Pallas kernels, project(): pl.pallas_call(functools.partial(project_kernel, order), out_shape=jax.Sh...  47.2 us
    pallas_call x1, Pallas kernels, attention(): pl.pallas_call(flash_kernel, out_shape=jax.ShapeDtypeStruct(queries.shape...  39.8 us
    ppermute x8, starting transfers between devices, shifted_2(): return lax.ppermute(block, axis, route)  23 us
    ppermute x8, waiting for transfers between devices, shifted_2(): return lax.ppermute(block, axis, route)  23 us
    dot_general x1, matrix products, body(): jnp.dot(expanded, reduce_weight, preferred_element_type=jnp.float32)  20.9 us
    all_to_all x1, blocking collectives, body(): lax.all_to_all(outgoing, 'req', split_axis=0, concat_axis=0, tiled=True)  17.8 us
    unnamed x51, local copies, waits for them, and re-layouts  16.2 us
  transfers between devices with their start and end apart: 10, of which 3 were waited for; matrix products, arithmetic and copies ran while one was open for 12% of the time, Pallas kernels for 11%

profile of v1, /device:TPU:1, one launch (start us, length us, event | category | flops | bytes accessed | tf_op | source)
XLA Modules:
  0.0 348.1 jit_solution(4609153929794418345)
XLA Ops:
  7.4 4.2 %collective-permute-start = (s32[1024]{0:T(1024)S(1)}, s32[1024]{0:T(1024)S(1)}, u32[]{:S(2)}, u32[]{:S(2)}) collective-permute-start(s32[1024]{0:T(1024)S(1)} %broadcast_add_fusion), channel_id=1, source_target_pairs={{0,8},{4,12},{8,16},{12,20},{16,24},{20,28},{24,32},{28,36},{32,40... | collective-permute-start | bytes 12296 | tf_op jit(solution)/shard_map/ppermute | solution.py:105
  11.6 4.0 %collective-permute-start.1 = (s32[1024]{0:T(1024)S(1)}, s32[1024]{0:T(1024)S(1)}, u32[]{:S(2)}, u32[]{:S(2)}) collective-permute-start(s32[1024]{0:T(1024)S(1)} %broadcast_add_fusion), channel_id=1, source_target_pairs={{0,4},{4,8},{8,12},{12,16},{16,20},{20,24},{24,28},{28,32},{32,36}... | collective-permute-start | bytes 12296 | tf_op jit(solution)/shard_map/ppermute | solution.py:105
  15.6 1.9 collective-permute-start.2
  18.8 2.2 convert_reduce_fusion
  21.0 2.6 fusion.2
  23.6 2.9 fusion.27
  29.0 5.0 %collective-permute-start.4 = (bf16[1024,640]{0,1:T(8,128)(2,1)}, bf16[1024,640]{0,1:T(8,128)(2,1)}, u32[]{:S(2)}, u32[]{:S(2)}) collective-permute-start(bf16[1024,640]{0,1:T(8,128)(2,1)} %slice.28), channel_id=1, source_target_pairs={{0,8},{4,12},{8,16},{12,20},{16,24},{20,28},{24,32},{28,36},{32,40... | collective-permute-start | bytes 3932168 | tf_op jit(solution)/shard_map/ppermute | solution.py:105
  34.3 2.0 slice.27
  37.3 2.2 copy.27
  39.5 3.1 collective-permute-start.5
  42.7 2.2 collective-permute-start.6
  46.4 3.6 %rev.3 = pred[4,5120]{1,0:T(4,128)(4,1)S(1)} reverse(pred[4,5120]{1,0:T(4,128)(4,1)S(1)} %compare_and_fusion), dimensions={1} | reverse | bytes 40960 | tf_op jit(solution)/shard_map/rev | solution.py:162
  51.5 9.6 %collective-permute-done.4 = bf16[1024,640]{0,1:T(8,128)(2,1)} collective-permute-done((bf16[1024,640]{0,1:T(8,128)(2,1)}, bf16[1024,640]{0,1:T(8,128)(2,1)}, u32[]{:S(2)}, u32[]{:S(2)}) %collective-permute-start.4) | collective-permute-done | bytes 1310752 | tf_op jit(solution)/shard_map/ppermute | solution.py:105
  62.5 13.4 %collective-permute-done.5 = bf16[1024,640]{0,1:T(8,128)(2,1)} collective-permute-done((bf16[1024,640]{0,1:T(8,128)(2,1)}, bf16[1024,640]{0,1:T(8,128)(2,1)}, u32[]{:S(2)}, u32[]{:S(2)}) %collective-permute-start.5) | collective-permute-done | bytes 1310752 | tf_op jit(solution)/shard_map/ppermute | solution.py:105
  80.3 3.2 fusion.74
  83.5 6.4 %copy.28 = bf16[5120,4,80]{2,0,1:T(8,128)(2,1)} copy(bf16[5120,4,80]{0,2,1:T(8,128)(2,1)} %bitcast.50) | data formatting | bytes 6553600 | tf_op jit(solution)/shard_map/reshape | solution.py:224
  89.9 1.9 copy-done.4
  94.1 39.8 %shard_map.118 = bf16[4,1024,80]{2,1,0:T(8,128)(2,1)S(1)} custom-call(s32[2,4]{1,0:T(2,128)S(1)} %pad_add_fusion.bounds, bf16[4,1024,80]{2,1,0:T(8,128)(2,1)S(1)} %bitcast.45, s32[1024,1]{1,0:T(8,128)S(1)} %copy-done.8, bf16[4,80,5120]{2,1,0:T(8,128)(2,1)S(1)} %bitcast.44, bf16[4,5120,80]{2,1,0:T(8,128)(2,1)} %bitcast.52, s32[1,5120]{1,0:T(1,128)S(1)} %bitcast.47), custom_call_target="tpu_custom_call" | custom-call | flops 2684354560 | bytes 7864320 | tf_op jit(solution)/shard_map/pallas_call | solution.py:164
  134.9 2.2 copy.30
  137.0 2.2 copy.31.ctx_ref
  142.2 47.2 %shard_map.119 = f32[1024,1280]{1,0:T(8,128)} custom-call(bf16[1024,320]{1,0:T(8,128)(2,1)S(1)} %copy-done.7, bf16[1280,1280]{1,0:T(8,128)(2,1)} %all-gather.2.cloned.1.call-done.weight_ref, bf16[1024,1280]{1,0:T(8,128)(2,1)S(1)} %copy-done.3), custom_call_target="tpu_custom_call" | custom-call | flops 3355443200 | bytes 13762560 | tf_op jit(solution)/shard_map/pallas_call | solution.py:81
  189.4 2.8 reduce_sum.69
  192.2 3.1 multiply_reduce_fusion.1
  195.4 20.9 %convolution_convert_fusion = bf16[1024,1280]{1,0:T(8,128)(2,1)} fusion(bf16[1280,1280]{1,0:T(8,128)(2,1)S(1)} %copy-done, bf16[1280,1280]{1,0:T(8,128)(2,1)} %param.18, f32[1024,1280]{1,0:T(8,128)} %shard_map.119, f32[1280]{0:T(1024)S(1)} %convert_element_type.50, f32[1024]{0:T(1024)S(1)} %add_rsqrt_fusion.1, f32[1024]{0:T(1024)S(1)} %broadcast_multiply_fusion.1), kind=kOutput, calls=%fused_computation.32 | convolution fusion | flops 6802636800 | bytes 14431232 | tf_op jit(solution)/shard_map/dot_general | solution.py:239
  220.3 75.1 %all-reduce.2.cloned.1.call-done = bf16[1024,1280]{1,0:T(8,128)(2,1)} async-done(((bf16[1024,1280]{1,0:T(8,128)(2,1)}), bf16[1024,1280]{1,0:T(8,128)(2,1)}) %all-reduce.2.cloned.1.call-update) | async-done | bytes 2621456 | tf_op jit(solution)/shard_map/psum | solution.py:240
  295.4 4.0 %fusion.26 = f32[1024]{0:T(1024)S(1)} fusion(f32[1024,1280]{1,0:T(8,128)} %shard_map.119, bf16[1024,1280]{1,0:T(8,128)(2,1)} %all-reduce.2.cloned.1.call-done), kind=kLoop, calls=%fused_computation.43 | loop fusion | flops 3931136 | bytes 7868416 | tf_op jit(solution)/shard_map/reduce_sum | solution.py:109
  299.4 3.7 %multiply_reduce_fusion = f32[1024]{0:T(1024)S(1)} fusion(f32[1024]{0:T(1024)S(1)} %broadcast_multiply_fusion, f32[1024,1280]{1,0:T(8,128)} %shard_map.119, bf16[1024,1280]{1,0:T(8,128)(2,1)S(1)} %copy-done.9), kind=kLoop, calls=%fused_computation.13 | loop fusion | flops 6552576 | bytes 7872512 | tf_op jit(solution)/shard_map/reduce_sum | solution.py:111
  304.7 5.5 %gather_fusion = bf16[1024,1280]{1,0:T(8,128)(2,1)} fusion(bf16[1024,1280]{1,0:T(8,128)(2,1)S(1)} %multiply_convert_fusion, s32[1024]{0:T(1024)S(1)} %broadcast_clamp_fusion), kind=kCustom, calls=%fused_computation | custom fusion | bytes 5246976 | tf_op jit(solution)/shard_map/jit(_take)/gather | solution.py:244
  310.2 5.2 %gather.7 = bf16[256,5120]{1,0:T(8,128)(2,1)} reshape(bf16[1024,1280]{1,0:T(8,128)(2,1)} %gather_fusion) | data formatting | bytes 5242880 | tf_op jit(solution)/shard_map/jit(_take)/gather | solution.py:244
  315.4 5.3 %convolution_convert_fusion.1 = bf16[512,320]{0,1:T(8,128)(2,1)} fusion(bf16[5120,320]{0,1:T(8,128)(2,1)} %param.21, pred[256,5120]{1,0:T(8,128)(4,1)} %bitcast.57, bf16[256,5120]{1,0:T(8,128)(2,1)} %gather.7, s32[256]{0:T(256)S(1)} %bitcast.63), kind=kOutput, calls=%fused_computation.46 | convolution fusion | flops 924434432 | bytes 7537664 | tf_op jit(solution)/shard_map/ms,mc->sc/dot_general | solution.py:257
  320.7 1.9 copy.33
  322.6 17.8 %all_to_all.5 = bf16[32,16,320]{2,1,0:T(8,128)(2,1)S(1)} all-to-all(bf16[32,16,320]{2,1,0:T(8,128)(2,1)} %bitcast.56), channel_id=1, replica_groups=mesh['req'=32,'tp'=4] {'req'}, dimensions={0} | all-to-all | bytes 655360 | tf_op jit(solution)/shard_map/all_to_all | solution.py:261
  (101 shorter events, 26.8 us)
Async XLA Ops:
  6.5 188.8 %copy-start = (bf16[1280,1280]{1,0:T(8,128)(2,1)S(1)}, bf16[1280,1280]{1,0:T(8,128)(2,1)}, u32[]{:S(2)}) copy-start(bf16[1280,1280]{1,0:T(8,128)(2,1)} %param.19) | copy-start | bytes 9830404
  6.5 17.0 %copy-start.14 = (bf16[1280]{0:T(1024)(128)(2,1)S(1)}, bf16[1280]{0:T(1024)(128)(2,1)}, u32[]{:S(2)}) copy-start(bf16[1280]{0:T(1024)(128)(2,1)} %param.14) | copy-start | bytes 7684
  6.5 132.7 %all-gather.2.cloned.1.call-start = ((), (), s32[]{:S(2)}) async-start(), calls=%async_computation.1 | async-start | bytes 4096000 | tf_op jit(solution)/shard_map/all_gather | solution.py:206
  6.5 17.0 %copy-start.2 = (bf16[1024,1280]{1,0:T(8,128)(2,1)S(1)}, bf16[1024,1280]{1,0:T(8,128)(2,1)}, u32[]{:S(2)}) copy-start(bf16[1024,1280]{1,0:T(8,128)(2,1)} %tokens_ref.1) | copy-start | bytes 7864324
  6.5 17.0 %copy-start.18 = (bf16[1280,3,320]{0,2,1:T(8,128)(2,1)S(1)}, bf16[1280,3,320]{0,2,1:T(8,128)(2,1)}, u32[]{:S(2)}) copy-start(bf16[1280,3,320]{0,2,1:T(8,128)(2,1)} %param.15) | copy-start | bytes 7372804
  7.4 32.1 %collective-permute-start = (s32[1024]{0:T(1024)S(1)}, s32[1024]{0:T(1024)S(1)}, u32[]{:S(2)}, u32[]{:S(2)}) collective-permute-start(s32[1024]{0:T(1024)S(1)} %broadcast_add_fusion), channel_id=1, source_target_pairs={{0,8},{4,12},{8,16},{12,20},{16,24},{20,28},{24,32},{28,36},{32,40... | collective-permute-start | bytes 12296 | tf_op jit(solution)/shard_map/ppermute | solution.py:105
  11.6 31.1 %collective-permute-start.1 = (s32[1024]{0:T(1024)S(1)}, s32[1024]{0:T(1024)S(1)}, u32[]{:S(2)}, u32[]{:S(2)}) collective-permute-start(s32[1024]{0:T(1024)S(1)} %broadcast_add_fusion), channel_id=1, source_target_pairs={{0,4},{4,8},{8,12},{12,16},{16,20},{20,24},{24,28},{28,32},{32,36}... | collective-permute-start | bytes 12296 | tf_op jit(solution)/shard_map/ppermute | solution.py:105
  15.6 29.3 %collective-permute-start.2 = (s32[1024]{0:T(1024)S(1)}, s32[1024]{0:T(1024)S(1)}, u32[]{:S(2)}, u32[]{:S(2)}) collective-permute-start(s32[1024]{0:T(1024)S(1)} %broadcast_add_fusion), channel_id=1, source_target_pairs={{4,0},{8,4},{12,8},{16,12},{20,16},{24,20},{28,24},{32,28},{36,32}... | collective-permute-start | bytes 12296 | tf_op jit(solution)/shard_map/ppermute | solution.py:105
  17.5 28.7 %collective-permute-start.3 = (s32[1024]{0:T(1024)S(1)}, s32[1024]{0:T(1024)S(1)}, u32[]{:S(2)}, u32[]{:S(2)}) collective-permute-start(s32[1024]{0:T(1024)S(1)} %broadcast_add_fusion), channel_id=1, source_target_pairs={{8,0},{12,4},{16,8},{20,12},{24,16},{28,20},{32,24},{36,28},{40,32... | collective-permute-start | bytes 12296 | tf_op jit(solution)/shard_map/ppermute | solution.py:105
  26.5 1.3 copy-start.10
  27.8 11.7 %copy-start.15 = (bf16[1280]{0:T(1024)(128)(2,1)S(1)}, bf16[1280]{0:T(1024)(128)(2,1)}, u32[]{:S(2)}) copy-start(bf16[1280]{0:T(1024)(128)(2,1)} %param.17) | copy-start | bytes 7684
  27.8 17.1 %copy-start.12 = (s32[1024]{0:T(1024)S(1)}, s32[1024]{0:T(1024)}, u32[]{:S(2)}) copy-start(s32[1024]{0:T(1024)} %param.13) | copy-start | bytes 12292
  29.0 32.0 %collective-permute-start.4 = (bf16[1024,640]{0,1:T(8,128)(2,1)}, bf16[1024,640]{0,1:T(8,128)(2,1)}, u32[]{:S(2)}, u32[]{:S(2)}) collective-permute-start(bf16[1024,640]{0,1:T(8,128)(2,1)} %slice.28), channel_id=1, source_target_pairs={{0,8},{4,12},{8,16},{12,20},{16,24},{20,28},{24,32},{28,36},{32,40... | collective-permute-start | bytes 3932168 | tf_op jit(solution)/shard_map/ppermute | solution.py:105
  34.1 261.3 %all-reduce.2.cloned.1.call-start = ((), (), s32[]{:S(2)}) async-start(), calls=%async_computation.2 | async-start | bytes 5242880 | tf_op jit(solution)/shard_map/psum | solution.py:240
  39.5 36.4 %collective-permute-start.5 = (bf16[1024,640]{0,1:T(8,128)(2,1)}, bf16[1024,640]{0,1:T(8,128)(2,1)}, u32[]{:S(2)}, u32[]{:S(2)}) collective-permute-start(bf16[1024,640]{0,1:T(8,128)(2,1)} %slice.28), channel_id=1, source_target_pairs={{0,4},{4,8},{8,12},{12,16},{16,20},{20,24},{24,28},{28,32},{32,36}... | collective-permute-start | bytes 3932168 | tf_op jit(solution)/shard_map/ppermute | solution.py:105
  42.7 34.7 %collective-permute-start.6 = (bf16[1024,640]{0,1:T(8,128)(2,1)}, bf16[1024,640]{0,1:T(8,128)(2,1)}, u32[]{:S(2)}, u32[]{:S(2)}) collective-permute-start(bf16[1024,640]{0,1:T(8,128)(2,1)} %slice.28), channel_id=1, source_target_pairs={{4,0},{8,4},{12,8},{16,12},{20,16},{24,20},{28,24},{32,28},{36,32}... | collective-permute-start | bytes 3932168 | tf_op jit(solution)/shard_map/ppermute | solution.py:105
  44.9 33.9 %collective-permute-start.7 = (bf16[1024,640]{0,1:T(8,128)(2,1)}, bf16[1024,640]{0,1:T(8,128)(2,1)}, u32[]{:S(2)}, u32[]{:S(2)}) collective-permute-start(bf16[1024,640]{0,1:T(8,128)(2,1)} %slice.28), channel_id=1, source_target_pairs={{8,0},{12,4},{16,8},{20,12},{24,16},{28,20},{32,24},{36,28},{40,32... | collective-permute-start | bytes 3932168 | tf_op jit(solution)/shard_map/ppermute | solution.py:105
  50.0 27.3 %copy-start.11 = (bf16[1024,960]{0,1:T(8,128)(2,1)S(1)}, bf16[1024,960]{0,1:T(8,128)(2,1)}, u32[]{:S(2)}) copy-start(bf16[1024,960]{0,1:T(8,128)(2,1)} %copy-done.10) | copy-start | bytes 5898244
  89.9 1.9 copy-start.4
  91.8 1.2 copy-start.5
  93.0 1.0 copy-start.8
  133.9 1.0 copy-start.6
  139.3 1.7 copy-start.3
  141.0 1.1 copy-start.7
  195.3 21.0 %copy-start.16 = (bf16[1280]{0:T(1024)(128)(2,1)S(1)}, bf16[1280]{0:T(1024)(128)(2,1)}, u32[]{:S(2)}) copy-start(bf16[1280]{0:T(1024)(128)(2,1)} %param.20) | copy-start | bytes 7684
  195.4 21.0 %copy-start.17 = (s32[256,4]{0,1:T(4,128)S(1)}, s32[256,4]{0,1:T(4,128)}, u32[]{:S(2)}) copy-start(s32[256,4]{0,1:T(4,128)} %param.22) | copy-start | bytes 12292
  195.4 21.3 %copy-start.13 = (s32[256,1]{0,1:T(1,128)S(1)}, s32[256,1]{0,1:T(1,128)}, u32[]{:S(2)}) copy-start(s32[256,1]{0,1:T(1,128)} %param.23) | copy-start | bytes 3076
  295.4 4.0 %copy-start.9 = (bf16[1024,1280]{1,0:T(8,128)(2,1)S(1)}, bf16[1024,1280]{1,0:T(8,128)(2,1)}, u32[]{:S(2)}) copy-start(bf16[1024,1280]{1,0:T(8,128)(2,1)} %all-reduce.2.cloned.1.call-done) | copy-start | bytes 7864324
  295.4 7.8 %slice-start = ((s8[5242880]{0:T(1024)(128)(4,1)}), s8[4194304]{0:T(1024)(128)(4,1)S(1)}, s32[]{:S(2)}) async-start(s8[5242880]{0:T(1024)(128)(4,1)} %bitcast.48), calls=%async_computation.3 | async-start | bytes 8388608
  299.4 3.8 %slice-start.1 = ((s8[5242880]{0:T(1024)(128)(4,1)}), s8[1048576]{0:T(1024)(128)(4,1)S(1)}, s32[]{:S(2)}) async-start(s8[5242880]{0:T(1024)(128)(4,1)} %bitcast.48), calls=%async_computation.4 | async-start | bytes 2097152
  315.4 25.8 %copy-start.1 = (bf16[1280,1280]{1,0:T(8,128)(2,1)S(1)}, bf16[1280,1280]{1,0:T(8,128)(2,1)}, u32[]{:S(2)}) copy-start(bf16[1280,1280]{1,0:T(8,128)(2,1)} %param.19) | copy-start | bytes 9830404
Sparse Core Ops, SparseCore 0:
  34.2 44.2 all-gather.1
  216.5 78.8 all-reduce.1

commit v2 on v1

--- a/solution.py
+++ b/solution.py
@@ -17,6 +17,7 @@
     n = slots.shape[0]
     rows, width = ctx_ref.shape
     cols = out_ref.shape[1]
+    half = rows // 2
     me = lax.axis_index("tp")
     place = {"tp": me, "req": lax.axis_index("req")}
 
@@ -24,22 +25,24 @@
         where = dict(place, tp=lax.rem(me + k, n))
         return tuple(where[a] for a in order)
 
-    barrier = pltpu.get_barrier_semaphore()
-    for k in range(1, n):
-        pl.semaphore_signal(barrier, inc=1, device_id=peer(k), device_id_type=MESH_IDS)
-    pl.semaphore_wait(barrier, n - 1)
-    copies = []
-    for k in range(1, n):
+    def send(src, dst, sem, k):
         copy = pltpu.make_async_remote_copy(
-            src_ref=ctx_ref,
-            dst_ref=slots.at[k],
-            send_sem=send_sem.at[k],
-            recv_sem=recv_sem.at[k],
+            src_ref=src,
+            dst_ref=dst,
+            send_sem=send_sem.at[sem],
+            recv_sem=recv_sem.at[sem],
             device_id=peer(k),
             device_id_type=MESH_IDS,
         )
         copy.start()
-        copies.append(copy)
+        return copy
+
+    barrier = pltpu.get_barrier_semaphore()
+    for k in (1, n - 1):
+        pl.semaphore_signal(barrier, inc=1, device_id=peer(k), device_id_type=MESH_IDS)
+    pl.semaphore_wait(barrier, 2)
+    right = send(ctx_ref, slots.at[1], 1, 1)
+    left = send(ctx_ref, slots.at[3], 3, n - 1)
     tile = 256
 
     def add_term(block, source, first):
@@ -62,16 +65,22 @@
                     out_ref[r, c] = out_ref[r, c] + term
 
     add_term(ctx_ref, me, True)
-    for k in range(1, n):
-        copies[k - 1].wait_recv()
-        add_term(slots.at[k], lax.rem(me - k + n, n), False)
+    right.wait_recv()
+    onward = send(slots.at[1, pl.ds(0, half)], slots.at[2, pl.ds(0, half)], 2, 1)
+    add_term(slots.at[1], lax.rem(me + n - 1, n), False)
+    left.wait_recv()
+    backward = send(slots.at[3, pl.ds(half, half)], slots.at[2, pl.ds(half, half)], 0, n - 1)
+    add_term(slots.at[3], lax.rem(me + 1, n), False)
+    onward.wait_recv()
+    backward.wait_recv()
+    add_term(slots.at[2], lax.rem(me + 2, n), False)
 
     @pl.loop(0, rows // tile)
     def _(i):
         r = pl.ds(pl.multiple_of(i * tile, tile), tile)
         out_ref[r, :] = out_ref[r, :] + tokens_ref[r, :].astype(jnp.float32)
 
-    for copy in copies:
+    for copy in (right, left, onward, backward):
         copy.wait_send()
 
 

time: 349 us -> 348 us (level)
  Pallas kernels: 87 us -> 73.1 us
  waiting for transfers between devices: 98.1 us -> 111 us
    psum x1, waiting for transfers between devices: 75.1 us -> 87.8 us  [body(): lax.psum(hidden_terms.astype(jnp.bfloat16), 'tp').astype(jnp.float32)]
    pallas_call x1, Pallas kernels: 47.2 us -> 37.2 us  [project(): pl.pallas_call(functools.partial(project_kernel, order), out_shape=jax.Sh...]
    pallas_call x1, Pallas kernels: 39.8 us -> 35.9 us  [attention(): pl.pallas_call(flash_kernel, out_shape=jax.ShapeDtypeStruct(queries.shape...]
  transfers between devices with their start and end apart: 10 -> 10, of which waited for: 3 -> 3; matrix products, arithmetic and copies ran while one was open for 12% -> 12% of each run, Pallas kernels for 11% -> 10%
where the time goes in v2:
time: 348 us; the launch traced here: 347 us
  waiting for transfers between devices  111 us (32%)
  Pallas kernels  73.1 us (21%)
  local copies, waits for them, and re-layouts  55.6 us (16%)
  matrix products  29.2 us (8%)
  other arithmetic  23.2 us (7%)
  starting transfers between devices  23.1 us (7%)
  blocking collectives  17.8 us (5%)
  between operations  13.9 us (4%)
    psum x1, waiting for transfers between devices, body(): lax.psum(hidden_terms.astype(jnp.bfloat16), 'tp').astype(jnp.float32)  87.8 us
    pallas_call x1, Pallas kernels, project(): pl.pallas_call(functools.partial(project_kernel, order), out_shape=jax.Sh...  37.2 us
    pallas_call x1, Pallas kernels, attention(): pl.pallas_call(flash_kernel, out_shape=jax.ShapeDtypeStruct(queries.shape...  35.9 us
    ppermute x8, starting transfers between devices, shifted_2(): return lax.ppermute(block, axis, route)  23 us
    ppermute x8, waiting for transfers between devices, shifted_2(): return lax.ppermute(block, axis, route)  23 us
    dot_general x1, matrix products, body(): jnp.dot(expanded, reduce_weight, preferred_element_type=jnp.float32)  20.9 us
    all_to_all x1, blocking collectives, body(): lax.all_to_all(outgoing, 'req', split_axis=0, concat_axis=0, tiled=True)  17.8 us
    unnamed x51, local copies, waits for them, and re-layouts  16.2 us
  transfers between devices with their start and end apart: 10, of which 3 were waited for; matrix products, arithmetic and copies ran while one was open for 12% of the time, Pallas kernels for 10%

profile of v2, /device:TPU:1, one launch (start us, length us, event | category | flops | bytes accessed | tf_op | source)
XLA Modules:
  0.0 346.8 jit_solution(5539993731339178526)
XLA Ops:
  7.4 4.2 %collective-permute-start = (s32[1024]{0:T(1024)S(1)}, s32[1024]{0:T(1024)S(1)}, u32[]{:S(2)}, u32[]{:S(2)}) collective-permute-start(s32[1024]{0:T(1024)S(1)} %broadcast_add_fusion), channel_id=1, source_target_pairs={{0,8},{4,12},{8,16},{12,20},{16,24},{20,28},{24,32},{28,36},{32,40... | collective-permute-start | bytes 12296 | tf_op jit(solution)/shard_map/ppermute | solution.py:114
  11.6 4.0 %collective-permute-start.1 = (s32[1024]{0:T(1024)S(1)}, s32[1024]{0:T(1024)S(1)}, u32[]{:S(2)}, u32[]{:S(2)}) collective-permute-start(s32[1024]{0:T(1024)S(1)} %broadcast_add_fusion), channel_id=1, source_target_pairs={{0,4},{4,8},{8,12},{12,16},{16,20},{20,24},{24,28},{28,32},{32,36}... | collective-permute-start | bytes 12296 | tf_op jit(solution)/shard_map/ppermute | solution.py:114
  15.6 1.9 collective-permute-start.2
  18.8 2.2 convert_reduce_fusion
  21.0 2.6 fusion.2
  23.6 2.9 fusion.27
  29.0 5.0 %collective-permute-start.4 = (bf16[1024,640]{0,1:T(8,128)(2,1)}, bf16[1024,640]{0,1:T(8,128)(2,1)}, u32[]{:S(2)}, u32[]{:S(2)}) collective-permute-start(bf16[1024,640]{0,1:T(8,128)(2,1)} %slice.28), channel_id=1, source_target_pairs={{0,8},{4,12},{8,16},{12,20},{16,24},{20,28},{24,32},{28,36},{32,40... | collective-permute-start | bytes 3932168 | tf_op jit(solution)/shard_map/ppermute | solution.py:114
  34.3 2.0 slice.27
  37.3 2.2 copy.27
  39.5 3.1 collective-permute-start.5
  42.7 2.2 collective-permute-start.6
  46.4 3.6 %rev.3 = pred[4,5120]{1,0:T(4,128)(4,1)S(1)} reverse(pred[4,5120]{1,0:T(4,128)(4,1)S(1)} %compare_and_fusion), dimensions={1} | reverse | bytes 40960 | tf_op jit(solution)/shard_map/rev | solution.py:171
  51.5 9.6 %collective-permute-done.4 = bf16[1024,640]{0,1:T(8,128)(2,1)} collective-permute-done((bf16[1024,640]{0,1:T(8,128)(2,1)}, bf16[1024,640]{0,1:T(8,128)(2,1)}, u32[]{:S(2)}, u32[]{:S(2)}) %collective-permute-start.4) | collective-permute-done | bytes 1310752 | tf_op jit(solution)/shard_map/ppermute | solution.py:114
  62.5 13.4 %collective-permute-done.5 = bf16[1024,640]{0,1:T(8,128)(2,1)} collective-permute-done((bf16[1024,640]{0,1:T(8,128)(2,1)}, bf16[1024,640]{0,1:T(8,128)(2,1)}, u32[]{:S(2)}, u32[]{:S(2)}) %collective-permute-start.5) | collective-permute-done | bytes 1310752 | tf_op jit(solution)/shard_map/ppermute | solution.py:114
  80.3 3.2 fusion.74
  83.5 6.4 %copy.28 = bf16[5120,4,80]{2,0,1:T(8,128)(2,1)} copy(bf16[5120,4,80]{0,2,1:T(8,128)(2,1)} %bitcast.50) | data formatting | bytes 6553600 | tf_op jit(solution)/shard_map/reshape | solution.py:233
  89.9 1.9 copy-done.4
  94.1 35.9 %shard_map.118 = bf16[4,1024,80]{2,1,0:T(8,128)(2,1)S(1)} custom-call(s32[2,4]{1,0:T(2,128)S(1)} %pad_add_fusion.bounds, bf16[4,1024,80]{2,1,0:T(8,128)(2,1)S(1)} %bitcast.45, s32[1024,1]{1,0:T(8,128)S(1)} %copy-done.8, bf16[4,80,5120]{2,1,0:T(8,128)(2,1)S(1)} %bitcast.44, bf16[4,5120,80]{2,1,0:T(8,128)(2,1)} %bitcast.52, s32[1,5120]{1,0:T(1,128)S(1)} %bitcast.47), custom_call_target="tpu_custom_call" | custom-call | flops 2684354560 | bytes 7864320 | tf_op jit(solution)/shard_map/pallas_call | solution.py:173
  131.0 2.2 copy.30
  133.1 2.2 copy.31.ctx_ref
  138.2 37.2 %shard_map.119 = f32[1024,1280]{1,0:T(8,128)} custom-call(bf16[1024,320]{1,0:T(8,128)(2,1)S(1)} %copy-done.7, bf16[1280,1280]{1,0:T(8,128)(2,1)} %all-gather.2.cloned.1.call-done.weight_ref, bf16[1024,1280]{1,0:T(8,128)(2,1)S(1)} %copy-done.3), custom_call_target="tpu_custom_call" | custom-call | flops 3355443200 | bytes 13762560 | tf_op jit(solution)/shard_map/pallas_call | solution.py:90
  175.4 2.8 reduce_sum.69
  178.2 3.1 multiply_reduce_fusion.1
  181.4 20.9 %convolution_convert_fusion = bf16[1024,1280]{1,0:T(8,128)(2,1)} fusion(bf16[1280,1280]{1,0:T(8,128)(2,1)S(1)} %copy-done, bf16[1280,1280]{1,0:T(8,128)(2,1)} %param.18, f32[1024,1280]{1,0:T(8,128)} %shard_map.119, f32[1280]{0:T(1024)S(1)} %convert_element_type.50, f32[1024]{0:T(1024)S(1)} %add_rsqrt_fusion.1, f32[1024]{0:T(1024)S(1)} %broadcast_multiply_fusion.1), kind=kOutput, calls=%fused_computation.32 | convolution fusion | flops 6802636800 | bytes 14431232 | tf_op jit(solution)/shard_map/dot_general | solution.py:248
  206.4 87.8 %all-reduce.2.cloned.1.call-done = bf16[1024,1280]{1,0:T(8,128)(2,1)} async-done(((bf16[1024,1280]{1,0:T(8,128)(2,1)}), bf16[1024,1280]{1,0:T(8,128)(2,1)}) %all-reduce.2.cloned.1.call-update) | async-done | bytes 2621456 | tf_op jit(solution)/shard_map/psum | solution.py:249
  294.1 4.0 %fusion.26 = f32[1024]{0:T(1024)S(1)} fusion(f32[1024,1280]{1,0:T(8,128)} %shard_map.119, bf16[1024,1280]{1,0:T(8,128)(2,1)} %all-reduce.2.cloned.1.call-done), kind=kLoop, calls=%fused_computation.43 | loop fusion | flops 3931136 | bytes 7868416 | tf_op jit(solution)/shard_map/reduce_sum | solution.py:118
  298.2 3.7 %multiply_reduce_fusion = f32[1024]{0:T(1024)S(1)} fusion(f32[1024]{0:T(1024)S(1)} %broadcast_multiply_fusion, f32[1024,1280]{1,0:T(8,128)} %shard_map.119, bf16[1024,1280]{1,0:T(8,128)(2,1)S(1)} %copy-done.9), kind=kLoop, calls=%fused_computation.13 | loop fusion | flops 6552576 | bytes 7872512 | tf_op jit(solution)/shard_map/reduce_sum | solution.py:120
  303.5 5.5 %gather_fusion = bf16[1024,1280]{1,0:T(8,128)(2,1)} fusion(bf16[1024,1280]{1,0:T(8,128)(2,1)S(1)} %multiply_convert_fusion, s32[1024]{0:T(1024)S(1)} %broadcast_clamp_fusion), kind=kCustom, calls=%fused_computation | custom fusion | bytes 5246976 | tf_op jit(solution)/shard_map/jit(_take)/gather | solution.py:253
  309.0 5.2 %gather.7 = bf16[256,5120]{1,0:T(8,128)(2,1)} reshape(bf16[1024,1280]{1,0:T(8,128)(2,1)} %gather_fusion) | data formatting | bytes 5242880 | tf_op jit(solution)/shard_map/jit(_take)/gather | solution.py:253
  314.2 5.3 %convolution_convert_fusion.1 = bf16[512,320]{0,1:T(8,128)(2,1)} fusion(bf16[5120,320]{0,1:T(8,128)(2,1)} %param.21, pred[256,5120]{1,0:T(8,128)(4,1)} %bitcast.57, bf16[256,5120]{1,0:T(8,128)(2,1)} %gather.7, s32[256]{0:T(256)S(1)} %bitcast.63), kind=kOutput, calls=%fused_computation.46 | convolution fusion | flops 924434432 | bytes 7537664 | tf_op jit(solution)/shard_map/ms,mc->sc/dot_general | solution.py:266
  319.5 1.9 copy.33
  321.4 17.8 %all_to_all.5 = bf16[32,16,320]{2,1,0:T(8,128)(2,1)S(1)} all-to-all(bf16[32,16,320]{2,1,0:T(8,128)(2,1)} %bitcast.56), channel_id=1, replica_groups=mesh['req'=32,'tp'=4] {'req'}, dimensions={0} | all-to-all | bytes 655360 | tf_op jit(solution)/shard_map/all_to_all | solution.py:270
  (101 shorter events, 26.8 us)
Async XLA Ops:
  6.5 174.9 %copy-start = (bf16[1280,1280]{1,0:T(8,128)(2,1)S(1)}, bf16[1280,1280]{1,0:T(8,128)(2,1)}, u32[]{:S(2)}) copy-start(bf16[1280,1280]{1,0:T(8,128)(2,1)} %param.19) | copy-start | bytes 9830404
  6.5 17.0 %copy-start.14 = (bf16[1280]{0:T(1024)(128)(2,1)S(1)}, bf16[1280]{0:T(1024)(128)(2,1)}, u32[]{:S(2)}) copy-start(bf16[1280]{0:T(1024)(128)(2,1)} %param.14) | copy-start | bytes 7684
  6.5 128.8 %all-gather.2.cloned.1.call-start = ((), (), s32[]{:S(2)}) async-start(), calls=%async_computation.1 | async-start | bytes 4096000 | tf_op jit(solution)/shard_map/all_gather | solution.py:215
  6.5 17.0 %copy-start.2 = (bf16[1024,1280]{1,0:T(8,128)(2,1)S(1)}, bf16[1024,1280]{1,0:T(8,128)(2,1)}, u32[]{:S(2)}) copy-start(bf16[1024,1280]{1,0:T(8,128)(2,1)} %tokens_ref.1) | copy-start | bytes 7864324
  6.5 17.0 %copy-start.18 = (bf16[1280,3,320]{0,2,1:T(8,128)(2,1)S(1)}, bf16[1280,3,320]{0,2,1:T(8,128)(2,1)}, u32[]{:S(2)}) copy-start(bf16[1280,3,320]{0,2,1:T(8,128)(2,1)} %param.15) | copy-start | bytes 7372804
  7.4 32.1 %collective-permute-start = (s32[1024]{0:T(1024)S(1)}, s32[1024]{0:T(1024)S(1)}, u32[]{:S(2)}, u32[]{:S(2)}) collective-permute-start(s32[1024]{0:T(1024)S(1)} %broadcast_add_fusion), channel_id=1, source_target_pairs={{0,8},{4,12},{8,16},{12,20},{16,24},{20,28},{24,32},{28,36},{32,40... | collective-permute-start | bytes 12296 | tf_op jit(solution)/shard_map/ppermute | solution.py:114
  11.6 31.1 %collective-permute-start.1 = (s32[1024]{0:T(1024)S(1)}, s32[1024]{0:T(1024)S(1)}, u32[]{:S(2)}, u32[]{:S(2)}) collective-permute-start(s32[1024]{0:T(1024)S(1)} %broadcast_add_fusion), channel_id=1, source_target_pairs={{0,4},{4,8},{8,12},{12,16},{16,20},{20,24},{24,28},{28,32},{32,36}... | collective-permute-start | bytes 12296 | tf_op jit(solution)/shard_map/ppermute | solution.py:114
  15.6 29.3 %collective-permute-start.2 = (s32[1024]{0:T(1024)S(1)}, s32[1024]{0:T(1024)S(1)}, u32[]{:S(2)}, u32[]{:S(2)}) collective-permute-start(s32[1024]{0:T(1024)S(1)} %broadcast_add_fusion), channel_id=1, source_target_pairs={{4,0},{8,4},{12,8},{16,12},{20,16},{24,20},{28,24},{32,28},{36,32}... | collective-permute-start | bytes 12296 | tf_op jit(solution)/shard_map/ppermute | solution.py:114
  17.5 28.7 %collective-permute-start.3 = (s32[1024]{0:T(1024)S(1)}, s32[1024]{0:T(1024)S(1)}, u32[]{:S(2)}, u32[]{:S(2)}) collective-permute-start(s32[1024]{0:T(1024)S(1)} %broadcast_add_fusion), channel_id=1, source_target_pairs={{8,0},{12,4},{16,8},{20,12},{24,16},{28,20},{32,24},{36,28},{40,32... | collective-permute-start | bytes 12296 | tf_op jit(solution)/shard_map/ppermute | solution.py:114
  26.5 1.3 copy-start.10
  27.8 11.7 %copy-start.15 = (bf16[1280]{0:T(1024)(128)(2,1)S(1)}, bf16[1280]{0:T(1024)(128)(2,1)}, u32[]{:S(2)}) copy-start(bf16[1280]{0:T(1024)(128)(2,1)} %param.17) | copy-start | bytes 7684
  27.8 17.1 %copy-start.12 = (s32[1024]{0:T(1024)S(1)}, s32[1024]{0:T(1024)}, u32[]{:S(2)}) copy-start(s32[1024]{0:T(1024)} %param.13) | copy-start | bytes 12292
  29.0 32.0 %collective-permute-start.4 = (bf16[1024,640]{0,1:T(8,128)(2,1)}, bf16[1024,640]{0,1:T(8,128)(2,1)}, u32[]{:S(2)}, u32[]{:S(2)}) collective-permute-start(bf16[1024,640]{0,1:T(8,128)(2,1)} %slice.28), channel_id=1, source_target_pairs={{0,8},{4,12},{8,16},{12,20},{16,24},{20,28},{24,32},{28,36},{32,40... | collective-permute-start | bytes 3932168 | tf_op jit(solution)/shard_map/ppermute | solution.py:114
  34.1 260.1 %all-reduce.2.cloned.1.call-start = ((), (), s32[]{:S(2)}) async-start(), calls=%async_computation.2 | async-start | bytes 5242880 | tf_op jit(solution)/shard_map/psum | solution.py:249
  39.5 36.4 %collective-permute-start.5 = (bf16[1024,640]{0,1:T(8,128)(2,1)}, bf16[1024,640]{0,1:T(8,128)(2,1)}, u32[]{:S(2)}, u32[]{:S(2)}) collective-permute-start(bf16[1024,640]{0,1:T(8,128)(2,1)} %slice.28), channel_id=1, source_target_pairs={{0,4},{4,8},{8,12},{12,16},{16,20},{20,24},{24,28},{28,32},{32,36}... | collective-permute-start | bytes 3932168 | tf_op jit(solution)/shard_map/ppermute | solution.py:114
  42.7 34.7 %collective-permute-start.6 = (bf16[1024,640]{0,1:T(8,128)(2,1)}, bf16[1024,640]{0,1:T(8,128)(2,1)}, u32[]{:S(2)}, u32[]{:S(2)}) collective-permute-start(bf16[1024,640]{0,1:T(8,128)(2,1)} %slice.28), channel_id=1, source_target_pairs={{4,0},{8,4},{12,8},{16,12},{20,16},{24,20},{28,24},{32,28},{36,32}... | collective-permute-start | bytes 3932168 | tf_op jit(solution)/shard_map/ppermute | solution.py:114
  44.9 33.9 %collective-permute-start.7 = (bf16[1024,640]{0,1:T(8,128)(2,1)}, bf16[1024,640]{0,1:T(8,128)(2,1)}, u32[]{:S(2)}, u32[]{:S(2)}) collective-permute-start(bf16[1024,640]{0,1:T(8,128)(2,1)} %slice.28), channel_id=1, source_target_pairs={{8,0},{12,4},{16,8},{20,12},{24,16},{28,20},{32,24},{36,28},{40,32... | collective-permute-start | bytes 3932168 | tf_op jit(solution)/shard_map/ppermute | solution.py:114
  50.0 27.3 %copy-start.11 = (bf16[1024,960]{0,1:T(8,128)(2,1)S(1)}, bf16[1024,960]{0,1:T(8,128)(2,1)}, u32[]{:S(2)}) copy-start(bf16[1024,960]{0,1:T(8,128)(2,1)} %copy-done.10) | copy-start | bytes 5898244
  89.9 1.9 copy-start.4
  91.8 1.2 copy-start.5
  93.0 1.0 copy-start.8
  130.0 1.0 copy-start.6
  135.4 1.7 copy-start.3
  137.1 1.1 copy-start.7
  181.4 21.0 %copy-start.16 = (bf16[1280]{0:T(1024)(128)(2,1)S(1)}, bf16[1280]{0:T(1024)(128)(2,1)}, u32[]{:S(2)}) copy-start(bf16[1280]{0:T(1024)(128)(2,1)} %param.20) | copy-start | bytes 7684
  181.4 21.0 %copy-start.17 = (s32[256,4]{0,1:T(4,128)S(1)}, s32[256,4]{0,1:T(4,128)}, u32[]{:S(2)}) copy-start(s32[256,4]{0,1:T(4,128)} %param.22) | copy-start | bytes 12292
  181.4 21.3 %copy-start.13 = (s32[256,1]{0,1:T(1,128)S(1)}, s32[256,1]{0,1:T(1,128)}, u32[]{:S(2)}) copy-start(s32[256,1]{0,1:T(1,128)} %param.23) | copy-start | bytes 3076
  294.1 4.0 %copy-start.9 = (bf16[1024,1280]{1,0:T(8,128)(2,1)S(1)}, bf16[1024,1280]{1,0:T(8,128)(2,1)}, u32[]{:S(2)}) copy-start(bf16[1024,1280]{1,0:T(8,128)(2,1)} %all-reduce.2.cloned.1.call-done) | copy-start | bytes 7864324
  294.1 7.8 %slice-start = ((s8[5242880]{0:T(1024)(128)(4,1)}), s8[4194304]{0:T(1024)(128)(4,1)S(1)}, s32[]{:S(2)}) async-start(s8[5242880]{0:T(1024)(128)(4,1)} %bitcast.48), calls=%async_computation.3 | async-start | bytes 8388608
  298.2 3.8 %slice-start.1 = ((s8[5242880]{0:T(1024)(128)(4,1)}), s8[1048576]{0:T(1024)(128)(4,1)S(1)}, s32[]{:S(2)}) async-start(s8[5242880]{0:T(1024)(128)(4,1)} %bitcast.48), calls=%async_computation.4 | async-start | bytes 2097152
  314.2 25.8 %copy-start.1 = (bf16[1280,1280]{1,0:T(8,128)(2,1)S(1)}, bf16[1280,1280]{1,0:T(8,128)(2,1)}, u32[]{:S(2)}) copy-start(bf16[1280,1280]{1,0:T(8,128)(2,1)} %param.19) | copy-start | bytes 9830404
Sparse Core Ops, SparseCore 0:
  34.2 44.2 all-gather.1
  202.5 91.5 all-reduce.1

commit v3 on v2

--- a/solution.py
+++ b/solution.py
@@ -10,6 +10,7 @@
 
 HD = 80
 TILE = 256
+NEAR = (1, -1, 2, -2)
 MESH_IDS = pl.DeviceIdType.MESH
 
 
@@ -82,6 +83,75 @@
 
     for copy in (right, left, onward, backward):
         copy.wait_send()
+
+
+def exchange_kernel(order, n, keys_ref, values_ref, marks_ref, keys_out, values_out, marks_out,
+                    send_sem, recv_sem, local_sem):
+    me = lax.axis_index("req")
+    place = {"req": me, "tp": lax.axis_index("tp")}
+    span = marks_ref.shape[1]
+
+    def peer(d):
+        where = dict(place, req=lax.rem(me + d + n, n))
+        return tuple(where[a] for a in order)
+
+    def windows(slot):
+        part = pl.ds(slot * span, span)
+        return (keys_out.at[:, :, part], values_out.at[:, part, :], marks_out.at[:, part])
+
+    sources = (keys_ref, values_ref, marks_ref)
+    barrier = pltpu.get_barrier_semaphore()
+    for d in NEAR:
+        pl.semaphore_signal(barrier, inc=1, device_id=peer(d), device_id_type=MESH_IDS)
+    pl.semaphore_wait(barrier, len(NEAR))
+    copies = []
+    for index, d in enumerate(NEAR):
+        for a, (src, dst) in enumerate(zip(sources, windows(2 - d))):
+            copy = pltpu.make_async_remote_copy(
+                src_ref=src,
+                dst_ref=dst,
+                send_sem=send_sem.at[3 * index + a],
+                recv_sem=recv_sem.at[3 * index + a],
+                device_id=peer(d),
+                device_id_type=MESH_IDS,
+            )
+            copy.start()
+            copies.append(copy)
+    local = []
+    for a, (src, dst) in enumerate(zip(sources, windows(2))):
+        copy = pltpu.make_async_copy(src, dst, local_sem.at[a])
+        copy.start()
+        local.append(copy)
+    for copy in local:
+        copy.wait()
+    for copy in copies:
+        copy.wait()
+
+
+def exchange(keys, values, marks, order):
+    n = lax.axis_size("req")
+    slots = 2 * max(NEAR) + 1
+    heads, width, span = keys.shape
+    any_spec = pl.BlockSpec(memory_space=pl.ANY)
+    keys_all, values_all, marks_all = pl.pallas_call(
+        functools.partial(exchange_kernel, order, n),
+        out_shape=(
+            jax.ShapeDtypeStruct((heads, width, slots * span), keys.dtype),
+            jax.ShapeDtypeStruct((heads, slots * span, width), values.dtype),
+            jax.ShapeDtypeStruct((1, slots * span), marks.dtype),
+        ),
+        in_specs=[any_spec] * 3,
+        out_specs=(any_spec, any_spec, any_spec),
+        scratch_shapes=[
+            pltpu.SemaphoreType.DMA((3 * len(NEAR),)),
+            pltpu.SemaphoreType.DMA((3 * len(NEAR),)),
+            pltpu.SemaphoreType.DMA((3,)),
+        ],
+        compiler_params=pltpu.CompilerParams(collective_id=1, has_side_effects=True),
+    )(keys, values, marks.reshape(1, span))
+    source = lax.axis_index("req") + jnp.arange(slots * span, dtype=jnp.int32) // span - max(NEAR)
+    present = (source >= 0) & (source < n)
+    return keys_all, values_all, jnp.where(present, marks_all[0], 0)
 
 
 def project(context, weight, tokens, order):
@@ -220,25 +290,18 @@
         attend_weight.reshape(attend_weight.shape[0], 3 * head_width),
         preferred_element_type=jnp.float32,
     ).astype(jnp.bfloat16)
-    key_value = projected[:, head_width:]
     marks = segments + 1
-    near = {0: (key_value, marks)}
-    for distance in (1, -1, 2, -2):
-        near[distance] = shifted_2((key_value, marks), "req", distance)
-    ordered = [near[d] for d in (2, 1, 0, -1, -2)]
-    all_kv = jnp.concatenate([p for p, _ in ordered], axis=0)
-    key_marks = jnp.concatenate([m for _, m in ordered], axis=0)
 
     def by_head(block):
         return jnp.transpose(block.reshape(block.shape[0], head_count, HD), (1, 0, 2))
 
-    context = attention(
-        by_head(projected[:, :head_width]),
+    keys_all, values_all, key_marks = exchange(
+        jnp.transpose(projected[:, head_width : 2 * head_width].reshape(-1, head_count, HD), (1, 2, 0)),
+        by_head(projected[:, 2 * head_width :]),
         marks,
-        jnp.transpose(all_kv[:, :head_width].reshape(-1, head_count, HD), (1, 2, 0)),
-        by_head(all_kv[:, head_width:]),
-        key_marks,
-    )
+        order,
+    )
+    context = attention(by_head(projected[:, :head_width]), marks, keys_all, values_all, key_marks)
     context = jnp.transpose(context, (1, 0, 2)).reshape(token_rows, head_width)
     middle = project(context, full_weight, tokens, order)
     mixer_in = layer_norm(middle, mixer_gain).astype(jnp.bfloat16)

time: 348 us -> 338 us (0.971)
  Pallas kernels: 73.1 us -> 143 us
  waiting for transfers between devices: 111 us -> 65.9 us
  starting transfers between devices: 23.1 us -> 0.04 us
  local copies, waits for them, and re-layouts: 55.6 us -> 43.7 us
    pallas_call x0 -> x1, Pallas kernels: none -> 63.9 us  [exchange(): pl.pallas_call(functools.partial(exchange_kernel, order, n), out_shape=(j...]
    ppermute x8 -> x0, starting transfers between devices: 23 us -> none  [shifted_2(): return lax.ppermute(block, axis, route)]
    ppermute x8 -> x0, waiting for transfers between devices: 23 us -> none  [shifted_2(): return lax.ppermute(block, axis, route)]
    psum x1, waiting for transfers between devices: 87.8 us -> 65.2 us  [body(): lax.psum(hidden_terms.astype(jnp.bfloat16), 'tp').astype(jnp.float32)]
    unnamed x51 -> x40, local copies, waits for them, and re-layouts: 16.2 us -> 11 us
    slice x3 -> x1, local copies, waits for them, and re-layouts: 4.59 us -> 0.18 us  [the longest x1 3.23 us: body(): all_kv[:, head_width:]]
    reshape x2, local copies, waits for them, and re-layouts: 8.57 us -> 4.39 us  [by_head(): block.reshape(block.shape[0], head_count, HD)]
    pallas_call x1, Pallas kernels: 35.9 us -> 39.8 us  [attention(): pl.pallas_call(flash_kernel, out_shape=jax.ShapeDtypeStruct(queries.shape...]
  transfers between devices with their start and end apart: 10 -> 2, of which waited for: 3 -> 1; matrix products, arithmetic and copies ran while one was open for 12% -> 9% of each run, Pallas kernels for 10% -> 31%
where the time goes in v3:
time: 338 us
  Pallas kernels  143 us (42%)
  waiting for transfers between devices  65.9 us (19%)
  local copies, waits for them, and re-layouts  43.7 us (13%)
  matrix products  29 us (9%)
  other arithmetic  24.5 us (7%)
  blocking collectives  17.8 us (5%)
  between operations  13.8 us (4%)
    psum x1, waiting for transfers between devices, body(): lax.psum(hidden_terms.astype(jnp.bfloat16), 'tp').astype(jnp.float32)  65.2 us
    pallas_call x1, Pallas kernels, exchange(): pl.pallas_call(functools.partial(exchange_kernel, order, n), out_shape=(j...  63.9 us
    pallas_call x1, Pallas kernels, attention(): pl.pallas_call(flash_kernel, out_shape=jax.ShapeDtypeStruct(queries.shape...  39.8 us
    pallas_call x1, Pallas kernels, project(): pl.pallas_call(functools.partial(project_kernel, order), out_shape=jax.Sh...  39.1 us
    dot_general x1, matrix products, body(): jnp.dot(expanded, reduce_weight, preferred_element_type=jnp.float32)  20.9 us
    all_to_all x1, blocking collectives, body(): lax.all_to_all(outgoing, 'req', split_axis=0, concat_axis=0, tiled=True)  17.8 us
    gather x2, local copies, waits for them, and re-layouts, body(): jnp.take(final_normed, local_index.reshape(-1), axis=0)  13.9 us
    unnamed x40, local copies, waits for them, and re-layouts  11 us
  transfers between devices with their start and end apart: 2, of which 1 were waited for; matrix products, arithmetic and copies ran while one was open for 9% of the time, Pallas kernels for 31%

profile of v3, /device:TPU:1, one launch (start us, length us, event | category | flops | bytes accessed | tf_op | source)
XLA Modules:
  0.0 337.5 jit_solution(292206810029007523)
XLA Ops:
  7.3 2.3 convert_reduce_fusion
  9.6 2.7 fusion.2
  12.4 2.9 fusion.27
  15.3 1.3 fusion.76
  16.6 2.2 copy.27
  19.4 63.9 %shard_map.118 = (bf16[4,80,5120]{2,1,0:T(8,128)(2,1)}, bf16[4,5120,80]{2,1,0:T(8,128)(2,1)}, s32[1,5120]{1,0:T(1,128)}) custom-call(bf16[4,80,1024]{2,1,0:T(8,128)(2,1)} %bitcast.55, bf16[4,1024,80]{2,1,0:T(8,128)(2,1)} %bitcast.52, s32[1,1024]{1,0:T(1,128)} %bitcast.60), custom_call_target="tpu_custom_call" | custom-call | tf_op jit(solution)/shard_map/pallas_call | solution.py:136
  84.2 3.6 %rev.3 = pred[4,5120]{1,0:T(4,128)(4,1)S(1)} reverse(pred[4,5120]{1,0:T(4,128)(4,1)S(1)} %compare_and_fusion), dimensions={1} | reverse | bytes 40960 | tf_op jit(solution)/shard_map/rev | solution.py:241
  87.9 2.2 copy.28
  90.0 1.7 copy.29.qm_ref
  93.2 1.2 copy-done.3
  94.5 1.0 copy-done.6
  95.5 1.9 copy-done.7
  97.4 39.8 %shard_map.119 = bf16[4,1024,80]{2,1,0:T(8,128)(2,1)S(1)} custom-call(s32[2,4]{1,0:T(2,128)S(1)} %pad_add_fusion.bounds, bf16[4,1024,80]{2,1,0:T(8,128)(2,1)S(1)} %bitcast.45, s32[1024,1]{1,0:T(8,128)S(1)} %copy-done.6, bf16[4,80,5120]{2,1,0:T(8,128)(2,1)S(1)} %copy-done.7, bf16[4,5120,80]{2,1,0:T(8,128)(2,1)} %get-tuple-element.14.v_ref, ...), custom_call_target="tpu_custom_call" | custom-call | flops 2684354560 | bytes 7864320 | tf_op jit(solution)/shard_map/pallas_call | solution.py:243
  137.2 1.0 copy-done.4
  138.2 2.2 copy.30
  140.4 2.2 copy.31.ctx_ref
  142.7 1.7 copy-done.2
  144.4 1.1 copy-done.5
  145.5 39.1 %shard_map.120 = f32[1024,1280]{1,0:T(8,128)} custom-call(bf16[1024,320]{1,0:T(8,128)(2,1)S(1)} %copy-done.5, bf16[1280,1280]{1,0:T(8,128)(2,1)} %all-gather.2.cloned.1.call-done.weight_ref, bf16[1024,1280]{1,0:T(8,128)(2,1)S(1)} %copy-done.2), custom_call_target="tpu_custom_call" | custom-call | flops 3355443200 | bytes 13762560 | tf_op jit(solution)/shard_map/pallas_call | solution.py:160
  184.6 2.8 reduce_sum.69
  187.4 3.1 multiply_reduce_fusion.1
  190.6 20.9 %convolution_convert_fusion = bf16[1024,1280]{1,0:T(8,128)(2,1)} fusion(bf16[1280,1280]{1,0:T(8,128)(2,1)S(1)} %copy-done, bf16[1280,1280]{1,0:T(8,128)(2,1)} %param.18, f32[1024,1280]{1,0:T(8,128)} %shard_map.120, f32[1280]{0:T(1024)S(1)} %convert_element_type.50, f32[1024]{0:T(1024)S(1)} %add_rsqrt_fusion.1, f32[1024]{0:T(1024)S(1)} %broadcast_multiply_fusion.1), kind=kOutput, calls=%fused_computation.32 | convolution fusion | flops 6802636800 | bytes 14431232 | tf_op jit(solution)/shard_map/dot_general | solution.py:311
  212.8 1.7 copy.35
  215.5 65.2 %all-reduce.2.cloned.1.call-done = bf16[1024,1280]{1,0:T(8,128)(2,1)} async-done(((bf16[1024,1280]{1,0:T(8,128)(2,1)}), bf16[1024,1280]{1,0:T(8,128)(2,1)}) %all-reduce.2.cloned.1.call-update) | async-done | bytes 2621456 | tf_op jit(solution)/shard_map/psum | solution.py:312
  280.7 4.0 %fusion.26 = f32[1024]{0:T(1024)S(1)} fusion(f32[1024,1280]{1,0:T(8,128)} %shard_map.120, bf16[1024,1280]{1,0:T(8,128)(2,1)} %all-reduce.2.cloned.1.call-done), kind=kLoop, calls=%fused_computation.43 | loop fusion | flops 3931136 | bytes 7868416 | tf_op jit(solution)/shard_map/reduce_sum | solution.py:188
  284.8 3.7 %multiply_reduce_fusion = f32[1024]{0:T(1024)S(1)} fusion(f32[1024]{0:T(1024)S(1)} %broadcast_multiply_fusion, f32[1024,1280]{1,0:T(8,128)} %shard_map.120, bf16[1024,1280]{1,0:T(8,128)(2,1)S(1)} %copy-done.8), kind=kLoop, calls=%fused_computation.13 | loop fusion | flops 6552576 | bytes 7872512 | tf_op jit(solution)/shard_map/reduce_sum | solution.py:190
  288.5 2.6 multiply_convert_fusion
  291.1 8.7 %gather_fusion = bf16[1024,1280]{1,0:T(8,128)(2,1)} fusion(bf16[1024,1280]{1,0:T(8,128)(2,1)} %multiply_convert_fusion, s32[1024]{0:T(1024)S(1)} %broadcast_clamp_fusion), kind=kCustom, calls=%fused_computation | custom fusion | bytes 5246976 | tf_op jit(solution)/shard_map/jit(_take)/gather | solution.py:316
  299.8 5.2 %gather.7 = bf16[256,5120]{1,0:T(8,128)(2,1)} reshape(bf16[1024,1280]{1,0:T(8,128)(2,1)} %gather_fusion) | data formatting | bytes 5242880 | tf_op jit(solution)/shard_map/jit(_take)/gather | solution.py:316
  305.0 5.2 %convolution_convert_fusion.1 = bf16[512,320]{0,1:T(8,128)(2,1)} fusion(bf16[5120,320]{0,1:T(8,128)(2,1)} %param.21, pred[256,5120]{1,0:T(8,128)(4,1)} %bitcast.59, bf16[256,5120]{1,0:T(8,128)(2,1)} %gather.7, s32[256]{0:T(256)S(1)} %bitcast.66), kind=kOutput, calls=%fused_computation.46 | convolution fusion | flops 924434432 | bytes 7537664 | tf_op jit(solution)/shard_map/ms,mc->sc/dot_general | solution.py:329
  310.2 1.9 copy.33
  312.1 17.8 %all_to_all.5 = bf16[32,16,320]{2,1,0:T(8,128)(2,1)S(1)} all-to-all(bf16[32,16,320]{2,1,0:T(8,128)(2,1)} %bitcast.58), channel_id=1, replica_groups=mesh['req'=32,'tp'=4] {'req'}, dimensions={0} | all-to-all | bytes 655360 | tf_op jit(solution)/shard_map/all_to_all | solution.py:333
  (71 shorter events, 6.7 us)
Async XLA Ops:
  6.5 184.0 %copy-start = (bf16[1280,1280]{1,0:T(8,128)(2,1)S(1)}, bf16[1280,1280]{1,0:T(8,128)(2,1)}, u32[]{:S(2)}) copy-start(bf16[1280,1280]{1,0:T(8,128)(2,1)} %param.19) | copy-start | bytes 9830404
  6.5 5.8 %copy-start.11 = (bf16[1280]{0:T(1024)(128)(2,1)S(1)}, bf16[1280]{0:T(1024)(128)(2,1)}, u32[]{:S(2)}) copy-start(bf16[1280]{0:T(1024)(128)(2,1)} %param.14) | copy-start | bytes 7684
  6.5 136.1 %all-gather.2.cloned.1.call-start = ((), (), s32[]{:S(2)}) async-start(), calls=%async_computation.1 | async-start | bytes 4096000 | tf_op jit(solution)/shard_map/all_gather | solution.py:285
  7.3 273.4 %all-reduce.2.cloned.1.call-start = ((), (), s32[]{:S(2)}) async-start(), calls=%async_computation.2 | async-start | bytes 5242880 | tf_op jit(solution)/shard_map/psum | solution.py:312
  7.3 5.1 %copy-start.1 = (bf16[1024,1280]{1,0:T(8,128)(2,1)S(1)}, bf16[1024,1280]{1,0:T(8,128)(2,1)}, u32[]{:S(2)}) copy-start(bf16[1024,1280]{1,0:T(8,128)(2,1)} %tokens_ref.1) | copy-start | bytes 7864324
  7.3 5.1 %copy-start.16 = (bf16[1280,3,320]{0,2,1:T(8,128)(2,1)S(1)}, bf16[1280,3,320]{0,2,1:T(8,128)(2,1)}, u32[]{:S(2)}) copy-start(bf16[1280,3,320]{0,2,1:T(8,128)(2,1)} %param.15) | copy-start | bytes 7372804
  15.3 3.6 %copy-start.14 = (s32[1024]{0:T(1024)S(1)}, s32[1024]{0:T(1024)}, u32[]{:S(2)}) copy-start(s32[1024]{0:T(1024)} %param.13) | copy-start | bytes 12292
  18.8 0.6 copy-start.9
  93.2 1.2 copy-start.3
  94.5 1.0 copy-start.6
  95.5 1.9 copy-start.7
  97.4 45.2 %copy-start.12 = (bf16[1280]{0:T(1024)(128)(2,1)S(1)}, bf16[1280]{0:T(1024)(128)(2,1)}, u32[]{:S(2)}) copy-start(bf16[1280]{0:T(1024)(128)(2,1)} %param.17) | copy-start | bytes 7684
  137.2 1.0 copy-start.4
  142.6 1.7 copy-start.2
  144.4 1.1 copy-start.5
  190.6 21.0 %copy-start.13 = (bf16[1280]{0:T(1024)(128)(2,1)S(1)}, bf16[1280]{0:T(1024)(128)(2,1)}, u32[]{:S(2)}) copy-start(bf16[1280]{0:T(1024)(128)(2,1)} %param.20) | copy-start | bytes 7684
  190.6 21.0 %copy-start.15 = (s32[256,4]{0,1:T(4,128)S(1)}, s32[256,4]{0,1:T(4,128)}, u32[]{:S(2)}) copy-start(s32[256,4]{0,1:T(4,128)} %param.22) | copy-start | bytes 12292
  211.5 3.0 copy-start.10
  280.7 4.0 %copy-start.8 = (bf16[1024,1280]{1,0:T(8,128)(2,1)S(1)}, bf16[1024,1280]{1,0:T(8,128)(2,1)}, u32[]{:S(2)}) copy-start(bf16[1024,1280]{1,0:T(8,128)(2,1)} %all-reduce.2.cloned.1.call-done) | copy-start | bytes 7864324
  280.7 7.8 %slice-start = ((s8[5242880]{0:T(1024)(128)(4,1)}), s8[4194304]{0:T(1024)(128)(4,1)S(1)}, s32[]{:S(2)}) async-start(s8[5242880]{0:T(1024)(128)(4,1)} %bitcast.49), calls=%async_computation.3 | async-start | bytes 8388608
  284.7 3.8 %slice-start.1 = ((s8[5242880]{0:T(1024)(128)(4,1)}), s8[1048576]{0:T(1024)(128)(4,1)S(1)}, s32[]{:S(2)}) async-start(s8[5242880]{0:T(1024)(128)(4,1)} %bitcast.49), calls=%async_computation.4 | async-start | bytes 2097152
Sparse Core Ops, SparseCore 0:
  9.0 43.8 all-gather.1
  211.7 68.9 all-reduce.1

commit v4 on v3

--- a/solution.py
+++ b/solution.py
@@ -104,27 +104,40 @@
     for d in NEAR:
         pl.semaphore_signal(barrier, inc=1, device_id=peer(d), device_id_type=MESH_IDS)
     pl.semaphore_wait(barrier, len(NEAR))
-    copies = []
-    for index, d in enumerate(NEAR):
-        for a, (src, dst) in enumerate(zip(sources, windows(2 - d))):
+    odd = lax.rem(me, 2)
+
+    def send(kind, slices, targets, d):
+        out = []
+        for a, (src, dst) in enumerate(zip(slices, targets)):
             copy = pltpu.make_async_remote_copy(
                 src_ref=src,
                 dst_ref=dst,
-                send_sem=send_sem.at[3 * index + a],
-                recv_sem=recv_sem.at[3 * index + a],
+                send_sem=send_sem.at[3 * kind + a],
+                recv_sem=recv_sem.at[3 * kind + a],
                 device_id=peer(d),
                 device_id_type=MESH_IDS,
             )
             copy.start()
-            copies.append(copy)
+            out.append(copy)
+        return out
+
+    right = send(0, sources, windows(1), 1)
+    left = send(1, sources, windows(3), -1)
+    far = send(2, sources, windows(4 * odd), 2 - 4 * odd)
     local = []
     for a, (src, dst) in enumerate(zip(sources, windows(2))):
         copy = pltpu.make_async_copy(src, dst, local_sem.at[a])
         copy.start()
         local.append(copy)
+    for a in range(3):
+        right[a].wait_recv()
+        left[a].wait_recv()
+    relay = send(3, windows(1 + 2 * odd), windows(4 * odd), 1 - 2 * odd)
     for copy in local:
         copy.wait()
-    for copy in copies:
+    for copy in right + left:
+        copy.wait_send()
+    for copy in far + relay:
         copy.wait()
 
 
@@ -143,8 +156,8 @@
         in_specs=[any_spec] * 3,
         out_specs=(any_spec, any_spec, any_spec),
         scratch_shapes=[
-            pltpu.SemaphoreType.DMA((3 * len(NEAR),)),
-            pltpu.SemaphoreType.DMA((3 * len(NEAR),)),
+            pltpu.SemaphoreType.DMA((12,)),
+            pltpu.SemaphoreType.DMA((12,)),
             pltpu.SemaphoreType.DMA((3,)),
         ],
         compiler_params=pltpu.CompilerParams(collective_id=1, has_side_effects=True),

time: 338 us -> 332 us (0.982)
  waiting for transfers between devices: 65.9 us -> 61.8 us
    psum x1, waiting for transfers between devices: 65.2 us -> 61.1 us  [body(): lax.psum(hidden_terms.astype(jnp.bfloat16), 'tp').astype(jnp.float32)]
    pallas_call x1, Pallas kernels: 63.9 us -> 59.9 us  [exchange(): pl.pallas_call(functools.partial(exchange_kernel, order, n), out_shape=(j...]
  transfers between devices with their start and end apart: 2 -> 2, of which waited for: 1 -> 1; matrix products, arithmetic and copies ran while one was open for 9% -> 9% of each run, Pallas kernels for 31% -> 30%
where the time goes in v4:
time: 332 us; the launch traced here: 331 us
  Pallas kernels  141 us (42%)
  waiting for transfers between devices  61.8 us (19%)
  local copies, waits for them, and re-layouts  43.7 us (13%)
  matrix products  29 us (9%)
  other arithmetic  24.5 us (7%)
  blocking collectives  17.9 us (5%)
  between operations  13.8 us (4%)
    psum x1, waiting for transfers between devices, body(): lax.psum(hidden_terms.astype(jnp.bfloat16), 'tp').astype(jnp.float32)  61.1 us
    pallas_call x1, Pallas kernels, exchange(): pl.pallas_call(functools.partial(exchange_kernel, order, n), out_shape=(j...  59.9 us
    pallas_call x1, Pallas kernels, project(): pl.pallas_call(functools.partial(project_kernel, order), out_shape=jax.Sh...  41.1 us
    pallas_call x1, Pallas kernels, attention(): pl.pallas_call(flash_kernel, out_shape=jax.ShapeDtypeStruct(queries.shape...  39.8 us
    dot_general x1, matrix products, body(): jnp.dot(expanded, reduce_weight, preferred_element_type=jnp.float32)  20.9 us
    all_to_all x1, blocking collectives, body(): lax.all_to_all(outgoing, 'req', split_axis=0, concat_axis=0, tiled=True)  17.9 us
    gather x2, local copies, waits for them, and re-layouts, body(): jnp.take(final_normed, local_index.reshape(-1), axis=0)  13.9 us
    unnamed x40, local copies, waits for them, and re-layouts  11 us
  transfers between devices with their start and end apart: 2, of which 1 were waited for; matrix products, arithmetic and copies ran while one was open for 9% of the time, Pallas kernels for 30%

profile of v4, /device:TPU:1, one launch (start us, length us, event | category | flops | bytes accessed | tf_op | source)
XLA Modules:
  0.0 331.4 jit_solution(1922617164496653489)
XLA Ops:
  7.3 2.3 convert_reduce_fusion
  9.6 2.7 fusion.2
  12.4 2.9 fusion.27
  15.3 1.3 fusion.76
  16.6 2.2 copy.27
  19.4 59.9 %shard_map.118 = (bf16[4,80,5120]{2,1,0:T(8,128)(2,1)}, bf16[4,5120,80]{2,1,0:T(8,128)(2,1)}, s32[1,5120]{1,0:T(1,128)}) custom-call(bf16[4,80,1024]{2,1,0:T(8,128)(2,1)} %bitcast.55, bf16[4,1024,80]{2,1,0:T(8,128)(2,1)} %bitcast.52, s32[1,1024]{1,0:T(1,128)} %bitcast.60), custom_call_target="tpu_custom_call" | custom-call | tf_op jit(solution)/shard_map/pallas_call | solution.py:149
  80.3 3.6 %rev.3 = pred[4,5120]{1,0:T(4,128)(4,1)S(1)} reverse(pred[4,5120]{1,0:T(4,128)(4,1)S(1)} %compare_and_fusion), dimensions={1} | reverse | bytes 40960 | tf_op jit(solution)/shard_map/rev | solution.py:254
  83.9 2.2 copy.28
  86.1 1.7 copy.29.qm_ref
  89.3 1.2 copy-done.3
  90.5 1.0 copy-done.6
  91.6 1.9 copy-done.7
  93.5 39.8 %shard_map.119 = bf16[4,1024,80]{2,1,0:T(8,128)(2,1)S(1)} custom-call(s32[2,4]{1,0:T(2,128)S(1)} %pad_add_fusion.bounds, bf16[4,1024,80]{2,1,0:T(8,128)(2,1)S(1)} %bitcast.45, s32[1024,1]{1,0:T(8,128)S(1)} %copy-done.6, bf16[4,80,5120]{2,1,0:T(8,128)(2,1)S(1)} %copy-done.7, bf16[4,5120,80]{2,1,0:T(8,128)(2,1)} %get-tuple-element.14.v_ref, ...), custom_call_target="tpu_custom_call" | custom-call | flops 2684354560 | bytes 7864320 | tf_op jit(solution)/shard_map/pallas_call | solution.py:256
  133.3 1.0 copy-done.4
  134.3 2.2 copy.30
  136.4 2.2 copy.31.ctx_ref
  138.7 1.7 copy-done.2
  140.4 1.1 copy-done.5
  141.6 41.1 %shard_map.120 = f32[1024,1280]{1,0:T(8,128)} custom-call(bf16[1024,320]{1,0:T(8,128)(2,1)S(1)} %copy-done.5, bf16[1280,1280]{1,0:T(8,128)(2,1)} %all-gather.2.cloned.1.call-done.weight_ref, bf16[1024,1280]{1,0:T(8,128)(2,1)S(1)} %copy-done.2), custom_call_target="tpu_custom_call" | custom-call | flops 3355443200 | bytes 13762560 | tf_op jit(solution)/shard_map/pallas_call | solution.py:173
  182.6 2.8 reduce_sum.69
  185.4 3.1 multiply_reduce_fusion.1
  188.6 20.9 %convolution_convert_fusion = bf16[1024,1280]{1,0:T(8,128)(2,1)} fusion(bf16[1280,1280]{1,0:T(8,128)(2,1)S(1)} %copy-done, bf16[1280,1280]{1,0:T(8,128)(2,1)} %param.18, f32[1024,1280]{1,0:T(8,128)} %shard_map.120, f32[1280]{0:T(1024)S(1)} %convert_element_type.50, f32[1024]{0:T(1024)S(1)} %add_rsqrt_fusion.1, f32[1024]{0:T(1024)S(1)} %broadcast_multiply_fusion.1), kind=kOutput, calls=%fused_computation.32 | convolution fusion | flops 6802636800 | bytes 14431232 | tf_op jit(solution)/shard_map/dot_general | solution.py:324
  210.8 1.7 copy.35
  213.5 61.1 %all-reduce.2.cloned.1.call-done = bf16[1024,1280]{1,0:T(8,128)(2,1)} async-done(((bf16[1024,1280]{1,0:T(8,128)(2,1)}), bf16[1024,1280]{1,0:T(8,128)(2,1)}) %all-reduce.2.cloned.1.call-update) | async-done | bytes 2621456 | tf_op jit(solution)/shard_map/psum | solution.py:325
  274.6 4.0 %fusion.26 = f32[1024]{0:T(1024)S(1)} fusion(f32[1024,1280]{1,0:T(8,128)} %shard_map.120, bf16[1024,1280]{1,0:T(8,128)(2,1)} %all-reduce.2.cloned.1.call-done), kind=kLoop, calls=%fused_computation.43 | loop fusion | flops 3931136 | bytes 7868416 | tf_op jit(solution)/shard_map/reduce_sum | solution.py:201
  278.6 3.7 %multiply_reduce_fusion = f32[1024]{0:T(1024)S(1)} fusion(f32[1024]{0:T(1024)S(1)} %broadcast_multiply_fusion, f32[1024,1280]{1,0:T(8,128)} %shard_map.120, bf16[1024,1280]{1,0:T(8,128)(2,1)S(1)} %copy-done.8), kind=kLoop, calls=%fused_computation.13 | loop fusion | flops 6552576 | bytes 7872512 | tf_op jit(solution)/shard_map/reduce_sum | solution.py:203
  282.4 2.6 multiply_convert_fusion
  285.0 8.7 %gather_fusion = bf16[1024,1280]{1,0:T(8,128)(2,1)} fusion(bf16[1024,1280]{1,0:T(8,128)(2,1)} %multiply_convert_fusion, s32[1024]{0:T(1024)S(1)} %broadcast_clamp_fusion), kind=kCustom, calls=%fused_computation | custom fusion | bytes 5246976 | tf_op jit(solution)/shard_map/jit(_take)/gather | solution.py:329
  293.7 5.2 %gather.7 = bf16[256,5120]{1,0:T(8,128)(2,1)} reshape(bf16[1024,1280]{1,0:T(8,128)(2,1)} %gather_fusion) | data formatting | bytes 5242880 | tf_op jit(solution)/shard_map/jit(_take)/gather | solution.py:329
  298.9 5.2 %convolution_convert_fusion.1 = bf16[512,320]{0,1:T(8,128)(2,1)} fusion(bf16[5120,320]{0,1:T(8,128)(2,1)} %param.21, pred[256,5120]{1,0:T(8,128)(4,1)} %bitcast.59, bf16[256,5120]{1,0:T(8,128)(2,1)} %gather.7, s32[256]{0:T(256)S(1)} %bitcast.66), kind=kOutput, calls=%fused_computation.46 | convolution fusion | flops 924434432 | bytes 7537664 | tf_op jit(solution)/shard_map/ms,mc->sc/dot_general | solution.py:342
  304.1 1.9 copy.33
  306.0 17.9 %all_to_all.5 = bf16[32,16,320]{2,1,0:T(8,128)(2,1)S(1)} all-to-all(bf16[32,16,320]{2,1,0:T(8,128)(2,1)} %bitcast.58), channel_id=1, replica_groups=mesh['req'=32,'tp'=4] {'req'}, dimensions={0} | all-to-all | bytes 655360 | tf_op jit(solution)/shard_map/all_to_all | solution.py:346
  (71 shorter events, 6.7 us)
Async XLA Ops:
  6.5 182.0 %copy-start = (bf16[1280,1280]{1,0:T(8,128)(2,1)S(1)}, bf16[1280,1280]{1,0:T(8,128)(2,1)}, u32[]{:S(2)}) copy-start(bf16[1280,1280]{1,0:T(8,128)(2,1)} %param.19) | copy-start | bytes 9830404
  6.5 5.8 %copy-start.11 = (bf16[1280]{0:T(1024)(128)(2,1)S(1)}, bf16[1280]{0:T(1024)(128)(2,1)}, u32[]{:S(2)}) copy-start(bf16[1280]{0:T(1024)(128)(2,1)} %param.14) | copy-start | bytes 7684
  6.5 132.1 %all-gather.2.cloned.1.call-start = ((), (), s32[]{:S(2)}) async-start(), calls=%async_computation.1 | async-start | bytes 4096000 | tf_op jit(solution)/shard_map/all_gather | solution.py:298
  7.3 267.3 %all-reduce.2.cloned.1.call-start = ((), (), s32[]{:S(2)}) async-start(), calls=%async_computation.2 | async-start | bytes 5242880 | tf_op jit(solution)/shard_map/psum | solution.py:325
  7.3 5.1 %copy-start.1 = (bf16[1024,1280]{1,0:T(8,128)(2,1)S(1)}, bf16[1024,1280]{1,0:T(8,128)(2,1)}, u32[]{:S(2)}) copy-start(bf16[1024,1280]{1,0:T(8,128)(2,1)} %tokens_ref.1) | copy-start | bytes 7864324
  7.3 5.1 %copy-start.16 = (bf16[1280,3,320]{0,2,1:T(8,128)(2,1)S(1)}, bf16[1280,3,320]{0,2,1:T(8,128)(2,1)}, u32[]{:S(2)}) copy-start(bf16[1280,3,320]{0,2,1:T(8,128)(2,1)} %param.15) | copy-start | bytes 7372804
  15.3 3.6 %copy-start.14 = (s32[1024]{0:T(1024)S(1)}, s32[1024]{0:T(1024)}, u32[]{:S(2)}) copy-start(s32[1024]{0:T(1024)} %param.13) | copy-start | bytes 12292
  18.8 0.6 copy-start.9
  89.3 1.2 copy-start.3
  90.5 1.0 copy-start.6
  91.5 1.9 copy-start.7
  93.5 45.2 %copy-start.12 = (bf16[1280]{0:T(1024)(128)(2,1)S(1)}, bf16[1280]{0:T(1024)(128)(2,1)}, u32[]{:S(2)}) copy-start(bf16[1280]{0:T(1024)(128)(2,1)} %param.17) | copy-start | bytes 7684
  133.3 1.0 copy-start.4
  138.7 1.7 copy-start.2
  140.4 1.1 copy-start.5
  188.6 21.0 %copy-start.13 = (bf16[1280]{0:T(1024)(128)(2,1)S(1)}, bf16[1280]{0:T(1024)(128)(2,1)}, u32[]{:S(2)}) copy-start(bf16[1280]{0:T(1024)(128)(2,1)} %param.20) | copy-start | bytes 7684
  188.6 21.0 %copy-start.15 = (s32[256,4]{0,1:T(4,128)S(1)}, s32[256,4]{0,1:T(4,128)}, u32[]{:S(2)}) copy-start(s32[256,4]{0,1:T(4,128)} %param.22) | copy-start | bytes 12292
  209.6 3.0 copy-start.10
  274.6 4.0 %copy-start.8 = (bf16[1024,1280]{1,0:T(8,128)(2,1)S(1)}, bf16[1024,1280]{1,0:T(8,128)(2,1)}, u32[]{:S(2)}) copy-start(bf16[1024,1280]{1,0:T(8,128)(2,1)} %all-reduce.2.cloned.1.call-done) | copy-start | bytes 7864324
  274.6 7.8 %slice-start = ((s8[5242880]{0:T(1024)(128)(4,1)}), s8[4194304]{0:T(1024)(128)(4,1)S(1)}, s32[]{:S(2)}) async-start(s8[5242880]{0:T(1024)(128)(4,1)} %bitcast.49), calls=%async_computation.3 | async-start | bytes 8388608
  278.6 3.8 %slice-start.1 = ((s8[5242880]{0:T(1024)(128)(4,1)}), s8[1048576]{0:T(1024)(128)(4,1)S(1)}, s32[]{:S(2)}) async-start(s8[5242880]{0:T(1024)(128)(4,1)} %bitcast.49), calls=%async_computation.4 | async-start | bytes 2097152
Sparse Core Ops, SparseCore 0:
  9.0 43.8 all-gather.1
  209.7 64.8 all-reduce.1

commit v5 on v4

--- a/solution.py
+++ b/solution.py
@@ -250,8 +250,9 @@
     low = query_marks.reshape(tiles, TILE).min(axis=1)
     high = query_marks.reshape(tiles, TILE).max(axis=1)
     valid = (key_marks[None, :] >= low[:, None]) & (key_marks[None, :] <= high[:, None])
-    first = jnp.argmax(valid, axis=1)
-    last = key_rows - 1 - jnp.argmax(valid[:, ::-1], axis=1)
+    place = jnp.arange(key_rows, dtype=jnp.int32)[None, :]
+    first = jnp.min(jnp.where(valid, place, key_rows), axis=1)
+    last = jnp.max(jnp.where(valid, place, -1), axis=1)
     bounds = jnp.stack([first // TILE, last // TILE + 1]).astype(jnp.int32)
     return pl.pallas_call(
         flash_kernel,
@@ -326,9 +327,10 @@
     final_normed = layer_norm(final_stream, output_gain).astype(jnp.bfloat16)
     merged_rows = merge_index.shape[0]
     local_index = merge_index - lax.axis_index("req") * token_rows
-    merged = jnp.take(final_normed, local_index.reshape(-1), axis=0).reshape(
-        merged_rows, 4 * final_normed.shape[1]
-    )
+    picks = (local_index[:, :, None] == jnp.arange(token_rows, dtype=jnp.int32)).astype(jnp.bfloat16)
+    merged = jnp.einsum(
+        "mkt,tc->mkc", picks, final_normed, preferred_element_type=jnp.float32
+    ).astype(jnp.bfloat16).reshape(merged_rows, 4 * final_normed.shape[1])
     feature = jnp.dot(merged, merge_weight, preferred_element_type=jnp.float32).astype(jnp.bfloat16)
     peers = lax.axis_size("req")
     capacity = 2 * merged_rows // peers

time: 332 us -> 323 us (0.973)
  local copies, waits for them, and re-layouts: 43.7 us -> 26.6 us
  waiting for transfers between devices: 61.8 us -> 71.2 us
  matrix products: 29 us -> 33.7 us
  Pallas kernels: 141 us -> 137 us
    gather x2 -> x0, local copies, waits for them, and re-layouts: 13.9 us -> none  [body(): jnp.take(final_normed, local_index.reshape(-1), axis=0)]
    psum x1, waiting for transfers between devices: 61.1 us -> 70.5 us  [body(): lax.psum(hidden_terms.astype(jnp.bfloat16), 'tp').astype(jnp.float32)]
    dot_general x0 -> x1, matrix products: none -> 5.14 us  [body(): jnp.einsum('mkt,tc->mkc', picks, final_normed, preferred_element_type=jnp...]
    convert_element_type x0 -> x1, local copies, waits for them, and re-layouts: none -> 4.38 us  [body(): merged = jnp.einsum('mkt,tc->mkc', picks, final_normed, preferred_element...]
    pallas_call x1, Pallas kernels: 41.1 us -> 36.9 us  [project(): pl.pallas_call(functools.partial(project_kernel, order), out_shape=jax.Sh...]
    rev x1 -> x0, local copies, waits for them, and re-layouts: 3.65 us -> none  [attention(): last = key_rows - 1 - jnp.argmax(valid[:, ::-1], axis=1)]
    unnamed x40 -> x37, local copies, waits for them, and re-layouts: 11 us -> 8.84 us
  transfers between devices with their start and end apart: 2 -> 2, of which waited for: 1 -> 1; matrix products, arithmetic and copies ran while one was open for 9% -> 7% of each run, Pallas kernels for 30% -> 31%
where the time goes in v5:
time: 323 us; the launch traced here: 322 us
  Pallas kernels  137 us (42%)
  waiting for transfers between devices  71.2 us (22%)
  matrix products  33.7 us (10%)
  local copies, waits for them, and re-layouts  26.6 us (8%)
  other arithmetic  22.2 us (7%)
  blocking collectives  17.8 us (6%)
  between operations  13.7 us (4%)
    psum x1, waiting for transfers between devices, body(): lax.psum(hidden_terms.astype(jnp.bfloat16), 'tp').astype(jnp.float32)  70.5 us
    pallas_call x1, Pallas kernels, exchange(): pl.pallas_call(functools.partial(exchange_kernel, order, n), out_shape=(j...  59.9 us
    pallas_call x1, Pallas kernels, attention(): pl.pallas_call(flash_kernel, out_shape=jax.ShapeDtypeStruct(queries.shape...  39.8 us
    pallas_call x1, Pallas kernels, project(): pl.pallas_call(functools.partial(project_kernel, order), out_shape=jax.Sh...  36.9 us
    dot_general x1, matrix products, body(): jnp.dot(expanded, reduce_weight, preferred_element_type=jnp.float32)  20.9 us
    all_to_all x1, blocking collectives, body(): lax.all_to_all(outgoing, 'req', split_axis=0, concat_axis=0, tiled=True)  17.8 us
    reduce_sum x3, other arithmetic, layer_norm(): center = jnp.mean(stream, axis=-1, keepdims=True)  9.63 us
    reduce_sum x3, other arithmetic, layer_norm(): spread = jnp.mean(shifted * shifted, axis=-1, keepdims=True)  9.44 us
  transfers between devices with their start and end apart: 2, of which 1 were waited for; matrix products, arithmetic and copies ran while one was open for 7% of the time, Pallas kernels for 31%

profile of v5, /device:TPU:1, one launch (start us, length us, event | category | flops | bytes accessed | tf_op | source)
XLA Modules:
  0.0 321.9 jit_solution(15391004164869705638)
XLA Ops:
  7.3 0.9 convert_element_type.51
  8.2 2.8 convert_reduce_fusion
  11.0 2.6 fusion.2
  13.6 2.9 fusion.33
  16.5 1.3 fusion.74
  17.9 2.2 copy.24
  20.1 2.3 copy.25
  22.4 1.1 copy.26.qm_ref
  23.4 59.9 %shard_map.118 = (bf16[4,80,5120]{2,1,0:T(8,128)(2,1)}, bf16[4,5120,80]{2,1,0:T(8,128)(2,1)}, s32[1,5120]{1,0:T(1,128)}) custom-call(bf16[4,80,1024]{2,1,0:T(8,128)(2,1)} %bitcast.69, bf16[4,1024,80]{2,1,0:T(8,128)(2,1)} %bitcast.66, s32[1,1024]{1,0:T(1,128)} %bitcast.75), custom_call_target="tpu_custom_call" | custom-call | tf_op jit(solution)/shard_map/pallas_call | solution.py:149
  83.5 0.8 and_select_fusion.km_ref
  84.6 1.2 copy-done.3
  85.8 1.0 copy-done.6
  86.9 1.9 copy-done.7
  88.8 39.8 %shard_map.119 = bf16[4,1024,80]{2,1,0:T(8,128)(2,1)S(1)} custom-call(s32[2,4]{1,0:T(2,128)S(1)} %pad_add_fusion.bounds, bf16[4,1024,80]{2,1,0:T(8,128)(2,1)S(1)} %bitcast.61, s32[1024,1]{1,0:T(8,128)S(1)} %copy-done.6, bf16[4,80,5120]{2,1,0:T(8,128)(2,1)S(1)} %copy-done.7, bf16[4,5120,80]{2,1,0:T(8,128)(2,1)} %get-tuple-element.10.v_ref, ...), custom_call_target="tpu_custom_call" | custom-call | flops 2684354560 | bytes 7864320 | tf_op jit(solution)/shard_map/pallas_call | solution.py:257
  128.6 1.0 copy-done.4
  129.6 2.2 copy.27
  131.8 2.2 copy.28.ctx_ref
  134.0 1.7 copy-done.2
  135.8 1.1 copy-done.5
  136.9 36.9 %shard_map.120 = f32[1024,1280]{1,0:T(8,128)} custom-call(bf16[1024,320]{1,0:T(8,128)(2,1)S(1)} %copy-done.5, bf16[1280,1280]{1,0:T(8,128)(2,1)} %all-gather.2.cloned.1.call-done.weight_ref, bf16[1024,1280]{1,0:T(8,128)(2,1)S(1)} %copy-done.2), custom_call_target="tpu_custom_call" | custom-call | flops 3355443200 | bytes 13762560 | tf_op jit(solution)/shard_map/pallas_call | solution.py:173
  173.8 2.8 reduce_sum.69
  176.6 3.1 multiply_reduce_fusion.1
  179.8 20.9 %convolution_convert_fusion = bf16[1024,1280]{1,0:T(8,128)(2,1)} fusion(bf16[1280,1280]{1,0:T(8,128)(2,1)S(1)} %copy-done, bf16[1280,1280]{1,0:T(8,128)(2,1)} %param.18, f32[1024,1280]{1,0:T(8,128)} %shard_map.120, f32[1280]{0:T(1024)S(1)} %convert_element_type.54, f32[1024]{0:T(1024)S(1)} %add_rsqrt_fusion.1, f32[1024]{0:T(1024)S(1)} %broadcast_multiply_fusion.1), kind=kOutput, calls=%fused_computation.34 | convolution fusion | flops 6802636800 | bytes 14431232 | tf_op jit(solution)/shard_map/dot_general | solution.py:325
  200.8 0.8 reduce-window.6
  202.0 70.5 %all-reduce.2.cloned.1.call-done = bf16[1024,1280]{1,0:T(8,128)(2,1)} async-done(((bf16[1024,1280]{1,0:T(8,128)(2,1)}), bf16[1024,1280]{1,0:T(8,128)(2,1)}) %all-reduce.2.cloned.1.call-update) | async-done | bytes 2621456 | tf_op jit(solution)/shard_map/psum | solution.py:326
  272.5 4.0 %fusion.32 = f32[1024]{0:T(1024)S(1)} fusion(f32[1024,1280]{1,0:T(8,128)} %shard_map.120, bf16[1024,1280]{1,0:T(8,128)(2,1)} %all-reduce.2.cloned.1.call-done), kind=kLoop, calls=%fused_computation.48 | loop fusion | flops 3931136 | bytes 7868416 | tf_op jit(solution)/shard_map/reduce_sum | solution.py:201
  276.6 3.7 %multiply_reduce_fusion = f32[1024]{0:T(1024)S(1)} fusion(f32[1024]{0:T(1024)S(1)} %broadcast_multiply_fusion, f32[1024,1280]{1,0:T(8,128)} %shard_map.120, bf16[1024,1280]{1,0:T(8,128)(2,1)S(1)} %copy-done.8), kind=kLoop, calls=%fused_computation.12 | loop fusion | flops 6552576 | bytes 7872512 | tf_op jit(solution)/shard_map/reduce_sum | solution.py:203
  280.3 5.1 %fusion.16 = bf16[256,4,1280]{2,0,1:T(8,128)(2,1)} fusion(f32[1280]{0:T(1024)S(1)} %convert_element_type.59, f32[1024]{0:T(1024)S(1)} %add_rsqrt_fusion, f32[1024]{0:T(1024)S(1)} %broadcast_multiply_fusion, s32[256,4]{0,1:T(4,128)S(1)} %broadcast_subtract_fusion, f32[1024,1280]{1,0:T(8,128)S(1)} %bitcast.65, bf16[1024,1280]{1,0:T(8,128)(2,1)S(1)} %copy-done.8), kind=kOutput, calls=%fused_computation.33 | convolution fusion | flops 2694578176 | bytes 10503168 | tf_op jit(solution)/shard_map/mkt,tc->mkc/dot_general | solution.py:331
  285.5 4.4 %copy.29 = bf16[256,4,1280]{0,2,1:T(8,128)(2,1)} copy(bf16[256,4,1280]{2,0,1:T(8,128)(2,1)} %fusion.16) | data formatting | bytes 5242880 | tf_op jit(solution)/shard_map/convert_element_type | solution.py:333
  289.9 4.8 %convolution_convert_fusion.1 = bf16[512,320]{0,1:T(8,128)(2,1)} fusion(bf16[5120,320]{0,1:T(8,128)(2,1)} %param.21, bf16[256,5120]{0,1:T(8,128)(2,1)} %bitcast.67, s32[256]{0:T(256)S(1)} %bitcast.79), kind=kOutput, calls=%fused_computation.50 | convolution fusion | flops 923123712 | bytes 6226944 | tf_op jit(solution)/shard_map/ms,mc->sc/dot_general | solution.py:344
  294.6 1.9 copy.30
  296.5 17.8 %all_to_all.5 = bf16[32,16,320]{2,1,0:T(8,128)(2,1)S(1)} all-to-all(bf16[32,16,320]{2,1,0:T(8,128)(2,1)} %bitcast.73), channel_id=1, replica_groups=mesh['req'=32,'tp'=4] {'req'}, dimensions={0} | all-to-all | bytes 655360 | tf_op jit(solution)/shard_map/all_to_all | solution.py:348
  (58 shorter events, 2.4 us)
Async XLA Ops:
  6.5 173.3 %copy-start = (bf16[1280,1280]{1,0:T(8,128)(2,1)S(1)}, bf16[1280,1280]{1,0:T(8,128)(2,1)}, u32[]{:S(2)}) copy-start(bf16[1280,1280]{1,0:T(8,128)(2,1)} %param.19) | copy-start | bytes 9830404
  6.5 127.5 %all-gather.2.cloned.1.call-start = ((), (), s32[]{:S(2)}) async-start(), calls=%async_computation.1 | async-start | bytes 4096000 | tf_op jit(solution)/shard_map/all_gather | solution.py:299
  7.3 265.2 %all-reduce.2.cloned.1.call-start = ((), (), s32[]{:S(2)}) async-start(), calls=%async_computation.2 | async-start | bytes 5242880 | tf_op jit(solution)/shard_map/psum | solution.py:326
  7.3 6.3 %copy-start.1 = (bf16[1024,1280]{1,0:T(8,128)(2,1)S(1)}, bf16[1024,1280]{1,0:T(8,128)(2,1)}, u32[]{:S(2)}) copy-start(bf16[1024,1280]{1,0:T(8,128)(2,1)} %tokens_ref.1) | copy-start | bytes 7864324
  7.3 6.3 %copy-start.15 = (bf16[1280,3,320]{0,2,1:T(8,128)(2,1)S(1)}, bf16[1280,3,320]{0,2,1:T(8,128)(2,1)}, u32[]{:S(2)}) copy-start(bf16[1280,3,320]{0,2,1:T(8,128)(2,1)} %param.15) | copy-start | bytes 7372804
  16.5 3.6 %copy-start.13 = (s32[1024]{0:T(1024)S(1)}, s32[1024]{0:T(1024)}, u32[]{:S(2)}) copy-start(s32[1024]{0:T(1024)} %param.13) | copy-start | bytes 12292
  20.1 3.3 %copy-start.9 = (s32[1024]{0:T(1024)}, s32[1024]{0:T(1024)S(1)}, u32[]{:S(2)}) copy-start(s32[1024]{0:T(1024)S(1)} %broadcast_add_fusion) | copy-start | bytes 12292
  84.6 1.2 copy-start.3
  85.8 1.0 copy-start.6
  86.9 1.9 copy-start.7
  88.8 45.2 %copy-start.11 = (bf16[1280]{0:T(1024)(128)(2,1)S(1)}, bf16[1280]{0:T(1024)(128)(2,1)}, u32[]{:S(2)}) copy-start(bf16[1280]{0:T(1024)(128)(2,1)} %param.17) | copy-start | bytes 7684
  128.6 1.0 copy-start.4
  134.0 1.7 copy-start.2
  135.8 1.1 copy-start.5
  179.8 21.0 %copy-start.12 = (bf16[1280]{0:T(1024)(128)(2,1)S(1)}, bf16[1280]{0:T(1024)(128)(2,1)}, u32[]{:S(2)}) copy-start(bf16[1280]{0:T(1024)(128)(2,1)} %param.20) | copy-start | bytes 7684
  179.8 21.0 %copy-start.10 = (s32[256,1]{0,1:T(1,128)S(1)}, s32[256,1]{0,1:T(1,128)}, u32[]{:S(2)}) copy-start(s32[256,1]{0,1:T(1,128)} %param.23) | copy-start | bytes 3076
  179.8 22.1 %copy-start.14 = (s32[256,4]{0,1:T(4,128)S(1)}, s32[256,4]{0,1:T(4,128)}, u32[]{:S(2)}) copy-start(s32[256,4]{0,1:T(4,128)} %param.22) | copy-start | bytes 12292
  272.5 4.0 %copy-start.8 = (bf16[1024,1280]{1,0:T(8,128)(2,1)S(1)}, bf16[1024,1280]{1,0:T(8,128)(2,1)}, u32[]{:S(2)}) copy-start(bf16[1024,1280]{1,0:T(8,128)(2,1)} %all-reduce.2.cloned.1.call-done) | copy-start | bytes 7864324
  272.5 7.8 %slice-start = ((s8[5242880]{0:T(1024)(128)(4,1)}), s8[4194304]{0:T(1024)(128)(4,1)S(1)}, s32[]{:S(2)}) async-start(s8[5242880]{0:T(1024)(128)(4,1)} %bitcast.64), calls=%async_computation.3 | async-start | bytes 8388608
  276.5 3.8 %slice-start.1 = ((s8[5242880]{0:T(1024)(128)(4,1)}), s8[1048576]{0:T(1024)(128)(4,1)S(1)}, s32[]{:S(2)}) async-start(s8[5242880]{0:T(1024)(128)(4,1)} %bitcast.64), calls=%async_computation.4 | async-start | bytes 2097152
Sparse Core Ops, SparseCore 0:
  9.0 43.8 all-gather.1
  200.9 71.5 all-reduce.1

commit v6 on v5

--- a/solution.py
+++ b/solution.py
@@ -165,6 +165,53 @@
     source = lax.axis_index("req") + jnp.arange(slots * span, dtype=jnp.int32) // span - max(NEAR)
     present = (source >= 0) & (source < n)
     return keys_all, values_all, jnp.where(present, marks_all[0], 0)
+
+
+def deliver_kernel(order, n, outgoing_ref, received_ref, send_sem, recv_sem, local_sem):
+    me = lax.axis_index("req")
+    place = {"req": me, "tp": lax.axis_index("tp")}
+
+    def peer(k):
+        where = dict(place, req=lax.rem(me + k, n))
+        return tuple(where[a] for a in order)
+
+    barrier = pltpu.get_barrier_semaphore()
+    for k in range(1, n):
+        pl.semaphore_signal(barrier, inc=1, device_id=peer(k), device_id_type=MESH_IDS)
+    pl.semaphore_wait(barrier, n - 1)
+    copies = []
+    for k in range(1, n):
+        copy = pltpu.make_async_remote_copy(
+            src_ref=outgoing_ref.at[lax.rem(me + k, n)],
+            dst_ref=received_ref.at[me],
+            send_sem=send_sem.at[k],
+            recv_sem=recv_sem.at[k],
+            device_id=peer(k),
+            device_id_type=MESH_IDS,
+        )
+        copy.start()
+        copies.append(copy)
+    own = pltpu.make_async_copy(outgoing_ref.at[me], received_ref.at[me], local_sem.at[0])
+    own.start()
+    own.wait()
+    for copy in copies:
+        copy.wait()
+
+
+def deliver(outgoing, order):
+    n = lax.axis_size("req")
+    return pl.pallas_call(
+        functools.partial(deliver_kernel, order, n),
+        out_shape=jax.ShapeDtypeStruct(outgoing.shape, outgoing.dtype),
+        in_specs=[pl.BlockSpec(memory_space=pltpu.VMEM)],
+        out_specs=pl.BlockSpec(memory_space=pltpu.VMEM),
+        scratch_shapes=[
+            pltpu.SemaphoreType.DMA((n,)),
+            pltpu.SemaphoreType.DMA((n,)),
+            pltpu.SemaphoreType.DMA((1,)),
+        ],
+        compiler_params=pltpu.CompilerParams(collective_id=2, has_side_effects=True),
+    )(outgoing)
 
 
 def project(context, weight, tokens, order):
@@ -345,7 +392,7 @@
         "ms,mc->sc", placement, feature, preferred_element_type=jnp.float32
     ).astype(jnp.bfloat16)
     outgoing = outgoing.reshape(peers, capacity, feature.shape[1])
-    received = lax.all_to_all(outgoing, "req", split_axis=0, concat_axis=0, tiled=True)
+    received = deliver(outgoing, order)
     return received.reshape(1, peers, capacity, feature.shape[1])
 
 

time: 323 us -> 322 us (level)
  blocking collectives: 17.8 us -> 0 us
  waiting for transfers between devices: 71.2 us -> 81.6 us
  Pallas kernels: 137 us -> 143 us
    all_to_all x1 -> x0, blocking collectives: 17.8 us -> none  [body(): lax.all_to_all(outgoing, 'req', split_axis=0, concat_axis=0, tiled=True)]
    pallas_call x0 -> x1, Pallas kernels: none -> 14.6 us  [deliver(): pl.pallas_call(functools.partial(deliver_kernel, order, n), out_shape=jax...]
    pallas_call x1, Pallas kernels: 39.8 us -> 29.1 us  [attention(): pl.pallas_call(flash_kernel, out_shape=jax.ShapeDtypeStruct(queries.shape...]
    psum x1, waiting for transfers between devices: 70.5 us -> 80.9 us  [body(): lax.psum(hidden_terms.astype(jnp.bfloat16), 'tp').astype(jnp.float32)]
  transfers between devices with their start and end apart: 2 -> 2, of which waited for: 1 -> 1; matrix products, arithmetic and copies ran while one was open for 7% -> 7% of each run, Pallas kernels for 31% -> 28%
where the time goes in v6:
time: 322 us
  Pallas kernels  143 us (44%)
  waiting for transfers between devices  81.6 us (25%)
  matrix products  33.7 us (10%)
  local copies, waits for them, and re-layouts  27.6 us (9%)
  other arithmetic  22.2 us (7%)
  between operations  13.7 us (4%)
    psum x1, waiting for transfers between devices, body(): lax.psum(hidden_terms.astype(jnp.bfloat16), 'tp').astype(jnp.float32)  80.9 us
    pallas_call x1, Pallas kernels, exchange(): pl.pallas_call(functools.partial(exchange_kernel, order, n), out_shape=(j...  59.9 us
    pallas_call x1, Pallas kernels, project(): pl.pallas_call(functools.partial(project_kernel, order), out_shape=jax.Sh...  39.1 us
    pallas_call x1, Pallas kernels, attention(): pl.pallas_call(flash_kernel, out_shape=jax.ShapeDtypeStruct(queries.shape...  29.1 us
    dot_general x1, matrix products, body(): jnp.dot(expanded, reduce_weight, preferred_element_type=jnp.float32)  20.9 us
    pallas_call x1, Pallas kernels, deliver(): pl.pallas_call(functools.partial(deliver_kernel, order, n), out_shape=jax...  14.6 us
    unnamed x37, local copies, waits for them, and re-layouts  9.88 us
    reduce_sum x3, other arithmetic, layer_norm(): center = jnp.mean(stream, axis=-1, keepdims=True)  9.63 us
  transfers between devices with their start and end apart: 2, of which 1 were waited for; matrix products, arithmetic and copies ran while one was open for 7% of the time, Pallas kernels for 28%

profile of v6, /device:TPU:1, one launch (start us, length us, event | category | flops | bytes accessed | tf_op | source)
XLA Modules:
  0.0 321.5 jit_solution(15446102739480024502)
XLA Ops:
  7.3 0.9 convert_element_type.51
  8.2 2.8 convert_reduce_fusion
  11.0 2.6 fusion.2
  13.6 2.9 fusion.33
  16.5 1.3 fusion.74
  17.9 2.2 copy.24
  20.1 2.3 copy.25
  22.4 1.1 copy.26.qm_ref
  23.4 59.9 %shard_map.118 = (bf16[4,80,5120]{2,1,0:T(8,128)(2,1)}, bf16[4,5120,80]{2,1,0:T(8,128)(2,1)}, s32[1,5120]{1,0:T(1,128)}) custom-call(bf16[4,80,1024]{2,1,0:T(8,128)(2,1)} %bitcast.69, bf16[4,1024,80]{2,1,0:T(8,128)(2,1)} %bitcast.66, s32[1,1024]{1,0:T(1,128)} %bitcast.75), custom_call_target="tpu_custom_call" | custom-call | tf_op jit(solution)/shard_map/pallas_call | solution.py:149
  84.6 1.2 copy-done.3
  85.8 1.0 copy-done.6
  86.9 1.9 copy-done.7
  88.8 29.1 %shard_map.119 = bf16[4,1024,80]{2,1,0:T(8,128)(2,1)S(1)} custom-call(s32[2,4]{1,0:T(2,128)S(1)} %pad_add_fusion.bounds, bf16[4,1024,80]{2,1,0:T(8,128)(2,1)S(1)} %bitcast.61, s32[1024,1]{1,0:T(8,128)S(1)} %copy-done.6, bf16[4,80,5120]{2,1,0:T(8,128)(2,1)S(1)} %copy-done.7, bf16[4,5120,80]{2,1,0:T(8,128)(2,1)} %get-tuple-element.10.v_ref, ...), custom_call_target="tpu_custom_call" | custom-call | flops 2684354560 | bytes 7864320 | tf_op jit(solution)/shard_map/pallas_call | solution.py:304
  117.9 1.0 copy-done.4
  118.9 2.2 copy.27
  121.1 2.2 copy.28.ctx_ref
  123.3 1.7 copy-done.2
  125.1 1.1 copy-done.5
  126.2 39.1 %shard_map.120 = f32[1024,1280]{1,0:T(8,128)} custom-call(bf16[1024,320]{1,0:T(8,128)(2,1)S(1)} %copy-done.5, bf16[1280,1280]{1,0:T(8,128)(2,1)} %all-gather.2.cloned.1.call-done.weight_ref, bf16[1024,1280]{1,0:T(8,128)(2,1)S(1)} %copy-done.2), custom_call_target="tpu_custom_call" | custom-call | flops 3355443200 | bytes 13762560 | tf_op jit(solution)/shard_map/pallas_call | solution.py:220
  165.3 2.8 reduce_sum.69
  168.1 3.1 multiply_reduce_fusion.1
  171.3 20.9 %convolution_convert_fusion = bf16[1024,1280]{1,0:T(8,128)(2,1)} fusion(bf16[1280,1280]{1,0:T(8,128)(2,1)S(1)} %copy-done, bf16[1280,1280]{1,0:T(8,128)(2,1)} %param.18, f32[1024,1280]{1,0:T(8,128)} %shard_map.120, f32[1280]{0:T(1024)S(1)} %convert_element_type.54, f32[1024]{0:T(1024)S(1)} %add_rsqrt_fusion.1, f32[1024]{0:T(1024)S(1)} %broadcast_multiply_fusion.1), kind=kOutput, calls=%fused_computation.34 | convolution fusion | flops 6802636800 | bytes 14431232 | tf_op jit(solution)/shard_map/dot_general | solution.py:372
  192.3 0.8 reduce-window.6
  193.4 80.9 %all-reduce.2.cloned.1.call-done = bf16[1024,1280]{1,0:T(8,128)(2,1)} async-done(((bf16[1024,1280]{1,0:T(8,128)(2,1)}), bf16[1024,1280]{1,0:T(8,128)(2,1)}) %all-reduce.2.cloned.1.call-update) | async-done | bytes 2621456 | tf_op jit(solution)/shard_map/psum | solution.py:373
  274.3 4.0 %fusion.32 = f32[1024]{0:T(1024)S(1)} fusion(f32[1024,1280]{1,0:T(8,128)} %shard_map.120, bf16[1024,1280]{1,0:T(8,128)(2,1)} %all-reduce.2.cloned.1.call-done), kind=kLoop, calls=%fused_computation.48 | loop fusion | flops 3931136 | bytes 7868416 | tf_op jit(solution)/shard_map/reduce_sum | solution.py:248
  278.4 3.7 %multiply_reduce_fusion = f32[1024]{0:T(1024)S(1)} fusion(f32[1024]{0:T(1024)S(1)} %broadcast_multiply_fusion, f32[1024,1280]{1,0:T(8,128)} %shard_map.120, bf16[1024,1280]{1,0:T(8,128)(2,1)S(1)} %copy-done.8), kind=kLoop, calls=%fused_computation.12 | loop fusion | flops 6552576 | bytes 7872512 | tf_op jit(solution)/shard_map/reduce_sum | solution.py:250
  282.2 5.1 %fusion.16 = bf16[256,4,1280]{2,0,1:T(8,128)(2,1)} fusion(f32[1280]{0:T(1024)S(1)} %convert_element_type.59, f32[1024]{0:T(1024)S(1)} %add_rsqrt_fusion, f32[1024]{0:T(1024)S(1)} %broadcast_multiply_fusion, s32[256,4]{0,1:T(4,128)S(1)} %broadcast_subtract_fusion, f32[1024,1280]{1,0:T(8,128)S(1)} %bitcast.65, bf16[1024,1280]{1,0:T(8,128)(2,1)S(1)} %copy-done.8), kind=kOutput, calls=%fused_computation.33 | convolution fusion | flops 2694578176 | bytes 10503168 | tf_op jit(solution)/shard_map/mkt,tc->mkc/dot_general | solution.py:378
  287.3 4.4 %copy.29 = bf16[256,4,1280]{0,2,1:T(8,128)(2,1)} copy(bf16[256,4,1280]{2,0,1:T(8,128)(2,1)} %fusion.16) | data formatting | bytes 5242880 | tf_op jit(solution)/shard_map/convert_element_type | solution.py:380
  291.7 4.8 %convolution_convert_fusion.1 = bf16[512,320]{0,1:T(8,128)(2,1)} fusion(bf16[5120,320]{0,1:T(8,128)(2,1)} %param.21, bf16[256,5120]{0,1:T(8,128)(2,1)} %bitcast.67, s32[256]{0:T(256)S(1)} %bitcast.79), kind=kOutput, calls=%fused_computation.50 | convolution fusion | flops 923123712 | bytes 6226944 | tf_op jit(solution)/shard_map/ms,mc->sc/dot_general | solution.py:391
  296.5 1.9 copy.30
  298.3 14.6 %shard_map.121 = bf16[32,16,320]{2,1,0:T(8,128)(2,1)} custom-call(bf16[32,16,320]{2,1,0:T(8,128)(2,1)} %bitcast.73), custom_call_target="tpu_custom_call" | custom-call | tf_op jit(solution)/shard_map/pallas_call | solution.py:203
  312.9 1.8 copy.35
  (58 shorter events, 2.5 us)
Async XLA Ops:
  6.5 164.7 %copy-start = (bf16[1280,1280]{1,0:T(8,128)(2,1)S(1)}, bf16[1280,1280]{1,0:T(8,128)(2,1)}, u32[]{:S(2)}) copy-start(bf16[1280,1280]{1,0:T(8,128)(2,1)} %param.19) | copy-start | bytes 9830404
  6.5 116.8 %all-gather.2.cloned.1.call-start = ((), (), s32[]{:S(2)}) async-start(), calls=%async_computation | async-start | bytes 4096000 | tf_op jit(solution)/shard_map/all_gather | solution.py:346
  7.3 267.1 %all-reduce.2.cloned.1.call-start = ((), (), s32[]{:S(2)}) async-start(), calls=%async_computation.1 | async-start | bytes 5242880 | tf_op jit(solution)/shard_map/psum | solution.py:373
  7.3 6.3 %copy-start.1 = (bf16[1024,1280]{1,0:T(8,128)(2,1)S(1)}, bf16[1024,1280]{1,0:T(8,128)(2,1)}, u32[]{:S(2)}) copy-start(bf16[1024,1280]{1,0:T(8,128)(2,1)} %tokens_ref.1) | copy-start | bytes 7864324
  7.3 6.3 %copy-start.15 = (bf16[1280,3,320]{0,2,1:T(8,128)(2,1)S(1)}, bf16[1280,3,320]{0,2,1:T(8,128)(2,1)}, u32[]{:S(2)}) copy-start(bf16[1280,3,320]{0,2,1:T(8,128)(2,1)} %param.15) | copy-start | bytes 7372804
  16.5 3.6 %copy-start.13 = (s32[1024]{0:T(1024)S(1)}, s32[1024]{0:T(1024)}, u32[]{:S(2)}) copy-start(s32[1024]{0:T(1024)} %param.13) | copy-start | bytes 12292
  20.1 3.3 %copy-start.9 = (s32[1024]{0:T(1024)}, s32[1024]{0:T(1024)S(1)}, u32[]{:S(2)}) copy-start(s32[1024]{0:T(1024)S(1)} %broadcast_add_fusion) | copy-start | bytes 12292
  84.6 1.2 copy-start.3
  85.8 1.0 copy-start.6
  86.9 1.9 copy-start.7
  88.8 34.5 %copy-start.11 = (bf16[1280]{0:T(1024)(128)(2,1)S(1)}, bf16[1280]{0:T(1024)(128)(2,1)}, u32[]{:S(2)}) copy-start(bf16[1280]{0:T(1024)(128)(2,1)} %param.17) | copy-start | bytes 7684
  117.9 1.0 copy-start.4
  123.3 1.7 copy-start.2
  125.1 1.1 copy-start.5
  171.2 21.0 %copy-start.12 = (bf16[1280]{0:T(1024)(128)(2,1)S(1)}, bf16[1280]{0:T(1024)(128)(2,1)}, u32[]{:S(2)}) copy-start(bf16[1280]{0:T(1024)(128)(2,1)} %param.20) | copy-start | bytes 7684
  171.3 21.0 %copy-start.10 = (s32[256,1]{0,1:T(1,128)S(1)}, s32[256,1]{0,1:T(1,128)}, u32[]{:S(2)}) copy-start(s32[256,1]{0,1:T(1,128)} %param.23) | copy-start | bytes 3076
  171.3 22.1 %copy-start.14 = (s32[256,4]{0,1:T(4,128)S(1)}, s32[256,4]{0,1:T(4,128)}, u32[]{:S(2)}) copy-start(s32[256,4]{0,1:T(4,128)} %param.22) | copy-start | bytes 12292
  274.3 4.0 %copy-start.8 = (bf16[1024,1280]{1,0:T(8,128)(2,1)S(1)}, bf16[1024,1280]{1,0:T(8,128)(2,1)}, u32[]{:S(2)}) copy-start(bf16[1024,1280]{1,0:T(8,128)(2,1)} %all-reduce.2.cloned.1.call-done) | copy-start | bytes 7864324
  274.3 7.8 %slice-start = ((s8[5242880]{0:T(1024)(128)(4,1)}), s8[4194304]{0:T(1024)(128)(4,1)S(1)}, s32[]{:S(2)}) async-start(s8[5242880]{0:T(1024)(128)(4,1)} %bitcast.64), calls=%async_computation.2 | async-start | bytes 8388608
  278.4 3.8 %slice-start.1 = ((s8[5242880]{0:T(1024)(128)(4,1)}), s8[1048576]{0:T(1024)(128)(4,1)S(1)}, s32[]{:S(2)}) async-start(s8[5242880]{0:T(1024)(128)(4,1)} %bitcast.64), calls=%async_computation.3 | async-start | bytes 2097152
Sparse Core Ops, SparseCore 0:
  9.0 43.8 all-gather.1
  192.3 81.9 all-reduce.1

commit v7 on v6

--- a/solution.py
+++ b/solution.py
@@ -267,11 +267,9 @@
         scores = lax.dot_general(
             q, keys, (((2,), (1,)), ((0,), (0,))), preferred_element_type=jnp.float32
         ) * factor
-        matches = (qm == km)[None]
-        new_max = jnp.maximum(
-            running_max, jnp.max(jnp.where(matches, scores, -1e30), axis=2, keepdims=True)
-        )
-        probs = jnp.where(matches, jnp.exp(scores - new_max), 0.0)
+        masked = jnp.where((qm == km)[None], scores, -1e30)
+        new_max = jnp.maximum(running_max, jnp.max(masked, axis=2, keepdims=True))
+        probs = jnp.exp(masked - new_max)
         shrink = jnp.exp(running_max - new_max)
         new_sum = running_sum * shrink + jnp.sum(probs, axis=2, keepdims=True)
         update = lax.dot_general(
@@ -377,8 +375,13 @@
     picks = (local_index[:, :, None] == jnp.arange(token_rows, dtype=jnp.int32)).astype(jnp.bfloat16)
     merged = jnp.einsum(
         "mkt,tc->mkc", picks, final_normed, preferred_element_type=jnp.float32
-    ).astype(jnp.bfloat16).reshape(merged_rows, 4 * final_normed.shape[1])
-    feature = jnp.dot(merged, merge_weight, preferred_element_type=jnp.float32).astype(jnp.bfloat16)
+    ).astype(jnp.bfloat16)
+    feature = jnp.einsum(
+        "mkc,kcd->md",
+        merged,
+        merge_weight.reshape(4, final_normed.shape[1], merge_weight.shape[1]),
+        preferred_element_type=jnp.float32,
+    ).astype(jnp.bfloat16)
     peers = lax.axis_size("req")
     capacity = 2 * merged_rows // peers
     target = owners[:, 0]

time: 322 us -> 312 us (0.969)
  waiting for transfers between devices: 81.6 us -> 68.7 us
  Pallas kernels: 143 us -> 149 us
  local copies, waits for them, and re-layouts: 27.6 us -> 23.2 us
    psum x1, waiting for transfers between devices: 80.9 us -> 68 us  [body(): lax.psum(hidden_terms.astype(jnp.bfloat16), 'tp').astype(jnp.float32)]
    convert_element_type x1 -> x0, local copies, waits for them, and re-layouts: 4.38 us -> none  [body(): merged = jnp.einsum('mkt,tc->mkc', picks, final_normed, preferred_element...]
    pallas_call x1, Pallas kernels: 29.1 us -> 32.5 us  [attention(): pl.pallas_call(flash_kernel, out_shape=jax.ShapeDtypeStruct(queries.shape...]
  transfers between devices with their start and end apart: 2 -> 2, of which waited for: 1 -> 1; matrix products, arithmetic and copies ran while one was open for 7% -> 7% of each run, Pallas kernels for 28% -> 30%
where the time goes in v7:
time: 312 us; the launch traced here: 311 us
  Pallas kernels  149 us (48%)
  waiting for transfers between devices  68.7 us (22%)
  matrix products  33.7 us (11%)
  local copies, waits for them, and re-layouts  23.2 us (7%)
  other arithmetic  22.2 us (7%)
  between operations  13.7 us (4%)
    psum x1, waiting for transfers between devices, body(): lax.psum(hidden_terms.astype(jnp.bfloat16), 'tp').astype(jnp.float32)  68 us
    pallas_call x1, Pallas kernels, exchange(): pl.pallas_call(functools.partial(exchange_kernel, order, n), out_shape=(j...  59.9 us
    pallas_call x1, Pallas kernels, project(): pl.pallas_call(functools.partial(project_kernel, order), out_shape=jax.Sh...  42.3 us
    pallas_call x1, Pallas kernels, attention(): pl.pallas_call(flash_kernel, out_shape=jax.ShapeDtypeStruct(queries.shape...  32.5 us
    dot_general x1, matrix products, body(): jnp.dot(expanded, reduce_weight, preferred_element_type=jnp.float32)  20.9 us
    pallas_call x1, Pallas kernels, deliver(): pl.pallas_call(functools.partial(deliver_kernel, order, n), out_shape=jax...  14.6 us
    unnamed x37, local copies, waits for them, and re-layouts  9.88 us
    reduce_sum x3, other arithmetic, layer_norm(): center = jnp.mean(stream, axis=-1, keepdims=True)  9.63 us
  transfers between devices with their start and end apart: 2, of which 1 were waited for; matrix products, arithmetic and copies ran while one was open for 7% of the time, Pallas kernels for 30%

profile of v7, /device:TPU:1, one launch (start us, length us, event | category | flops | bytes accessed | tf_op | source)
XLA Modules:
  0.0 310.9 jit_solution(13041716933660291690)
XLA Ops:
  7.3 0.9 convert_element_type.51
  8.2 2.8 convert_reduce_fusion
  11.0 2.6 fusion.2
  13.6 2.9 fusion.36
  16.5 1.3 fusion.85
  17.9 2.2 copy.25
  20.1 2.3 copy.26
  22.4 1.1 copy.27.qm_ref
  23.4 59.9 %shard_map.118 = (bf16[4,80,5120]{2,1,0:T(8,128)(2,1)}, bf16[4,5120,80]{2,1,0:T(8,128)(2,1)}, s32[1,5120]{1,0:T(1,128)}) custom-call(bf16[4,80,1024]{2,1,0:T(8,128)(2,1)} %bitcast.82, bf16[4,1024,80]{2,1,0:T(8,128)(2,1)} %bitcast.80, s32[1,1024]{1,0:T(1,128)} %bitcast.88), custom_call_target="tpu_custom_call" | custom-call | tf_op jit(solution)/shard_map/pallas_call | solution.py:149
  83.5 0.8 and_select_fusion.km_ref
  84.6 1.2 copy-done.3
  85.8 1.0 copy-done.6
  86.9 1.9 copy-done.7
  88.8 32.5 %shard_map.119 = bf16[4,1024,80]{2,1,0:T(8,128)(2,1)S(1)} custom-call(s32[2,4]{1,0:T(2,128)S(1)} %pad_add_fusion.bounds, bf16[4,1024,80]{2,1,0:T(8,128)(2,1)S(1)} %bitcast.75, s32[1024,1]{1,0:T(8,128)S(1)} %copy-done.6, bf16[4,80,5120]{2,1,0:T(8,128)(2,1)S(1)} %copy-done.7, bf16[4,5120,80]{2,1,0:T(8,128)(2,1)} %get-tuple-element.10.v_ref, ...), custom_call_target="tpu_custom_call" | custom-call | flops 2684354560 | bytes 7864320 | tf_op jit(solution)/shard_map/pallas_call | solution.py:302
  121.3 1.0 copy-done.4
  122.3 2.2 copy.28
  124.5 2.2 copy.29.ctx_ref
  126.7 1.7 copy-done.2
  128.5 1.1 copy-done.5
  129.6 42.3 %shard_map.120 = f32[1024,1280]{1,0:T(8,128)} custom-call(bf16[1024,320]{1,0:T(8,128)(2,1)S(1)} %copy-done.5, bf16[1280,1280]{1,0:T(8,128)(2,1)} %all-gather.2.cloned.1.call-done.weight_ref, bf16[1024,1280]{1,0:T(8,128)(2,1)S(1)} %copy-done.2), custom_call_target="tpu_custom_call" | custom-call | flops 3355443200 | bytes 13762560 | tf_op jit(solution)/shard_map/pallas_call | solution.py:220
  171.9 2.8 reduce_sum.69
  174.7 3.1 %multiply_reduce_fusion.1 = f32[1024]{0:T(1024)S(1)} fusion(f32[1024,1280]{1,0:T(8,128)} %shard_map.120, f32[1024]{0:T(1024)S(1)} %broadcast_multiply_fusion.1), kind=kLoop, calls=%fused_computation.28 | loop fusion | flops 3931136 | bytes 5251072 | tf_op jit(solution)/shard_map/reduce_sum | solution.py:250
  177.9 20.9 %convolution_convert_fusion = bf16[1024,1280]{1,0:T(8,128)(2,1)} fusion(bf16[1280,1280]{1,0:T(8,128)(2,1)S(1)} %copy-done, bf16[1280,1280]{1,0:T(8,128)(2,1)} %param.18, f32[1024,1280]{1,0:T(8,128)} %shard_map.120, f32[1280]{0:T(1024)S(1)} %convert_element_type.54, f32[1024]{0:T(1024)S(1)} %add_rsqrt_fusion.1, f32[1024]{0:T(1024)S(1)} %broadcast_multiply_fusion.1), kind=kOutput, calls=%fused_computation.34 | convolution fusion | flops 6802636800 | bytes 14431232 | tf_op jit(solution)/shard_map/dot_general | solution.py:370
  198.9 0.8 reduce-window.6
  200.1 68.0 %all-reduce.2.cloned.1.call-done = bf16[1024,1280]{1,0:T(8,128)(2,1)} async-done(((bf16[1024,1280]{1,0:T(8,128)(2,1)}), bf16[1024,1280]{1,0:T(8,128)(2,1)}) %all-reduce.2.cloned.1.call-update) | async-done | bytes 2621456 | tf_op jit(solution)/shard_map/psum | solution.py:371
  268.1 4.0 %fusion.35 = f32[1024]{0:T(1024)S(1)} fusion(f32[1024,1280]{1,0:T(8,128)} %shard_map.120, bf16[1024,1280]{1,0:T(8,128)(2,1)} %all-reduce.2.cloned.1.call-done), kind=kLoop, calls=%fused_computation.51 | loop fusion | flops 3931136 | bytes 7868416 | tf_op jit(solution)/shard_map/reduce_sum | solution.py:248
  272.1 3.7 %multiply_reduce_fusion = f32[1024]{0:T(1024)S(1)} fusion(f32[1024]{0:T(1024)S(1)} %broadcast_multiply_fusion, f32[1024,1280]{1,0:T(8,128)} %shard_map.120, bf16[1024,1280]{1,0:T(8,128)(2,1)S(1)} %copy-done.8), kind=kLoop, calls=%fused_computation.12 | loop fusion | flops 6552576 | bytes 7872512 | tf_op jit(solution)/shard_map/reduce_sum | solution.py:250
  275.9 5.1 %fusion.16 = bf16[256,4,1280]{2,0,1:T(8,128)(2,1)} fusion(f32[1280]{0:T(1024)S(1)} %convert_element_type.59, f32[1024]{0:T(1024)S(1)} %add_rsqrt_fusion, f32[1024]{0:T(1024)S(1)} %broadcast_multiply_fusion, s32[256,4]{0,1:T(4,128)S(1)} %broadcast_subtract_fusion, f32[1024,1280]{1,0:T(8,128)S(1)} %bitcast.79, bf16[1024,1280]{1,0:T(8,128)(2,1)S(1)} %copy-done.8), kind=kOutput, calls=%fused_computation.33 | convolution fusion | flops 2694578176 | bytes 10503168 | tf_op jit(solution)/shard_map/mkt,tc->mkc/dot_general | solution.py:376
  281.0 4.8 %convolution_convert_fusion.1 = bf16[512,320]{0,1:T(8,128)(2,1)} fusion(bf16[256,4,1280]{2,0,1:T(8,128)(2,1)} %fusion.16, bf16[40,4,8,1280]{3,2,1,0:T(8,128)(2,1)} %bitcast.93, s32[256]{0:T(256)S(1)} %bitcast.92), kind=kOutput, calls=%fused_computation.53 | convolution fusion | flops 923123712 | bytes 6226944 | tf_op jit(solution)/shard_map/ms,mc->sc/dot_general | solution.py:394
  285.8 1.9 copy.31
  287.7 14.6 %shard_map.121 = bf16[32,16,320]{2,1,0:T(8,128)(2,1)} custom-call(bf16[32,16,320]{2,1,0:T(8,128)(2,1)} %bitcast.86), custom_call_target="tpu_custom_call" | custom-call | tf_op jit(solution)/shard_map/pallas_call | solution.py:203
  302.3 1.8 copy.47
  (57 shorter events, 1.7 us)
Async XLA Ops:
  6.5 171.3 %copy-start = (bf16[1280,1280]{1,0:T(8,128)(2,1)S(1)}, bf16[1280,1280]{1,0:T(8,128)(2,1)}, u32[]{:S(2)}) copy-start(bf16[1280,1280]{1,0:T(8,128)(2,1)} %param.19) | copy-start | bytes 9830404
  6.5 120.2 %all-gather.2.cloned.1.call-start = ((), (), s32[]{:S(2)}) async-start(), calls=%async_computation | async-start | bytes 4096000 | tf_op jit(solution)/shard_map/all_gather | solution.py:344
  7.3 260.8 %all-reduce.2.cloned.1.call-start = ((), (), s32[]{:S(2)}) async-start(), calls=%async_computation.1 | async-start | bytes 5242880 | tf_op jit(solution)/shard_map/psum | solution.py:371
  7.3 6.3 %copy-start.1 = (bf16[1024,1280]{1,0:T(8,128)(2,1)S(1)}, bf16[1024,1280]{1,0:T(8,128)(2,1)}, u32[]{:S(2)}) copy-start(bf16[1024,1280]{1,0:T(8,128)(2,1)} %tokens_ref.1) | copy-start | bytes 7864324
  7.3 6.3 %copy-start.15 = (bf16[1280,3,320]{0,2,1:T(8,128)(2,1)S(1)}, bf16[1280,3,320]{0,2,1:T(8,128)(2,1)}, u32[]{:S(2)}) copy-start(bf16[1280,3,320]{0,2,1:T(8,128)(2,1)} %param.15) | copy-start | bytes 7372804
  16.5 3.6 %copy-start.13 = (s32[1024]{0:T(1024)S(1)}, s32[1024]{0:T(1024)}, u32[]{:S(2)}) copy-start(s32[1024]{0:T(1024)} %param.13) | copy-start | bytes 12292
  20.1 3.3 %copy-start.9 = (s32[1024]{0:T(1024)}, s32[1024]{0:T(1024)S(1)}, u32[]{:S(2)}) copy-start(s32[1024]{0:T(1024)S(1)} %broadcast_add_fusion) | copy-start | bytes 12292
  84.6 1.2 copy-start.3
  85.8 1.0 copy-start.6
  86.9 1.9 copy-start.7
  88.8 37.9 %copy-start.11 = (bf16[1280]{0:T(1024)(128)(2,1)S(1)}, bf16[1280]{0:T(1024)(128)(2,1)}, u32[]{:S(2)}) copy-start(bf16[1280]{0:T(1024)(128)(2,1)} %param.17) | copy-start | bytes 7684
  121.3 1.0 copy-start.4
  126.7 1.7 copy-start.2
  128.5 1.1 copy-start.5
  177.9 21.0 %copy-start.12 = (bf16[1280]{0:T(1024)(128)(2,1)S(1)}, bf16[1280]{0:T(1024)(128)(2,1)}, u32[]{:S(2)}) copy-start(bf16[1280]{0:T(1024)(128)(2,1)} %param.20) | copy-start | bytes 7684
  177.9 21.0 %copy-start.10 = (s32[256,1]{0,1:T(1,128)S(1)}, s32[256,1]{0,1:T(1,128)}, u32[]{:S(2)}) copy-start(s32[256,1]{0,1:T(1,128)} %param.23) | copy-start | bytes 3076
  177.9 22.2 %copy-start.14 = (s32[256,4]{0,1:T(4,128)S(1)}, s32[256,4]{0,1:T(4,128)}, u32[]{:S(2)}) copy-start(s32[256,4]{0,1:T(4,128)} %param.22) | copy-start | bytes 12292
  268.1 4.0 %copy-start.8 = (bf16[1024,1280]{1,0:T(8,128)(2,1)S(1)}, bf16[1024,1280]{1,0:T(8,128)(2,1)}, u32[]{:S(2)}) copy-start(bf16[1024,1280]{1,0:T(8,128)(2,1)} %all-reduce.2.cloned.1.call-done) | copy-start | bytes 7864324
  268.1 7.8 %slice-start = ((s8[5242880]{0:T(1024)(128)(4,1)}), s8[4194304]{0:T(1024)(128)(4,1)S(1)}, s32[]{:S(2)}) async-start(s8[5242880]{0:T(1024)(128)(4,1)} %bitcast.78), calls=%async_computation.2 | async-start | bytes 8388608
  272.1 3.8 %slice-start.1 = ((s8[5242880]{0:T(1024)(128)(4,1)}), s8[1048576]{0:T(1024)(128)(4,1)S(1)}, s32[]{:S(2)}) async-start(s8[5242880]{0:T(1024)(128)(4,1)} %bitcast.78), calls=%async_computation.3 | async-start | bytes 2097152
Sparse Core Ops, SparseCore 0:
  9.0 43.8 all-gather.1
  199.0 69.0 all-reduce.1

commit v8 on v7

--- a/solution.py
+++ b/solution.py
@@ -14,7 +14,8 @@
 MESH_IDS = pl.DeviceIdType.MESH
 
 
-def project_kernel(order, ctx_ref, weight_ref, tokens_ref, out_ref, slots, send_sem, recv_sem):
+def project_kernel(order, ctx_ref, weight_ref, tokens_ref, gain_ref, out_ref, norm_ref, slots, send_sem,
+                   recv_sem):
     n = slots.shape[0]
     rows, width = ctx_ref.shape
     cols = out_ref.shape[1]
@@ -79,7 +80,9 @@
     @pl.loop(0, rows // tile)
     def _(i):
         r = pl.ds(pl.multiple_of(i * tile, tile), tile)
-        out_ref[r, :] = out_ref[r, :] + tokens_ref[r, :].astype(jnp.float32)
+        middle = out_ref[r, :] + tokens_ref[r, :].astype(jnp.float32)
+        out_ref[r, :] = middle
+        norm_ref[r, :] = layer_norm(middle, gain_ref[...]).astype(norm_ref.dtype)
 
     for copy in (right, left, onward, backward):
         copy.wait_send()
@@ -214,14 +217,17 @@
     )(outgoing)
 
 
-def project(context, weight, tokens, order):
+def project(context, weight, tokens, gain, order):
     n = weight.shape[0] // context.shape[1]
     rows, cols = tokens.shape
     return pl.pallas_call(
         functools.partial(project_kernel, order),
-        out_shape=jax.ShapeDtypeStruct((rows, cols), jnp.float32),
-        in_specs=[pl.BlockSpec(memory_space=pltpu.VMEM)] * 3,
-        out_specs=pl.BlockSpec(memory_space=pltpu.VMEM),
+        out_shape=(
+            jax.ShapeDtypeStruct((rows, cols), jnp.float32),
+            jax.ShapeDtypeStruct((rows, cols), jnp.bfloat16),
+        ),
+        in_specs=[pl.BlockSpec(memory_space=pltpu.VMEM)] * 4,
+        out_specs=(pl.BlockSpec(memory_space=pltpu.VMEM), pl.BlockSpec(memory_space=pltpu.VMEM)),
         scratch_shapes=[
             pltpu.VMEM((n,) + context.shape, context.dtype),
             pltpu.SemaphoreType.DMA((n,)),
@@ -235,7 +241,7 @@
             bytes_accessed=4 * rows * cols + 2 * weight.size + 2 * rows * cols + 2 * n * context.size,
             transcendentals=0,
         ),
-    )(context, weight, tokens)
+    )(context, weight, tokens, gain.reshape(1, cols))
 
 
 def shifted_2(block, axis, distance):
@@ -362,8 +368,7 @@
     )
     context = attention(by_head(projected[:, :head_width]), marks, keys_all, values_all, key_marks)
     context = jnp.transpose(context, (1, 0, 2)).reshape(token_rows, head_width)
-    middle = project(context, full_weight, tokens, order)
-    mixer_in = layer_norm(middle, mixer_gain).astype(jnp.bfloat16)
+    middle, mixer_in = project(context, full_weight, tokens, mixer_gain, order)
     expanded = jax.nn.gelu(
         jnp.dot(mixer_in, expand_weight, preferred_element_type=jnp.float32), approximate=False
     ).astype(jnp.bfloat16)

time: 312 us -> 310 us (level)
  waiting for transfers between devices: 68.7 us -> 80.1 us
  Pallas kernels: 149 us -> 141 us
  other arithmetic: 22.2 us -> 16 us
    psum x1, waiting for transfers between devices: 68 us -> 79.4 us  [body(): lax.psum(hidden_terms.astype(jnp.bfloat16), 'tp').astype(jnp.float32)]
    pallas_call x1, Pallas kernels: 32.5 us -> 23.8 us  [attention(): pl.pallas_call(flash_kernel, out_shape=jax.ShapeDtypeStruct(queries.shape...]
    reduce_sum x3 -> x2, other arithmetic: 9.44 us -> 6.31 us  [layer_norm(): spread = jnp.mean(shifted * shifted, axis=-1, keepdims=True)]
    reduce_sum x3 -> x2, other arithmetic: 9.63 us -> 6.83 us  [layer_norm(): center = jnp.mean(stream, axis=-1, keepdims=True)]
    unnamed x37 -> x39, local copies, waits for them, and re-layouts: 9.88 us -> 11.4 us
  transfers between devices with their start and end apart: 2 -> 2, of which waited for: 1 -> 1; matrix products, arithmetic and copies ran while one was open for 7% -> 7% of each run, Pallas kernels for 30% -> 27%
where the time goes in v8:
time: 310 us; the launch traced here: 309 us
  Pallas kernels  141 us (45%)
  waiting for transfers between devices  80.1 us (26%)
  matrix products  32.8 us (11%)
  local copies, waits for them, and re-layouts  24.8 us (8%)
  other arithmetic  16 us (5%)
  between operations  13.7 us (4%)
    psum x1, waiting for transfers between devices, body(): lax.psum(hidden_terms.astype(jnp.bfloat16), 'tp').astype(jnp.float32)  79.4 us
    pallas_call x1, Pallas kernels, exchange(): pl.pallas_call(functools.partial(exchange_kernel, order, n), out_shape=(j...  59.9 us
    pallas_call x1, Pallas kernels, project(): pl.pallas_call(functools.partial(project_kernel, order), out_shape=(jax.S...  43.1 us
    pallas_call x1, Pallas kernels, attention(): pl.pallas_call(flash_kernel, out_shape=jax.ShapeDtypeStruct(queries.shape...  23.8 us
    dot_general x1, matrix products, body(): jnp.dot(expanded, reduce_weight, preferred_element_type=jnp.float32)  20.1 us
    pallas_call x1, Pallas kernels, deliver(): pl.pallas_call(functools.partial(deliver_kernel, order, n), out_shape=jax...  14.6 us
    unnamed x39, local copies, waits for them, and re-layouts  11.4 us
    reduce_sum x2, other arithmetic, layer_norm(): center = jnp.mean(stream, axis=-1, keepdims=True)  6.83 us
  transfers between devices with their start and end apart: 2, of which 1 were waited for; matrix products, arithmetic and copies ran while one was open for 7% of the time, Pallas kernels for 27%

profile of v8, /device:TPU:1, one launch (start us, length us, event | category | flops | bytes accessed | tf_op | source)
XLA Modules:
  0.0 309.0 jit_solution(6646585400219667852)
XLA Ops:
  6.5 0.7 all-gather.2.cloned.1.call-update
  7.3 0.9 convert_element_type.45
  8.2 2.8 convert_reduce_fusion
  11.0 2.6 fusion.2
  13.6 2.9 fusion.62
  16.5 1.3 fusion.111
  17.9 2.2 copy.25
  20.1 2.3 copy.26
  22.4 1.1 copy.27.qm_ref
  23.4 59.9 %shard_map.118 = (bf16[4,80,5120]{2,1,0:T(8,128)(2,1)}, bf16[4,5120,80]{2,1,0:T(8,128)(2,1)}, s32[1,5120]{1,0:T(1,128)}) custom-call(bf16[4,80,1024]{2,1,0:T(8,128)(2,1)} %bitcast.83, bf16[4,1024,80]{2,1,0:T(8,128)(2,1)} %bitcast.81, s32[1,1024]{1,0:T(1,128)} %bitcast.89), custom_call_target="tpu_custom_call" | custom-call | tf_op jit(solution)/shard_map/pallas_call | solution.py:152
  83.5 0.8 and_select_fusion.km_ref
  84.6 1.2 copy-done.3
  85.8 1.0 copy-done.6
  86.9 1.9 copy-done.7
  88.8 23.8 %shard_map.119 = bf16[4,1024,80]{2,1,0:T(8,128)(2,1)S(1)} custom-call(s32[2,4]{1,0:T(2,128)S(1)} %pad_add_fusion.bounds, bf16[4,1024,80]{2,1,0:T(8,128)(2,1)S(1)} %bitcast.76, s32[1024,1]{1,0:T(8,128)S(1)} %copy-done.6, bf16[4,80,5120]{2,1,0:T(8,128)(2,1)S(1)} %copy-done.7, bf16[4,5120,80]{2,1,0:T(8,128)(2,1)} %get-tuple-element.12.v_ref, ...), custom_call_target="tpu_custom_call" | custom-call | flops 2684354560 | bytes 7864320 | tf_op jit(solution)/shard_map/pallas_call | solution.py:308
  112.6 1.0 copy-done.4
  113.6 2.2 copy.28
  115.8 2.2 copy.29.ctx_ref
  118.1 1.7 copy-done.2
  119.8 1.1 copy-done.5
  121.0 43.1 %shard_map.120 = (f32[1024,1280]{1,0:T(8,128)}, bf16[1024,1280]{1,0:T(8,128)(2,1)S(1)}) custom-call(bf16[1024,320]{1,0:T(8,128)(2,1)S(1)} %copy-done.5, bf16[1280,1280]{1,0:T(8,128)(2,1)} %all-gather.2.cloned.1.call-done.weight_ref, bf16[1024,1280]{1,0:T(8,128)(2,1)S(1)} %copy-done.2, bf16[1,1280]{1,0:T(2,128)(2,1)S(1)} %reshape.245.gain_ref), custom_call_target="tpu_custom_call" | custom-call | flops 3355443200 | bytes 13762560 | tf_op jit(solution)/shard_map/pallas_call | solution.py:223
  164.1 1.6 copy-done.8
  165.7 20.1 %convolution_convert_fusion = bf16[1024,1280]{1,0:T(8,128)(2,1)} fusion(bf16[1280,1280]{1,0:T(8,128)(2,1)S(1)} %copy-done, bf16[1024,1280]{1,0:T(8,128)(2,1)} %copy-done.8, bf16[1280,1280]{1,0:T(8,128)(2,1)} %param.18), kind=kOutput, calls=%fused_computation.32 | convolution fusion | flops 6797393920 | bytes 11796480 | tf_op jit(solution)/shard_map/dot_general | solution.py:375
  185.8 0.6 reduce-window.6
  186.8 79.4 %all-reduce.2.cloned.1.call-done = bf16[1024,1280]{1,0:T(8,128)(2,1)} async-done(((bf16[1024,1280]{1,0:T(8,128)(2,1)}), bf16[1024,1280]{1,0:T(8,128)(2,1)}) %all-reduce.2.cloned.1.call-update) | async-done | bytes 2621456 | tf_op jit(solution)/shard_map/psum | solution.py:376
  266.2 4.0 %fusion.61 = f32[1024]{0:T(1024)S(1)} fusion(f32[1024,1280]{1,0:T(8,128)} %get-tuple-element.13, bf16[1024,1280]{1,0:T(8,128)(2,1)} %all-reduce.2.cloned.1.call-done), kind=kLoop, calls=%fused_computation.74 | loop fusion | flops 3931136 | bytes 7868416 | tf_op jit(solution)/shard_map/reduce_sum | solution.py:254
  270.2 3.7 %multiply_reduce_fusion = f32[1024]{0:T(1024)S(1)} fusion(f32[1024]{0:T(1024)S(1)} %broadcast_multiply_fusion, f32[1024,1280]{1,0:T(8,128)} %get-tuple-element.13, bf16[1024,1280]{1,0:T(8,128)(2,1)S(1)} %copy-done.9), kind=kLoop, calls=%fused_computation.12 | loop fusion | flops 6552576 | bytes 7872512 | tf_op jit(solution)/shard_map/reduce_sum | solution.py:256
  274.0 5.1 %fusion.16 = bf16[256,4,1280]{2,0,1:T(8,128)(2,1)} fusion(f32[1280]{0:T(1024)S(1)} %convert_element_type.51, f32[1024]{0:T(1024)S(1)} %add_rsqrt_fusion, f32[1024]{0:T(1024)S(1)} %broadcast_multiply_fusion, s32[256,4]{0,1:T(4,128)S(1)} %broadcast_subtract_fusion, f32[1024,1280]{1,0:T(8,128)S(1)} %bitcast.80, bf16[1024,1280]{1,0:T(8,128)(2,1)S(1)} %copy-done.9), kind=kOutput, calls=%fused_computation.31 | convolution fusion | flops 2694578176 | bytes 10503168 | tf_op jit(solution)/shard_map/mkt,tc->mkc/dot_general | solution.py:381
  279.1 4.8 %convolution_convert_fusion.1 = bf16[512,320]{0,1:T(8,128)(2,1)} fusion(bf16[256,4,1280]{2,0,1:T(8,128)(2,1)} %fusion.16, bf16[40,4,8,1280]{3,2,1,0:T(8,128)(2,1)} %bitcast.94, s32[256]{0:T(256)S(1)} %bitcast.93), kind=kOutput, calls=%fused_computation.76 | convolution fusion | flops 923123712 | bytes 6226944 | tf_op jit(solution)/shard_map/ms,mc->sc/dot_general | solution.py:399
  283.9 1.9 copy.31
  285.8 14.6 %shard_map.121 = bf16[32,16,320]{2,1,0:T(8,128)(2,1)} custom-call(bf16[32,16,320]{2,1,0:T(8,128)(2,1)} %bitcast.87), custom_call_target="tpu_custom_call" | custom-call | tf_op jit(solution)/shard_map/pallas_call | solution.py:206
  300.4 1.8 copy.47
  (55 shorter events, 1.0 us)
Async XLA Ops:
  6.5 159.1 %copy-start = (bf16[1280,1280]{1,0:T(8,128)(2,1)S(1)}, bf16[1280,1280]{1,0:T(8,128)(2,1)}, u32[]{:S(2)}) copy-start(bf16[1280,1280]{1,0:T(8,128)(2,1)} %param.19) | copy-start | bytes 9830404
  6.5 111.5 %all-gather.2.cloned.1.call-start = ((), (), s32[]{:S(2)}) async-start(), calls=%async_computation | async-start | bytes 4096000 | tf_op jit(solution)/shard_map/all_gather | solution.py:350
  7.3 258.9 %all-reduce.2.cloned.1.call-start = ((), (), s32[]{:S(2)}) async-start(), calls=%async_computation.1 | async-start | bytes 5242880 | tf_op jit(solution)/shard_map/psum | solution.py:376
  7.3 6.3 %copy-start.1 = (bf16[1024,1280]{1,0:T(8,128)(2,1)S(1)}, bf16[1024,1280]{1,0:T(8,128)(2,1)}, u32[]{:S(2)}) copy-start(bf16[1024,1280]{1,0:T(8,128)(2,1)} %tokens_ref.1) | copy-start | bytes 7864324
  7.3 6.3 %copy-start.16 = (bf16[1280,3,320]{0,2,1:T(8,128)(2,1)S(1)}, bf16[1280,3,320]{0,2,1:T(8,128)(2,1)}, u32[]{:S(2)}) copy-start(bf16[1280,3,320]{0,2,1:T(8,128)(2,1)} %param.15) | copy-start | bytes 7372804
  16.5 3.6 %copy-start.13 = (s32[1024]{0:T(1024)S(1)}, s32[1024]{0:T(1024)}, u32[]{:S(2)}) copy-start(s32[1024]{0:T(1024)} %param.13) | copy-start | bytes 12292
  20.1 3.3 %copy-start.10 = (s32[1024]{0:T(1024)}, s32[1024]{0:T(1024)S(1)}, u32[]{:S(2)}) copy-start(s32[1024]{0:T(1024)S(1)} %broadcast_add_fusion) | copy-start | bytes 12292
  84.6 1.2 copy-start.3
  85.8 1.0 copy-start.6
  86.9 1.9 copy-start.7
  88.8 29.2 %copy-start.14 = (bf16[1280]{0:T(1024)(128)(2,1)S(1)}, bf16[1280]{0:T(1024)(128)(2,1)}, u32[]{:S(2)}) copy-start(bf16[1280]{0:T(1024)(128)(2,1)} %param.17) | copy-start | bytes 7684
  112.6 1.0 copy-start.4
  118.1 1.7 copy-start.2
  119.8 1.1 copy-start.5
  164.1 1.6 copy-start.8
  165.7 20.1 %copy-start.12 = (bf16[1280]{0:T(1024)(128)(2,1)S(1)}, bf16[1280]{0:T(1024)(128)(2,1)}, u32[]{:S(2)}) copy-start(bf16[1280]{0:T(1024)(128)(2,1)} %param.20) | copy-start | bytes 7684
  165.7 20.1 %copy-start.11 = (s32[256,1]{0,1:T(1,128)S(1)}, s32[256,1]{0,1:T(1,128)}, u32[]{:S(2)}) copy-start(s32[256,1]{0,1:T(1,128)} %param.23) | copy-start | bytes 3076
  165.7 21.1 %copy-start.15 = (s32[256,4]{0,1:T(4,128)S(1)}, s32[256,4]{0,1:T(4,128)}, u32[]{:S(2)}) copy-start(s32[256,4]{0,1:T(4,128)} %param.22) | copy-start | bytes 12292
  266.2 4.0 %copy-start.9 = (bf16[1024,1280]{1,0:T(8,128)(2,1)S(1)}, bf16[1024,1280]{1,0:T(8,128)(2,1)}, u32[]{:S(2)}) copy-start(bf16[1024,1280]{1,0:T(8,128)(2,1)} %all-reduce.2.cloned.1.call-done) | copy-start | bytes 7864324
  266.2 7.8 %slice-start = ((s8[5242880]{0:T(1024)(128)(4,1)}), s8[4194304]{0:T(1024)(128)(4,1)S(1)}, s32[]{:S(2)}) async-start(s8[5242880]{0:T(1024)(128)(4,1)} %bitcast.79), calls=%async_computation.2 | async-start | bytes 8388608
  270.2 3.8 %slice-start.1 = ((s8[5242880]{0:T(1024)(128)(4,1)}), s8[1048576]{0:T(1024)(128)(4,1)S(1)}, s32[]{:S(2)}) async-start(s8[5242880]{0:T(1024)(128)(4,1)} %bitcast.79), calls=%async_computation.3 | async-start | bytes 2097152
Sparse Core Ops, SparseCore 0:
  9.0 43.8 all-gather.1
  185.9 80.2 all-reduce.1

commit v9 on v8

--- a/solution.py
+++ b/solution.py
@@ -215,6 +215,26 @@
         ],
         compiler_params=pltpu.CompilerParams(collective_id=2, has_side_effects=True),
     )(outgoing)
+
+
+def norm_kernel(*refs):
+    *inputs, gain_ref, out_ref = refs
+    stream = inputs[0][...].astype(jnp.float32)
+    for extra in inputs[1:]:
+        stream = stream + extra[...].astype(jnp.float32)
+    out_ref[...] = layer_norm(stream, gain_ref[...]).astype(out_ref.dtype)
+
+
+def norm_rows(inputs, gain):
+    rows, cols = inputs[0].shape
+    block = pl.BlockSpec((TILE, cols), lambda i: (i, 0))
+    return pl.pallas_call(
+        norm_kernel,
+        out_shape=jax.ShapeDtypeStruct((rows, cols), jnp.bfloat16),
+        grid=(rows // TILE,),
+        in_specs=[block] * len(inputs) + [pl.BlockSpec((1, cols), lambda i: (0, 0))],
+        out_specs=block,
+    )(*inputs, gain.reshape(1, cols))
 
 
 def project(context, weight, tokens, gain, order):
@@ -348,8 +368,7 @@
     head_width = attend_weight.shape[2]
     head_count = head_width // HD
     full_weight = lax.all_gather(output_weight, "tp", axis=0, tiled=True)
-    stream = tokens.astype(jnp.float32)
-    attend_in = layer_norm(stream, attend_gain).astype(jnp.bfloat16)
+    attend_in = norm_rows([tokens], attend_gain)
     projected = jnp.dot(
         attend_in,
         attend_weight.reshape(attend_weight.shape[0], 3 * head_width),
@@ -373,8 +392,7 @@
         jnp.dot(mixer_in, expand_weight, preferred_element_type=jnp.float32), approximate=False
     ).astype(jnp.bfloat16)
     hidden_terms = jnp.dot(expanded, reduce_weight, preferred_element_type=jnp.float32)
-    final_stream = middle + lax.psum(hidden_terms.astype(jnp.bfloat16), "tp").astype(jnp.float32)
-    final_normed = layer_norm(final_stream, output_gain).astype(jnp.bfloat16)
+    final_normed = norm_rows([middle, lax.psum(hidden_terms.astype(jnp.bfloat16), "tp")], output_gain)
     merged_rows = merge_index.shape[0]
     local_index = merge_index - lax.axis_index("req") * token_rows
     picks = (local_index[:, :, None] == jnp.arange(token_rows, dtype=jnp.int32)).astype(jnp.bfloat16)

time: 310 us -> 311 us (level)
  Pallas kernels: 141 us -> 165 us
  other arithmetic: 16 us -> 1.98 us
  waiting for transfers between devices: 80.1 us -> 66.8 us
  matrix products: 32.8 us -> 36.3 us
    pallas_call x1, Pallas kernels: 23.8 us -> 39.4 us  [attention(): pl.pallas_call(flash_kernel, out_shape=jax.ShapeDtypeStruct(queries.shape...]
    psum x1, waiting for transfers between devices: 79.4 us -> 66 us  [body(): lax.psum(hidden_terms.astype(jnp.bfloat16), 'tp')]
    reduce_sum x4 -> x0, other arithmetic: 13.1 us -> none  [the longest x2 6.83 us: layer_norm(): center = jnp.mean(stream, axis=-1, keepdims=True)]
    pallas_call x0 -> x2, Pallas kernels: none -> 10.6 us  [norm_rows(): pl.pallas_call(norm_kernel, out_shape=jax.ShapeDtypeStruct((rows, cols),...]
    unnamed x39 -> x29, local copies, waits for them, and re-layouts: 11.4 us -> 11.3 us
  transfers between devices with their start and end apart: 2 -> 2, of which waited for: 1 -> 1; matrix products, arithmetic and copies ran while one was open for 7% -> 7% of each run, Pallas kernels for 27% -> 34%
where the time goes in v9:
time: 311 us; the launch traced here: 310 us
  Pallas kernels  165 us (53%)
  waiting for transfers between devices  66.8 us (21%)
  matrix products  36.3 us (12%)
  local copies, waits for them, and re-layouts  26.8 us (9%)
  between operations  13.6 us (4%)
    psum x1, waiting for transfers between devices, body(): lax.psum(hidden_terms.astype(jnp.bfloat16), 'tp')  66 us
    pallas_call x1, Pallas kernels, exchange(): pl.pallas_call(functools.partial(exchange_kernel, order, n), out_shape=(j...  59.9 us
    pallas_call x1, Pallas kernels, project(): pl.pallas_call(functools.partial(project_kernel, order), out_shape=(jax.S...  40.3 us
    pallas_call x1, Pallas kernels, attention(): pl.pallas_call(flash_kernel, out_shape=jax.ShapeDtypeStruct(queries.shape...  39.4 us
    dot_general x1, matrix products, body(): jnp.dot(expanded, reduce_weight, preferred_element_type=jnp.float32)  20.2 us
    pallas_call x1, Pallas kernels, deliver(): pl.pallas_call(functools.partial(deliver_kernel, order, n), out_shape=jax...  14.6 us
    unnamed x29, local copies, waits for them, and re-layouts  11.3 us
    pallas_call x2, Pallas kernels, norm_rows(): pl.pallas_call(norm_kernel, out_shape=jax.ShapeDtypeStruct((rows, cols),...  10.6 us
  transfers between devices with their start and end apart: 2, of which 1 were waited for; matrix products, arithmetic and copies ran while one was open for 7% of the time, Pallas kernels for 34%

profile of v9, /device:TPU:1, one launch (start us, length us, event | category | flops | bytes accessed | tf_op | source)
XLA Modules:
  0.0 310.2 jit_solution(12066689150055702944)
XLA Ops:
  6.5 0.7 all-gather.2.cloned.1.call-update
  7.3 1.5 reshape.217.refs_1_
  8.8 4.8 %shard_map.118 = bf16[1024,1280]{1,0:T(8,128)(2,1)} custom-call(bf16[1024,1280]{1,0:T(8,128)(2,1)} %tokens_ref.1, bf16[1,1280]{1,0:T(2,128)(2,1)} %reshape.217.refs_1_), custom_call_target="tpu_custom_call" | custom-call | tf_op jit(solution)/shard_map/pallas_call | solution.py:231
  13.6 5.2 %convolution_convert_fusion.1 = bf16[1024,960]{0,1:T(8,128)(2,1)S(1)} fusion(bf16[1024,1280]{1,0:T(8,128)(2,1)} %shard_map.118, bf16[1280,960]{0,1:T(8,128)(2,1)} %bitcast.94), kind=kOutput, calls=%fused_computation.57 | convolution fusion | flops 2517565440 | bytes 7045120 | tf_op jit(solution)/shard_map/dot_general | solution.py:372
  18.8 1.3 fusion.93
  20.1 2.2 copy.25
  22.4 2.3 copy.26
  24.6 1.1 copy.27.qm_ref
  25.7 59.9 %shard_map.119 = (bf16[4,80,5120]{2,1,0:T(8,128)(2,1)}, bf16[4,5120,80]{2,1,0:T(8,128)(2,1)}, s32[1,5120]{1,0:T(1,128)}) custom-call(bf16[4,80,1024]{2,1,0:T(8,128)(2,1)} %bitcast.82, bf16[4,1024,80]{2,1,0:T(8,128)(2,1)} %bitcast.80, s32[1,1024]{1,0:T(1,128)} %bitcast.88), custom_call_target="tpu_custom_call" | custom-call | tf_op jit(solution)/shard_map/pallas_call | solution.py:152
  85.8 0.8 and_select_fusion.km_ref
  86.6 0.3 select_reduce_fusion.1
  86.9 1.2 copy-done.2
  88.1 1.0 copy-done.5
  89.1 1.9 copy-done.6
  91.1 39.4 %shard_map.120 = bf16[4,1024,80]{2,1,0:T(8,128)(2,1)S(1)} custom-call(s32[2,4]{1,0:T(2,128)S(1)} %pad_add_fusion.bounds, bf16[4,1024,80]{2,1,0:T(8,128)(2,1)S(1)} %bitcast.77, s32[1024,1]{1,0:T(8,128)S(1)} %copy-done.5, bf16[4,80,5120]{2,1,0:T(8,128)(2,1)S(1)} %copy-done.6, bf16[4,5120,80]{2,1,0:T(8,128)(2,1)} %get-tuple-element.12.v_ref, ...), custom_call_target="tpu_custom_call" | custom-call | flops 2684354560 | bytes 7864320 | tf_op jit(solution)/shard_map/pallas_call | solution.py:328
  130.5 1.0 copy-done.3
  131.5 2.2 copy.28
  133.7 2.2 copy.29.ctx_ref
  136.0 1.7 copy-done.1
  137.7 1.1 copy-done.4
  138.8 40.3 %shard_map.121 = (f32[1024,1280]{1,0:T(8,128)}, bf16[1024,1280]{1,0:T(8,128)(2,1)S(1)}) custom-call(bf16[1024,320]{1,0:T(8,128)(2,1)S(1)} %copy-done.4, bf16[1280,1280]{1,0:T(8,128)(2,1)} %all-gather.2.cloned.1.call-done.weight_ref, bf16[1024,1280]{1,0:T(8,128)(2,1)S(1)} %copy-done.1, bf16[1,1280]{1,0:T(2,128)(2,1)S(1)} %reshape.226.gain_ref), custom_call_target="tpu_custom_call" | custom-call | flops 3355443200 | bytes 13762560 | tf_op jit(solution)/shard_map/pallas_call | solution.py:243
  179.1 1.5 copy-done.7
  180.6 20.2 %convolution_convert_fusion = bf16[1024,1280]{1,0:T(8,128)(2,1)} fusion(bf16[1280,1280]{1,0:T(8,128)(2,1)S(1)} %copy-done, bf16[1024,1280]{1,0:T(8,128)(2,1)} %copy-done.7, bf16[1280,1280]{1,0:T(8,128)(2,1)} %param.18), kind=kOutput, calls=%fused_computation.22 | convolution fusion | flops 6797393920 | bytes 11796480 | tf_op jit(solution)/shard_map/dot_general | solution.py:394
  200.9 0.6 reshape.227.refs_2_
  201.5 0.6 reduce-window.6
  202.5 66.0 %all-reduce.2.cloned.1.call-done.refs_1_ = bf16[1024,1280]{1,0:T(8,128)(2,1)} async-done(((bf16[1024,1280]{1,0:T(8,128)(2,1)}), bf16[1024,1280]{1,0:T(8,128)(2,1)}) %all-reduce.2.cloned.1.call-update) | async-done | bytes 2621456 | tf_op jit(solution)/shard_map/psum | solution.py:395
  268.5 5.8 %shard_map.122 = bf16[1024,1280]{1,0:T(8,128)(2,1)} custom-call(f32[1024,1280]{1,0:T(8,128)} %get-tuple-element.13.refs_0_, bf16[1024,1280]{1,0:T(8,128)(2,1)} %all-reduce.2.cloned.1.call-done.refs_1_, bf16[1,1280]{1,0:T(2,128)(2,1)} %reshape.227.refs_2_), custom_call_target="tpu_custom_call" | custom-call | tf_op jit(solution)/shard_map/pallas_call | solution.py:231
  274.3 6.1 %fusion.11 = bf16[256,4,1280]{2,0,1:T(8,128)(2,1)} fusion(bf16[1024,1280]{1,0:T(8,128)(2,1)} %shard_map.122, s32[256,4]{0,1:T(4,128)S(1)} %broadcast_subtract_fusion), kind=kOutput, calls=%fused_computation.21 | convolution fusion | flops 2686713856 | bytes 5246976 | tf_op jit(solution)/shard_map/mkt,tc->mkc/dot_general | solution.py:399
  280.4 4.8 %convolution_convert_fusion.2 = bf16[512,320]{0,1:T(8,128)(2,1)} fusion(bf16[256,4,1280]{2,0,1:T(8,128)(2,1)} %fusion.11, bf16[40,4,8,1280]{3,2,1,0:T(8,128)(2,1)} %bitcast.93, s32[256]{0:T(256)S(1)} %bitcast.92), kind=kOutput, calls=%fused_computation.58 | convolution fusion | flops 923123712 | bytes 6226944 | tf_op jit(solution)/shard_map/ms,mc->sc/dot_general | solution.py:417
  285.1 1.9 copy.31
  287.0 14.6 %shard_map.123 = bf16[32,16,320]{2,1,0:T(8,128)(2,1)} custom-call(bf16[32,16,320]{2,1,0:T(8,128)(2,1)} %bitcast.86), custom_call_target="tpu_custom_call" | custom-call | tf_op jit(solution)/shard_map/pallas_call | solution.py:206
  301.6 1.8 copy.47
  (38 shorter events, 0.7 us)
Async XLA Ops:
  6.5 174.1 %copy-start = (bf16[1280,1280]{1,0:T(8,128)(2,1)S(1)}, bf16[1280,1280]{1,0:T(8,128)(2,1)}, u32[]{:S(2)}) copy-start(bf16[1280,1280]{1,0:T(8,128)(2,1)} %param.19) | copy-start | bytes 9830404
  6.5 129.4 %all-gather.2.cloned.1.call-start = ((), (), s32[]{:S(2)}) async-start(), calls=%async_computation | async-start | bytes 4096000 | tf_op jit(solution)/shard_map/all_gather | solution.py:370
  7.3 261.2 %all-reduce.2.cloned.1.call-start = ((), (), s32[]{:S(2)}) async-start(), calls=%async_computation.1 | async-start | bytes 5242880 | tf_op jit(solution)/shard_map/psum | solution.py:395
  18.8 3.6 %copy-start.10 = (s32[1024]{0:T(1024)S(1)}, s32[1024]{0:T(1024)}, u32[]{:S(2)}) copy-start(s32[1024]{0:T(1024)} %param.13) | copy-start | bytes 12292
  22.4 3.3 %copy-start.8 = (s32[1024]{0:T(1024)}, s32[1024]{0:T(1024)S(1)}, u32[]{:S(2)}) copy-start(s32[1024]{0:T(1024)S(1)} %broadcast_add_fusion) | copy-start | bytes 12292
  86.9 1.2 copy-start.2
  88.1 1.0 copy-start.5
  89.1 1.9 copy-start.6
  91.1 44.8 %copy-start.11 = (bf16[1280]{0:T(1024)(128)(2,1)S(1)}, bf16[1280]{0:T(1024)(128)(2,1)}, u32[]{:S(2)}) copy-start(bf16[1280]{0:T(1024)(128)(2,1)} %param.17) | copy-start | bytes 7684
  130.5 1.0 copy-start.3
  135.9 1.7 copy-start.1
  137.7 1.1 copy-start.4
  179.1 1.5 copy-start.7
  180.6 20.3 %copy-start.12 = (bf16[1280]{0:T(1024)(128)(2,1)S(1)}, bf16[1280]{0:T(1024)(128)(2,1)}, u32[]{:S(2)}) copy-start(bf16[1280]{0:T(1024)(128)(2,1)} %param.20) | copy-start | bytes 7684
  180.6 20.9 %copy-start.9 = (s32[256,1]{0,1:T(1,128)S(1)}, s32[256,1]{0,1:T(1,128)}, u32[]{:S(2)}) copy-start(s32[256,1]{0,1:T(1,128)} %param.23) | copy-start | bytes 3076
  180.6 21.8 %copy-start.13 = (s32[256,4]{0,1:T(4,128)S(1)}, s32[256,4]{0,1:T(4,128)}, u32[]{:S(2)}) copy-start(s32[256,4]{0,1:T(4,128)} %param.22) | copy-start | bytes 12292
Sparse Core Ops, SparseCore 0:
  9.0 43.8 all-gather.1
  201.0 67.4 all-reduce.1

commit v10 on v8

--- a/solution.py
+++ b/solution.py
@@ -10,6 +10,7 @@
 
 HD = 80
 TILE = 256
+QTILE = 128
 NEAR = (1, -1, 2, -2)
 MESH_IDS = pl.DeviceIdType.MESH
 
@@ -297,9 +298,9 @@
 def attention(queries, query_marks, keys, values, key_marks):
     heads, rows, width = queries.shape
     key_rows = keys.shape[2]
-    tiles = rows // TILE
-    low = query_marks.reshape(tiles, TILE).min(axis=1)
-    high = query_marks.reshape(tiles, TILE).max(axis=1)
+    tiles = rows // QTILE
+    low = query_marks.reshape(tiles, QTILE).min(axis=1)
+    high = query_marks.reshape(tiles, QTILE).max(axis=1)
     valid = (key_marks[None, :] >= low[:, None]) & (key_marks[None, :] <= high[:, None])
     place = jnp.arange(key_rows, dtype=jnp.int32)[None, :]
     first = jnp.min(jnp.where(valid, place, key_rows), axis=1)
@@ -312,13 +313,13 @@
             num_scalar_prefetch=1,
             grid=(tiles,),
             in_specs=[
-                pl.BlockSpec((heads, TILE, width), lambda i, b: (0, i, 0)),
-                pl.BlockSpec((TILE, 1), lambda i, b: (i, 0)),
+                pl.BlockSpec((heads, QTILE, width), lambda i, b: (0, i, 0)),
+                pl.BlockSpec((QTILE, 1), lambda i, b: (i, 0)),
                 pl.BlockSpec((heads, width, key_rows), lambda i, b: (0, 0, 0)),
                 pl.BlockSpec((heads, key_rows, width), lambda i, b: (0, 0, 0)),
                 pl.BlockSpec((1, key_rows), lambda i, b: (0, 0)),
             ],
-            out_specs=pl.BlockSpec((heads, TILE, width), lambda i, b: (0, i, 0)),
+            out_specs=pl.BlockSpec((heads, QTILE, width), lambda i, b: (0, i, 0)),
         ),
         compiler_params=pltpu.CompilerParams(vmem_limit_bytes=48 * 1024 * 1024),
         cost_estimate=pl.CostEstimate(

time: 310 us -> 312 us (level)
    pallas_call x1, Pallas kernels: 23.8 us -> 31.1 us  [attention(): pl.pallas_call(flash_kernel, out_shape=jax.ShapeDtypeStruct(queries.shape...]
    pallas_call x1, Pallas kernels: 43.1 us -> 37.6 us  [project(): pl.pallas_call(functools.partial(project_kernel, order), out_shape=(jax.S...]
  transfers between devices with their start and end apart: 2 -> 2, of which waited for: 1 -> 1; matrix products, arithmetic and copies ran while one was open for 7% -> 7% of each run, Pallas kernels for 27% -> 29%
where the time goes in v10:
time: 312 us; the launch traced here: 311 us
  Pallas kernels  143 us (46%)
  waiting for transfers between devices  80.3 us (26%)
  matrix products  32.8 us (11%)
  local copies, waits for them, and re-layouts  24.8 us (8%)
  other arithmetic  16.2 us (5%)
  between operations  13.7 us (4%)
    psum x1, waiting for transfers between devices, body(): lax.psum(hidden_terms.astype(jnp.bfloat16), 'tp').astype(jnp.float32)  79.5 us
    pallas_call x1, Pallas kernels, exchange(): pl.pallas_call(functools.partial(exchange_kernel, order, n), out_shape=(j...  59.9 us
    pallas_call x1, Pallas kernels, project(): pl.pallas_call(functools.partial(project_kernel, order), out_shape=(jax.S...  37.6 us
    pallas_call x1, Pallas kernels, attention(): pl.pallas_call(flash_kernel, out_shape=jax.ShapeDtypeStruct(queries.shape...  31.1 us
    dot_general x1, matrix products, body(): jnp.dot(expanded, reduce_weight, preferred_element_type=jnp.float32)  20.1 us
    pallas_call x1, Pallas kernels, deliver(): pl.pallas_call(functools.partial(deliver_kernel, order, n), out_shape=jax...  14.6 us
    unnamed x39, local copies, waits for them, and re-layouts  11.4 us
    reduce_sum x2, other arithmetic, layer_norm(): center = jnp.mean(stream, axis=-1, keepdims=True)  6.83 us
  transfers between devices with their start and end apart: 2, of which 1 were waited for; matrix products, arithmetic and copies ran while one was open for 7% of the time, Pallas kernels for 29%

profile of v10, /device:TPU:1, one launch (start us, length us, event | category | flops | bytes accessed | tf_op | source)
XLA Modules:
  0.0 311.0 jit_solution(8439299946338818599)
XLA Ops:
  6.5 0.7 all-gather.2.cloned.1.call-update
  7.3 0.9 convert_element_type.45
  8.2 2.8 convert_reduce_fusion
  11.0 2.6 fusion.2
  13.6 2.9 fusion.62
  16.5 1.3 fusion.110
  17.9 2.2 copy.25
  20.1 2.3 copy.26
  22.3 1.1 copy.27.qm_ref
  23.4 59.9 %shard_map.118 = (bf16[4,80,5120]{2,1,0:T(8,128)(2,1)}, bf16[4,5120,80]{2,1,0:T(8,128)(2,1)}, s32[1,5120]{1,0:T(1,128)}) custom-call(bf16[4,80,1024]{2,1,0:T(8,128)(2,1)} %bitcast.86, bf16[4,1024,80]{2,1,0:T(8,128)(2,1)} %bitcast.84, s32[1,1024]{1,0:T(1,128)} %bitcast.92), custom_call_target="tpu_custom_call" | custom-call | tf_op jit(solution)/shard_map/pallas_call | solution.py:153
  83.5 0.8 and_select_fusion.km_ref
  84.6 1.2 copy-done.3
  85.8 1.0 copy-done.6
  86.9 1.9 copy-done.7
  88.8 31.1 %shard_map.119 = bf16[4,1024,80]{2,1,0:T(8,128)(2,1)S(1)} custom-call(s32[2,8]{1,0:T(2,128)S(1)} %pad_add_fusion.bounds, bf16[4,1024,80]{2,1,0:T(8,128)(2,1)S(1)} %bitcast.79, s32[1024,1]{1,0:T(8,128)S(1)} %copy-done.6, bf16[4,80,5120]{2,1,0:T(8,128)(2,1)S(1)} %copy-done.7, bf16[4,5120,80]{2,1,0:T(8,128)(2,1)} %get-tuple-element.12.v_ref, ...), custom_call_target="tpu_custom_call" | custom-call | flops 2684354560 | bytes 7864320 | tf_op jit(solution)/shard_map/pallas_call | solution.py:309
  119.9 1.0 copy-done.4
  120.8 2.2 copy.28
  123.0 2.2 copy.29.ctx_ref
  125.3 1.7 copy-done.2
  127.0 1.1 copy-done.5
  128.2 37.6 %shard_map.120 = (f32[1024,1280]{1,0:T(8,128)}, bf16[1024,1280]{1,0:T(8,128)(2,1)S(1)}) custom-call(bf16[1024,320]{1,0:T(8,128)(2,1)S(1)} %copy-done.5, bf16[1280,1280]{1,0:T(8,128)(2,1)} %all-gather.2.cloned.1.call-done.weight_ref, bf16[1024,1280]{1,0:T(8,128)(2,1)S(1)} %copy-done.2, bf16[1,1280]{1,0:T(2,128)(2,1)S(1)} %reshape.245.gain_ref), custom_call_target="tpu_custom_call" | custom-call | flops 3355443200 | bytes 13762560 | tf_op jit(solution)/shard_map/pallas_call | solution.py:224
  165.8 1.6 copy-done.8
  167.3 20.1 %convolution_convert_fusion = bf16[1024,1280]{1,0:T(8,128)(2,1)} fusion(bf16[1280,1280]{1,0:T(8,128)(2,1)S(1)} %copy-done, bf16[1024,1280]{1,0:T(8,128)(2,1)} %copy-done.8, bf16[1280,1280]{1,0:T(8,128)(2,1)} %param.18), kind=kOutput, calls=%fused_computation.32 | convolution fusion | flops 6797393920 | bytes 11796480 | tf_op jit(solution)/shard_map/dot_general | solution.py:376
  187.5 0.8 reduce-window.6
  188.6 79.5 %all-reduce.2.cloned.1.call-done = bf16[1024,1280]{1,0:T(8,128)(2,1)} async-done(((bf16[1024,1280]{1,0:T(8,128)(2,1)}), bf16[1024,1280]{1,0:T(8,128)(2,1)}) %all-reduce.2.cloned.1.call-update) | async-done | bytes 2621456 | tf_op jit(solution)/shard_map/psum | solution.py:377
  268.2 4.0 %fusion.61 = f32[1024]{0:T(1024)S(1)} fusion(f32[1024,1280]{1,0:T(8,128)} %get-tuple-element.13, bf16[1024,1280]{1,0:T(8,128)(2,1)} %all-reduce.2.cloned.1.call-done), kind=kLoop, calls=%fused_computation.74 | loop fusion | flops 3931136 | bytes 7868416 | tf_op jit(solution)/shard_map/reduce_sum | solution.py:255
  272.2 3.7 %multiply_reduce_fusion = f32[1024]{0:T(1024)S(1)} fusion(f32[1024]{0:T(1024)S(1)} %broadcast_multiply_fusion, f32[1024,1280]{1,0:T(8,128)} %get-tuple-element.13, bf16[1024,1280]{1,0:T(8,128)(2,1)S(1)} %copy-done.9), kind=kLoop, calls=%fused_computation.12 | loop fusion | flops 6552576 | bytes 7872512 | tf_op jit(solution)/shard_map/reduce_sum | solution.py:257
  276.0 5.1 %fusion.16 = bf16[256,4,1280]{2,0,1:T(8,128)(2,1)} fusion(f32[1280]{0:T(1024)S(1)} %convert_element_type.51, f32[1024]{0:T(1024)S(1)} %add_rsqrt_fusion, f32[1024]{0:T(1024)S(1)} %broadcast_multiply_fusion, s32[256,4]{0,1:T(4,128)S(1)} %broadcast_subtract_fusion, f32[1024,1280]{1,0:T(8,128)S(1)} %bitcast.83, bf16[1024,1280]{1,0:T(8,128)(2,1)S(1)} %copy-done.9), kind=kOutput, calls=%fused_computation.31 | convolution fusion | flops 2694578176 | bytes 10503168 | tf_op jit(solution)/shard_map/mkt,tc->mkc/dot_general | solution.py:382
  281.1 4.8 %convolution_convert_fusion.1 = bf16[512,320]{0,1:T(8,128)(2,1)} fusion(bf16[256,4,1280]{2,0,1:T(8,128)(2,1)} %fusion.16, bf16[40,4,8,1280]{3,2,1,0:T(8,128)(2,1)} %bitcast.97, s32[256]{0:T(256)S(1)} %bitcast.96), kind=kOutput, calls=%fused_computation.76 | convolution fusion | flops 923123712 | bytes 6226944 | tf_op jit(solution)/shard_map/ms,mc->sc/dot_general | solution.py:400
  285.9 1.9 copy.31
  287.8 14.6 %shard_map.121 = bf16[32,16,320]{2,1,0:T(8,128)(2,1)} custom-call(bf16[32,16,320]{2,1,0:T(8,128)(2,1)} %bitcast.90), custom_call_target="tpu_custom_call" | custom-call | tf_op jit(solution)/shard_map/pallas_call | solution.py:207
  302.4 1.8 copy.47
  (54 shorter events, 1.0 us)
Async XLA Ops:
  6.5 160.8 %copy-start = (bf16[1280,1280]{1,0:T(8,128)(2,1)S(1)}, bf16[1280,1280]{1,0:T(8,128)(2,1)}, u32[]{:S(2)}) copy-start(bf16[1280,1280]{1,0:T(8,128)(2,1)} %param.19) | copy-start | bytes 9830404
  6.5 118.7 %all-gather.2.cloned.1.call-start = ((), (), s32[]{:S(2)}) async-start(), calls=%async_computation | async-start | bytes 4096000 | tf_op jit(solution)/shard_map/all_gather | solution.py:351
  7.3 260.9 %all-reduce.2.cloned.1.call-start = ((), (), s32[]{:S(2)}) async-start(), calls=%async_computation.1 | async-start | bytes 5242880 | tf_op jit(solution)/shard_map/psum | solution.py:377
  7.3 6.3 %copy-start.1 = (bf16[1024,1280]{1,0:T(8,128)(2,1)S(1)}, bf16[1024,1280]{1,0:T(8,128)(2,1)}, u32[]{:S(2)}) copy-start(bf16[1024,1280]{1,0:T(8,128)(2,1)} %tokens_ref.1) | copy-start | bytes 7864324
  7.3 6.3 %copy-start.16 = (bf16[1280,3,320]{0,2,1:T(8,128)(2,1)S(1)}, bf16[1280,3,320]{0,2,1:T(8,128)(2,1)}, u32[]{:S(2)}) copy-start(bf16[1280,3,320]{0,2,1:T(8,128)(2,1)} %param.15) | copy-start | bytes 7372804
  16.5 5.8 %copy-start.11 = (s32[1024]{0:T(1024)S(1)}, s32[1024]{0:T(1024)}, u32[]{:S(2)}) copy-start(s32[1024]{0:T(1024)} %param.13) | copy-start | bytes 12292
  22.3 1.1 copy-start.10
  84.6 1.2 copy-start.3
  85.8 1.0 copy-start.6
  86.9 1.9 copy-start.7
  88.8 36.5 %copy-start.14 = (bf16[1280]{0:T(1024)(128)(2,1)S(1)}, bf16[1280]{0:T(1024)(128)(2,1)}, u32[]{:S(2)}) copy-start(bf16[1280]{0:T(1024)(128)(2,1)} %param.17) | copy-start | bytes 7684
  119.9 1.0 copy-start.4
  125.3 1.7 copy-start.2
  127.0 1.1 copy-start.5
  165.7 1.6 copy-start.8
  167.3 20.1 %copy-start.13 = (bf16[1280]{0:T(1024)(128)(2,1)S(1)}, bf16[1280]{0:T(1024)(128)(2,1)}, u32[]{:S(2)}) copy-start(bf16[1280]{0:T(1024)(128)(2,1)} %param.20) | copy-start | bytes 7684
  167.3 20.1 %copy-start.12 = (s32[256,1]{0,1:T(1,128)S(1)}, s32[256,1]{0,1:T(1,128)}, u32[]{:S(2)}) copy-start(s32[256,1]{0,1:T(1,128)} %param.23) | copy-start | bytes 3076
  167.3 21.3 %copy-start.15 = (s32[256,4]{0,1:T(4,128)S(1)}, s32[256,4]{0,1:T(4,128)}, u32[]{:S(2)}) copy-start(s32[256,4]{0,1:T(4,128)} %param.22) | copy-start | bytes 12292
  268.2 4.0 %copy-start.9 = (bf16[1024,1280]{1,0:T(8,128)(2,1)S(1)}, bf16[1024,1280]{1,0:T(8,128)(2,1)}, u32[]{:S(2)}) copy-start(bf16[1024,1280]{1,0:T(8,128)(2,1)} %all-reduce.2.cloned.1.call-done) | copy-start | bytes 7864324
  268.2 7.8 %slice-start = ((s8[5242880]{0:T(1024)(128)(4,1)}), s8[4194304]{0:T(1024)(128)(4,1)S(1)}, s32[]{:S(2)}) async-start(s8[5242880]{0:T(1024)(128)(4,1)} %bitcast.82), calls=%async_computation.2 | async-start | bytes 8388608
  272.2 3.8 %slice-start.1 = ((s8[5242880]{0:T(1024)(128)(4,1)}), s8[1048576]{0:T(1024)(128)(4,1)S(1)}, s32[]{:S(2)}) async-start(s8[5242880]{0:T(1024)(128)(4,1)} %bitcast.82), calls=%async_computation.3 | async-start | bytes 2097152
Sparse Core Ops, SparseCore 0:
  9.0 43.8 all-gather.1
  187.5 80.5 all-reduce.1

commit v11 on v10

--- a/solution.py
+++ b/solution.py
@@ -10,7 +10,7 @@
 
 HD = 80
 TILE = 256
-QTILE = 128
+QTILE = 512
 NEAR = (1, -1, 2, -2)
 MESH_IDS = pl.DeviceIdType.MESH
 

time: 312 us -> 309 us (level)
  waiting for transfers between devices: 80.3 us -> 68.2 us
  Pallas kernels: 143 us -> 153 us
    psum x1, waiting for transfers between devices: 79.5 us -> 67.4 us  [body(): lax.psum(hidden_terms.astype(jnp.bfloat16), 'tp').astype(jnp.float32)]
    pallas_call x1, Pallas kernels: 37.6 us -> 43.3 us  [project(): pl.pallas_call(functools.partial(project_kernel, order), out_shape=(jax.S...]
    pallas_call x1, Pallas kernels: 31.1 us -> 35 us  [attention(): pl.pallas_call(flash_kernel, out_shape=jax.ShapeDtypeStruct(queries.shape...]
  transfers between devices with their start and end apart: 2 -> 2, of which waited for: 1 -> 1; matrix products, arithmetic and copies ran while one was open for 7% -> 7% of each run, Pallas kernels for 29% -> 31%
where the time goes in v11:
time: 309 us
  Pallas kernels  153 us (50%)
  waiting for transfers between devices  68.2 us (22%)
  matrix products  33 us (11%)
  local copies, waits for them, and re-layouts  24.8 us (8%)
  other arithmetic  16.2 us (5%)
  between operations  13.7 us (4%)
    psum x1, waiting for transfers between devices, body(): lax.psum(hidden_terms.astype(jnp.bfloat16), 'tp').astype(jnp.float32)  67.4 us
    pallas_call x1, Pallas kernels, exchange(): pl.pallas_call(functools.partial(exchange_kernel, order, n), out_shape=(j...  59.9 us
    pallas_call x1, Pallas kernels, project(): pl.pallas_call(functools.partial(project_kernel, order), out_shape=(jax.S...  43.3 us
    pallas_call x1, Pallas kernels, attention(): pl.pallas_call(flash_kernel, out_shape=jax.ShapeDtypeStruct(queries.shape...  35 us
    dot_general x1, matrix products, body(): jnp.dot(expanded, reduce_weight, preferred_element_type=jnp.float32)  20.2 us
    pallas_call x1, Pallas kernels, deliver(): pl.pallas_call(functools.partial(deliver_kernel, order, n), out_shape=jax...  14.6 us
    unnamed x39, local copies, waits for them, and re-layouts  11.4 us
    reduce_sum x2, other arithmetic, layer_norm(): center = jnp.mean(stream, axis=-1, keepdims=True)  6.83 us
  transfers between devices with their start and end apart: 2, of which 1 were waited for; matrix products, arithmetic and copies ran while one was open for 7% of the time, Pallas kernels for 31%

profile of v11, /device:TPU:1, one launch (start us, length us, event | category | flops | bytes accessed | tf_op | source)
XLA Modules:
  0.0 308.7 jit_solution(10254184464366812371)
XLA Ops:
  6.5 0.7 all-gather.2.cloned.1.call-update
  7.3 0.9 convert_element_type.45
  8.2 2.8 convert_reduce_fusion
  11.0 2.6 fusion.2
  13.6 2.9 fusion.62
  16.5 1.3 fusion.111
  17.9 2.2 copy.25
  20.1 2.3 copy.26
  22.4 1.1 copy.27.qm_ref
  23.4 59.9 %shard_map.118 = (bf16[4,80,5120]{2,1,0:T(8,128)(2,1)}, bf16[4,5120,80]{2,1,0:T(8,128)(2,1)}, s32[1,5120]{1,0:T(1,128)}) custom-call(bf16[4,80,1024]{2,1,0:T(8,128)(2,1)} %bitcast.83, bf16[4,1024,80]{2,1,0:T(8,128)(2,1)} %bitcast.81, s32[1,1024]{1,0:T(1,128)} %bitcast.89), custom_call_target="tpu_custom_call" | custom-call | tf_op jit(solution)/shard_map/pallas_call | solution.py:153
  83.5 0.8 and_select_fusion.km_ref
  84.6 1.2 copy-done.3
  85.8 1.0 copy-done.6
  86.9 1.9 copy-done.7
  88.8 35.0 %shard_map.119 = bf16[4,1024,80]{2,1,0:T(8,128)(2,1)S(1)} custom-call(s32[2,2]{1,0:T(2,128)S(1)} %pad_add_fusion.bounds, bf16[4,1024,80]{2,1,0:T(8,128)(2,1)S(1)} %bitcast.76, s32[1024,1]{1,0:T(8,128)S(1)} %copy-done.6, bf16[4,80,5120]{2,1,0:T(8,128)(2,1)S(1)} %copy-done.7, bf16[4,5120,80]{2,1,0:T(8,128)(2,1)} %get-tuple-element.12.v_ref, ...), custom_call_target="tpu_custom_call" | custom-call | flops 2684354560 | bytes 7864320 | tf_op jit(solution)/shard_map/pallas_call | solution.py:309
  123.8 1.0 copy-done.4
  124.8 2.2 copy.28
  127.0 2.2 copy.29.ctx_ref
  129.2 1.7 copy-done.2
  131.0 1.1 copy-done.5
  132.1 43.3 %shard_map.120 = (f32[1024,1280]{1,0:T(8,128)}, bf16[1024,1280]{1,0:T(8,128)(2,1)S(1)}) custom-call(bf16[1024,320]{1,0:T(8,128)(2,1)S(1)} %copy-done.5, bf16[1280,1280]{1,0:T(8,128)(2,1)} %all-gather.2.cloned.1.call-done.weight_ref, bf16[1024,1280]{1,0:T(8,128)(2,1)S(1)} %copy-done.2, bf16[1,1280]{1,0:T(2,128)(2,1)S(1)} %reshape.245.gain_ref), custom_call_target="tpu_custom_call" | custom-call | flops 3355443200 | bytes 13762560 | tf_op jit(solution)/shard_map/pallas_call | solution.py:224
  175.4 1.6 copy-done.8
  177.0 20.2 %convolution_convert_fusion = bf16[1024,1280]{1,0:T(8,128)(2,1)} fusion(bf16[1280,1280]{1,0:T(8,128)(2,1)S(1)} %copy-done, bf16[1024,1280]{1,0:T(8,128)(2,1)} %copy-done.8, bf16[1280,1280]{1,0:T(8,128)(2,1)} %param.18), kind=kOutput, calls=%fused_computation.32 | convolution fusion | flops 6797393920 | bytes 11796480 | tf_op jit(solution)/shard_map/dot_general | solution.py:376
  197.3 0.8 reduce-window.6
  198.5 67.4 %all-reduce.2.cloned.1.call-done = bf16[1024,1280]{1,0:T(8,128)(2,1)} async-done(((bf16[1024,1280]{1,0:T(8,128)(2,1)}), bf16[1024,1280]{1,0:T(8,128)(2,1)}) %all-reduce.2.cloned.1.call-update) | async-done | bytes 2621456 | tf_op jit(solution)/shard_map/psum | solution.py:377
  265.9 4.0 %fusion.61 = f32[1024]{0:T(1024)S(1)} fusion(f32[1024,1280]{1,0:T(8,128)} %get-tuple-element.13, bf16[1024,1280]{1,0:T(8,128)(2,1)} %all-reduce.2.cloned.1.call-done), kind=kLoop, calls=%fused_computation.74 | loop fusion | flops 3931136 | bytes 7868416 | tf_op jit(solution)/shard_map/reduce_sum | solution.py:255
  270.0 3.7 %multiply_reduce_fusion = f32[1024]{0:T(1024)S(1)} fusion(f32[1024]{0:T(1024)S(1)} %broadcast_multiply_fusion, f32[1024,1280]{1,0:T(8,128)} %get-tuple-element.13, bf16[1024,1280]{1,0:T(8,128)(2,1)S(1)} %copy-done.9), kind=kLoop, calls=%fused_computation.12 | loop fusion | flops 6552576 | bytes 7872512 | tf_op jit(solution)/shard_map/reduce_sum | solution.py:257
  273.8 5.1 %fusion.16 = bf16[256,4,1280]{2,0,1:T(8,128)(2,1)} fusion(f32[1280]{0:T(1024)S(1)} %convert_element_type.51, f32[1024]{0:T(1024)S(1)} %add_rsqrt_fusion, f32[1024]{0:T(1024)S(1)} %broadcast_multiply_fusion, s32[256,4]{0,1:T(4,128)S(1)} %broadcast_subtract_fusion, f32[1024,1280]{1,0:T(8,128)S(1)} %bitcast.80, bf16[1024,1280]{1,0:T(8,128)(2,1)S(1)} %copy-done.9), kind=kOutput, calls=%fused_computation.31 | convolution fusion | flops 2694578176 | bytes 10503168 | tf_op jit(solution)/shard_map/mkt,tc->mkc/dot_general | solution.py:382
  278.9 4.8 %convolution_convert_fusion.1 = bf16[512,320]{0,1:T(8,128)(2,1)} fusion(bf16[256,4,1280]{2,0,1:T(8,128)(2,1)} %fusion.16, bf16[40,4,8,1280]{3,2,1,0:T(8,128)(2,1)} %bitcast.94, s32[256]{0:T(256)S(1)} %bitcast.93), kind=kOutput, calls=%fused_computation.76 | convolution fusion | flops 923123712 | bytes 6226944 | tf_op jit(solution)/shard_map/ms,mc->sc/dot_general | solution.py:400
  283.6 1.9 copy.31
  285.5 14.6 %shard_map.121 = bf16[32,16,320]{2,1,0:T(8,128)(2,1)} custom-call(bf16[32,16,320]{2,1,0:T(8,128)(2,1)} %bitcast.87), custom_call_target="tpu_custom_call" | custom-call | tf_op jit(solution)/shard_map/pallas_call | solution.py:207
  300.1 1.8 copy.47
  (55 shorter events, 1.0 us)
Async XLA Ops:
  6.5 170.5 %copy-start = (bf16[1280,1280]{1,0:T(8,128)(2,1)S(1)}, bf16[1280,1280]{1,0:T(8,128)(2,1)}, u32[]{:S(2)}) copy-start(bf16[1280,1280]{1,0:T(8,128)(2,1)} %param.19) | copy-start | bytes 9830404
  6.5 122.7 %all-gather.2.cloned.1.call-start = ((), (), s32[]{:S(2)}) async-start(), calls=%async_computation | async-start | bytes 4096000 | tf_op jit(solution)/shard_map/all_gather | solution.py:351
  7.3 258.7 %all-reduce.2.cloned.1.call-start = ((), (), s32[]{:S(2)}) async-start(), calls=%async_computation.1 | async-start | bytes 5242880 | tf_op jit(solution)/shard_map/psum | solution.py:377
  7.3 6.3 %copy-start.1 = (bf16[1024,1280]{1,0:T(8,128)(2,1)S(1)}, bf16[1024,1280]{1,0:T(8,128)(2,1)}, u32[]{:S(2)}) copy-start(bf16[1024,1280]{1,0:T(8,128)(2,1)} %tokens_ref.1) | copy-start | bytes 7864324
  7.3 6.3 %copy-start.16 = (bf16[1280,3,320]{0,2,1:T(8,128)(2,1)S(1)}, bf16[1280,3,320]{0,2,1:T(8,128)(2,1)}, u32[]{:S(2)}) copy-start(bf16[1280,3,320]{0,2,1:T(8,128)(2,1)} %param.15) | copy-start | bytes 7372804
  16.5 3.6 %copy-start.13 = (s32[1024]{0:T(1024)S(1)}, s32[1024]{0:T(1024)}, u32[]{:S(2)}) copy-start(s32[1024]{0:T(1024)} %param.13) | copy-start | bytes 12292
  20.1 3.3 %copy-start.10 = (s32[1024]{0:T(1024)}, s32[1024]{0:T(1024)S(1)}, u32[]{:S(2)}) copy-start(s32[1024]{0:T(1024)S(1)} %broadcast_add_fusion) | copy-start | bytes 12292
  84.6 1.2 copy-start.3
  85.8 1.0 copy-start.6
  86.9 1.9 copy-start.7
  88.8 40.4 %copy-start.14 = (bf16[1280]{0:T(1024)(128)(2,1)S(1)}, bf16[1280]{0:T(1024)(128)(2,1)}, u32[]{:S(2)}) copy-start(bf16[1280]{0:T(1024)(128)(2,1)} %param.17) | copy-start | bytes 7684
  123.8 1.0 copy-start.4
  129.2 1.7 copy-start.2
  131.0 1.1 copy-start.5
  175.4 1.6 copy-start.8
  177.0 20.3 %copy-start.12 = (bf16[1280]{0:T(1024)(128)(2,1)S(1)}, bf16[1280]{0:T(1024)(128)(2,1)}, u32[]{:S(2)}) copy-start(bf16[1280]{0:T(1024)(128)(2,1)} %param.20) | copy-start | bytes 7684
  177.0 20.3 %copy-start.11 = (s32[256,1]{0,1:T(1,128)S(1)}, s32[256,1]{0,1:T(1,128)}, u32[]{:S(2)}) copy-start(s32[256,1]{0,1:T(1,128)} %param.23) | copy-start | bytes 3076
  177.0 21.4 %copy-start.15 = (s32[256,4]{0,1:T(4,128)S(1)}, s32[256,4]{0,1:T(4,128)}, u32[]{:S(2)}) copy-start(s32[256,4]{0,1:T(4,128)} %param.22) | copy-start | bytes 12292
  265.9 4.0 %copy-start.9 = (bf16[1024,1280]{1,0:T(8,128)(2,1)S(1)}, bf16[1024,1280]{1,0:T(8,128)(2,1)}, u32[]{:S(2)}) copy-start(bf16[1024,1280]{1,0:T(8,128)(2,1)} %all-reduce.2.cloned.1.call-done) | copy-start | bytes 7864324
  265.9 7.8 %slice-start = ((s8[5242880]{0:T(1024)(128)(4,1)}), s8[4194304]{0:T(1024)(128)(4,1)S(1)}, s32[]{:S(2)}) async-start(s8[5242880]{0:T(1024)(128)(4,1)} %bitcast.79), calls=%async_computation.2 | async-start | bytes 8388608
  270.0 3.8 %slice-start.1 = ((s8[5242880]{0:T(1024)(128)(4,1)}), s8[1048576]{0:T(1024)(128)(4,1)S(1)}, s32[]{:S(2)}) async-start(s8[5242880]{0:T(1024)(128)(4,1)} %bitcast.79), calls=%async_computation.3 | async-start | bytes 2097152
Sparse Core Ops, SparseCore 0:
  9.0 43.8 all-gather.1
  197.4 68.4 all-reduce.1

commit v12 on v8

--- a/solution.py
+++ b/solution.py
@@ -291,7 +291,9 @@
         jnp.zeros((heads, rows, width), jnp.float32),
     )
     _, total, weighted = lax.fori_loop(bounds[0, i], bounds[1, i], step, init)
-    o_ref[...] = (weighted / total).astype(o_ref.dtype)
+    result = (weighted / total).astype(o_ref.dtype)
+    for h in range(heads):
+        o_ref[:, h * width : (h + 1) * width] = result[h]
 
 
 def attention(queries, query_marks, keys, values, key_marks):
@@ -307,7 +309,7 @@
     bounds = jnp.stack([first // TILE, last // TILE + 1]).astype(jnp.int32)
     return pl.pallas_call(
         flash_kernel,
-        out_shape=jax.ShapeDtypeStruct(queries.shape, queries.dtype),
+        out_shape=jax.ShapeDtypeStruct((rows, heads * width), queries.dtype),
         grid_spec=pltpu.PrefetchScalarGridSpec(
             num_scalar_prefetch=1,
             grid=(tiles,),
@@ -318,7 +320,7 @@
                 pl.BlockSpec((heads, key_rows, width), lambda i, b: (0, 0, 0)),
                 pl.BlockSpec((1, key_rows), lambda i, b: (0, 0)),
             ],
-            out_specs=pl.BlockSpec((heads, TILE, width), lambda i, b: (0, i, 0)),
+            out_specs=pl.BlockSpec((TILE, heads * width), lambda i, b: (i, 0)),
         ),
         compiler_params=pltpu.CompilerParams(vmem_limit_bytes=48 * 1024 * 1024),
         cost_estimate=pl.CostEstimate(
@@ -367,7 +369,6 @@
         order,
     )
     context = attention(by_head(projected[:, :head_width]), marks, keys_all, values_all, key_marks)
-    context = jnp.transpose(context, (1, 0, 2)).reshape(token_rows, head_width)
     middle, mixer_in = project(context, full_weight, tokens, mixer_gain, order)
     expanded = jax.nn.gelu(
         jnp.dot(mixer_in, expand_weight, preferred_element_type=jnp.float32), approximate=False

time: 310 us -> 305 us (0.984)
  Pallas kernels: 141 us -> 151 us
  waiting for transfers between devices: 80.1 us -> 70.8 us
  local copies, waits for them, and re-layouts: 24.8 us -> 20.3 us
    psum x1, waiting for transfers between devices: 79.4 us -> 70.1 us  [body(): lax.psum(hidden_terms.astype(jnp.bfloat16), 'tp').astype(jnp.float32)]
    pallas_call x1, Pallas kernels: 23.8 us -> 32.8 us  [attention(): pl.pallas_call(flash_kernel, out_shape=jax.ShapeDtypeStruct((rows, heads...]
  transfers between devices with their start and end apart: 2 -> 2, of which waited for: 1 -> 1; matrix products, arithmetic and copies ran while one was open for 7% -> 6% of each run, Pallas kernels for 27% -> 30%
where the time goes in v12:
time: 305 us
  Pallas kernels  151 us (50%)
  waiting for transfers between devices  70.8 us (23%)
  matrix products  32.8 us (11%)
  local copies, waits for them, and re-layouts  20.3 us (7%)
  other arithmetic  16.2 us (5%)
  between operations  13.7 us (4%)
    psum x1, waiting for transfers between devices, body(): lax.psum(hidden_terms.astype(jnp.bfloat16), 'tp').astype(jnp.float32)  70.1 us
    pallas_call x1, Pallas kernels, exchange(): pl.pallas_call(functools.partial(exchange_kernel, order, n), out_shape=(j...  60 us
    pallas_call x1, Pallas kernels, project(): pl.pallas_call(functools.partial(project_kernel, order), out_shape=(jax.S...  43.5 us
    pallas_call x1, Pallas kernels, attention(): pl.pallas_call(flash_kernel, out_shape=jax.ShapeDtypeStruct((rows, heads...  32.8 us
    dot_general x1, matrix products, body(): jnp.dot(expanded, reduce_weight, preferred_element_type=jnp.float32)  20.1 us
    pallas_call x1, Pallas kernels, deliver(): pl.pallas_call(functools.partial(deliver_kernel, order, n), out_shape=jax...  14.6 us
    unnamed x39, local copies, waits for them, and re-layouts  11.3 us
    reduce_sum x2, other arithmetic, layer_norm(): center = jnp.mean(stream, axis=-1, keepdims=True)  6.83 us
  transfers between devices with their start and end apart: 2, of which 1 were waited for; matrix products, arithmetic and copies ran while one was open for 6% of the time, Pallas kernels for 30%

profile of v12, /device:TPU:1, one launch (start us, length us, event | category | flops | bytes accessed | tf_op | source)
XLA Modules:
  0.0 304.8 jit_solution(13766973745936136319)
XLA Ops:
  6.5 0.7 all-gather.2.cloned.1.call-update
  7.3 0.9 convert_element_type.45
  8.2 2.8 convert_reduce_fusion
  11.0 2.6 fusion.2
  13.6 2.9 fusion.62
  16.5 1.3 fusion.111
  17.9 2.2 copy.22
  20.1 2.3 copy.23
  22.4 1.1 copy.24.qm_ref
  23.4 60.0 %shard_map.118 = (bf16[4,80,5120]{2,1,0:T(8,128)(2,1)}, bf16[4,5120,80]{2,1,0:T(8,128)(2,1)}, s32[1,5120]{1,0:T(1,128)}) custom-call(bf16[4,80,1024]{2,1,0:T(8,128)(2,1)} %bitcast.79, bf16[4,1024,80]{2,1,0:T(8,128)(2,1)} %bitcast.78, s32[1,1024]{1,0:T(1,128)} %bitcast.85), custom_call_target="tpu_custom_call" | custom-call | tf_op jit(solution)/shard_map/pallas_call | solution.py:152
  83.6 0.8 and_select_fusion.km_ref
  84.4 0.3 select_reduce_fusion.1
  84.7 1.2 copy-done.3
  86.0 1.0 copy-done.4
  87.0 1.9 copy-done.5
  88.9 32.8 %shard_map.119.ctx_ref = bf16[1024,320]{1,0:T(8,128)(2,1)S(1)} custom-call(s32[2,4]{1,0:T(2,128)S(1)} %pad_add_fusion.bounds, bf16[4,1024,80]{2,1,0:T(8,128)(2,1)S(1)} %bitcast.74, s32[1024,1]{1,0:T(8,128)S(1)} %copy-done.4, bf16[4,80,5120]{2,1,0:T(8,128)(2,1)S(1)} %copy-done.5, bf16[4,5120,80]{2,1,0:T(8,128)(2,1)} %get-tuple-element.12.v_ref, ...), custom_call_target="tpu_custom_call" | custom-call | flops 2684354560 | bytes 7864320 | tf_op jit(solution)/shard_map/pallas_call | solution.py:310
  121.8 0.9 copy-done.7
  122.6 1.7 copy-done.2
  124.4 1.1 copy-done.8
  125.5 43.5 %shard_map.120 = (f32[1024,1280]{1,0:T(8,128)}, bf16[1024,1280]{1,0:T(8,128)(2,1)S(1)}) custom-call(bf16[1024,320]{1,0:T(8,128)(2,1)S(1)} %copy-done.8, bf16[1280,1280]{1,0:T(8,128)(2,1)} %all-gather.2.cloned.1.call-done.weight_ref, bf16[1024,1280]{1,0:T(8,128)(2,1)S(1)} %copy-done.2, bf16[1,1280]{1,0:T(2,128)(2,1)S(1)} %reshape.241.gain_ref), custom_call_target="tpu_custom_call" | custom-call | flops 3355443200 | bytes 13762560 | tf_op jit(solution)/shard_map/pallas_call | solution.py:223
  169.0 1.6 copy-done.6
  170.6 20.1 %convolution_convert_fusion = bf16[1024,1280]{1,0:T(8,128)(2,1)} fusion(bf16[1280,1280]{1,0:T(8,128)(2,1)S(1)} %copy-done, bf16[1024,1280]{1,0:T(8,128)(2,1)} %copy-done.6, bf16[1280,1280]{1,0:T(8,128)(2,1)} %param.18), kind=kOutput, calls=%fused_computation.32 | convolution fusion | flops 6797393920 | bytes 11796480 | tf_op jit(solution)/shard_map/dot_general | solution.py:376
  190.7 0.8 reduce-window.6
  191.5 0.2 slice_reduce_fusion
  191.9 70.1 %all-reduce.2.cloned.1.call-done = bf16[1024,1280]{1,0:T(8,128)(2,1)} async-done(((bf16[1024,1280]{1,0:T(8,128)(2,1)}), bf16[1024,1280]{1,0:T(8,128)(2,1)}) %all-reduce.2.cloned.1.call-update) | async-done | bytes 2621456 | tf_op jit(solution)/shard_map/psum | solution.py:377
  262.0 4.0 %fusion.61 = f32[1024]{0:T(1024)S(1)} fusion(f32[1024,1280]{1,0:T(8,128)} %get-tuple-element.13, bf16[1024,1280]{1,0:T(8,128)(2,1)} %all-reduce.2.cloned.1.call-done), kind=kLoop, calls=%fused_computation.74 | loop fusion | flops 3931136 | bytes 7868416 | tf_op jit(solution)/shard_map/reduce_sum | solution.py:254
  266.0 3.7 %multiply_reduce_fusion = f32[1024]{0:T(1024)S(1)} fusion(f32[1024]{0:T(1024)S(1)} %broadcast_multiply_fusion, f32[1024,1280]{1,0:T(8,128)} %get-tuple-element.13, bf16[1024,1280]{1,0:T(8,128)(2,1)S(1)} %copy-done.9), kind=kLoop, calls=%fused_computation.12 | loop fusion | flops 6552576 | bytes 7872512 | tf_op jit(solution)/shard_map/reduce_sum | solution.py:256
  269.8 5.1 %fusion.16 = bf16[256,4,1280]{2,0,1:T(8,128)(2,1)} fusion(f32[1280]{0:T(1024)S(1)} %convert_element_type.51, f32[1024]{0:T(1024)S(1)} %add_rsqrt_fusion, f32[1024]{0:T(1024)S(1)} %broadcast_multiply_fusion, s32[256,4]{0,1:T(4,128)S(1)} %broadcast_subtract_fusion, f32[1024,1280]{1,0:T(8,128)S(1)} %bitcast.77, bf16[1024,1280]{1,0:T(8,128)(2,1)S(1)} %copy-done.9), kind=kOutput, calls=%fused_computation.31 | convolution fusion | flops 2694578176 | bytes 10503168 | tf_op jit(solution)/shard_map/mkt,tc->mkc/dot_general | solution.py:382
  274.9 4.8 %convolution_convert_fusion.1 = bf16[512,320]{0,1:T(8,128)(2,1)} fusion(bf16[256,4,1280]{2,0,1:T(8,128)(2,1)} %fusion.16, bf16[40,4,8,1280]{3,2,1,0:T(8,128)(2,1)} %bitcast.90, s32[256]{0:T(256)S(1)} %bitcast.89), kind=kOutput, calls=%fused_computation.76 | convolution fusion | flops 923123712 | bytes 6226944 | tf_op jit(solution)/shard_map/ms,mc->sc/dot_general | solution.py:400
  279.7 1.9 copy.26
  281.6 14.6 %shard_map.121 = bf16[32,16,320]{2,1,0:T(8,128)(2,1)} custom-call(bf16[32,16,320]{2,1,0:T(8,128)(2,1)} %bitcast.83), custom_call_target="tpu_custom_call" | custom-call | tf_op jit(solution)/shard_map/pallas_call | solution.py:206
  296.2 1.8 copy.42
  (53 shorter events, 0.5 us)
Async XLA Ops:
  6.5 164.0 %copy-start = (bf16[1280,1280]{1,0:T(8,128)(2,1)S(1)}, bf16[1280,1280]{1,0:T(8,128)(2,1)}, u32[]{:S(2)}) copy-start(bf16[1280,1280]{1,0:T(8,128)(2,1)} %param.19) | copy-start | bytes 9830404
  6.5 116.1 %all-gather.2.cloned.1.call-start = ((), (), s32[]{:S(2)}) async-start(), calls=%async_computation | async-start | bytes 4096000 | tf_op jit(solution)/shard_map/all_gather | solution.py:352
  7.3 254.7 %all-reduce.2.cloned.1.call-start = ((), (), s32[]{:S(2)}) async-start(), calls=%async_computation.1 | async-start | bytes 5242880 | tf_op jit(solution)/shard_map/psum | solution.py:377
  7.3 6.3 %copy-start.1 = (bf16[1024,1280]{1,0:T(8,128)(2,1)S(1)}, bf16[1024,1280]{1,0:T(8,128)(2,1)}, u32[]{:S(2)}) copy-start(bf16[1024,1280]{1,0:T(8,128)(2,1)} %tokens_ref.1) | copy-start | bytes 7864324
  7.3 6.3 %copy-start.16 = (bf16[1280,3,320]{0,2,1:T(8,128)(2,1)S(1)}, bf16[1280,3,320]{0,2,1:T(8,128)(2,1)}, u32[]{:S(2)}) copy-start(bf16[1280,3,320]{0,2,1:T(8,128)(2,1)} %param.15) | copy-start | bytes 7372804
  16.5 3.6 %copy-start.13 = (s32[1024]{0:T(1024)S(1)}, s32[1024]{0:T(1024)}, u32[]{:S(2)}) copy-start(s32[1024]{0:T(1024)} %param.13) | copy-start | bytes 12292
  16.5 6.9 %copy-start.14 = (bf16[1280]{0:T(1024)(128)(2,1)S(1)}, bf16[1280]{0:T(1024)(128)(2,1)}, u32[]{:S(2)}) copy-start(bf16[1280]{0:T(1024)(128)(2,1)} %param.17) | copy-start | bytes 7684
  20.1 3.3 %copy-start.10 = (s32[1024]{0:T(1024)}, s32[1024]{0:T(1024)S(1)}, u32[]{:S(2)}) copy-start(s32[1024]{0:T(1024)S(1)} %broadcast_add_fusion) | copy-start | bytes 12292
  84.7 1.2 copy-start.3
  86.0 1.0 copy-start.4
  87.0 1.9 copy-start.5
  121.8 0.9 copy-start.7
  122.6 1.7 copy-start.2
  124.4 1.1 copy-start.8
  169.0 1.6 copy-start.6
  170.6 20.1 %copy-start.12 = (bf16[1280]{0:T(1024)(128)(2,1)S(1)}, bf16[1280]{0:T(1024)(128)(2,1)}, u32[]{:S(2)}) copy-start(bf16[1280]{0:T(1024)(128)(2,1)} %param.20) | copy-start | bytes 7684
  170.6 20.1 %copy-start.11 = (s32[256,1]{0,1:T(1,128)S(1)}, s32[256,1]{0,1:T(1,128)}, u32[]{:S(2)}) copy-start(s32[256,1]{0,1:T(1,128)} %param.23) | copy-start | bytes 3076
  170.6 21.3 %copy-start.15 = (s32[256,4]{0,1:T(4,128)S(1)}, s32[256,4]{0,1:T(4,128)}, u32[]{:S(2)}) copy-start(s32[256,4]{0,1:T(4,128)} %param.22) | copy-start | bytes 12292
  262.0 4.0 %copy-start.9 = (bf16[1024,1280]{1,0:T(8,128)(2,1)S(1)}, bf16[1024,1280]{1,0:T(8,128)(2,1)}, u32[]{:S(2)}) copy-start(bf16[1024,1280]{1,0:T(8,128)(2,1)} %all-reduce.2.cloned.1.call-done) | copy-start | bytes 7864324
  262.0 7.8 %slice-start = ((s8[5242880]{0:T(1024)(128)(4,1)}), s8[4194304]{0:T(1024)(128)(4,1)S(1)}, s32[]{:S(2)}) async-start(s8[5242880]{0:T(1024)(128)(4,1)} %bitcast.76), calls=%async_computation.2 | async-start | bytes 8388608
  266.0 3.8 %slice-start.1 = ((s8[5242880]{0:T(1024)(128)(4,1)}), s8[1048576]{0:T(1024)(128)(4,1)S(1)}, s32[]{:S(2)}) async-start(s8[5242880]{0:T(1024)(128)(4,1)} %bitcast.76), calls=%async_computation.3 | async-start | bytes 2097152
Sparse Core Ops, SparseCore 0:
  9.0 43.8 all-gather.1
  190.8 71.1 all-reduce.1

commit v13 on v12

--- a/solution.py
+++ b/solution.py
@@ -261,7 +261,8 @@
     i = pl.program_id(0)
     tile = TILE
     factor = 1.0 / math.sqrt(HD)
-    q = q_ref[...]
+    heads = k_ref.shape[0]
+    q = jnp.stack([q_ref[:, h * HD : (h + 1) * HD] for h in range(heads)])
     qm = qm_ref[...]
 
     def step(j, carry):
@@ -297,7 +298,8 @@
 
 
 def attention(queries, query_marks, keys, values, key_marks):
-    heads, rows, width = queries.shape
+    heads = keys.shape[0]
+    rows, width = queries.shape[0], queries.shape[1] // heads
     key_rows = keys.shape[2]
     tiles = rows // TILE
     low = query_marks.reshape(tiles, TILE).min(axis=1)
@@ -314,7 +316,7 @@
             num_scalar_prefetch=1,
             grid=(tiles,),
             in_specs=[
-                pl.BlockSpec((heads, TILE, width), lambda i, b: (0, i, 0)),
+                pl.BlockSpec((TILE, heads * width), lambda i, b: (i, 0)),
                 pl.BlockSpec((TILE, 1), lambda i, b: (i, 0)),
                 pl.BlockSpec((heads, width, key_rows), lambda i, b: (0, 0, 0)),
                 pl.BlockSpec((heads, key_rows, width), lambda i, b: (0, 0, 0)),
@@ -368,7 +370,7 @@
         marks,
         order,
     )
-    context = attention(by_head(projected[:, :head_width]), marks, keys_all, values_all, key_marks)
+    context = attention(projected[:, :head_width], marks, keys_all, values_all, key_marks)
     middle, mixer_in = project(context, full_weight, tokens, mixer_gain, order)
     expanded = jax.nn.gelu(
         jnp.dot(mixer_in, expand_weight, preferred_element_type=jnp.float32), approximate=False

time: 305 us -> 309 us (1.013)
    pallas_call x1, Pallas kernels: 43.5 us -> 38.1 us  [project(): pl.pallas_call(functools.partial(project_kernel, order), out_shape=(jax.S...]
    slice x1 -> x3, local copies, waits for them, and re-layouts: 0.18 us -> 4.71 us  [the longest x1 2.29 us: body(): projected[:, head_width:2 * head_width].reshape(-1, head_count, HD)]
    pallas_call x1, Pallas kernels: 32.8 us -> 36.5 us  [attention(): pl.pallas_call(flash_kernel, out_shape=jax.ShapeDtypeStruct((rows, heads...]
  transfers between devices with their start and end apart: 2 -> 2, of which waited for: 1 -> 1; matrix products, arithmetic and copies ran while one was open for 6% -> 7% of each run, Pallas kernels for 30% -> 31%
where the time goes in v13:
time: 309 us
  Pallas kernels  149 us (48%)
  waiting for transfers between devices  72.9 us (24%)
  matrix products  33.6 us (11%)
  local copies, waits for them, and re-layouts  22.9 us (7%)
  other arithmetic  16.2 us (5%)
  between operations  13.7 us (4%)
    psum x1, waiting for transfers between devices, body(): lax.psum(hidden_terms.astype(jnp.bfloat16), 'tp').astype(jnp.float32)  72.1 us
    pallas_call x1, Pallas kernels, exchange(): pl.pallas_call(functools.partial(exchange_kernel, order, n), out_shape=(j...  60 us
    pallas_call x1, Pallas kernels, project(): pl.pallas_call(functools.partial(project_kernel, order), out_shape=(jax.S...  38.1 us
    pallas_call x1, Pallas kernels, attention(): pl.pallas_call(flash_kernel, out_shape=jax.ShapeDtypeStruct((rows, heads...  36.5 us
    dot_general x1, matrix products, body(): jnp.dot(expanded, reduce_weight, preferred_element_type=jnp.float32)  20.2 us
    pallas_call x1, Pallas kernels, deliver(): pl.pallas_call(functools.partial(deliver_kernel, order, n), out_shape=jax...  14.6 us
    unnamed x39, local copies, waits for them, and re-layouts  11.2 us
    reduce_sum x2, other arithmetic, layer_norm(): center = jnp.mean(stream, axis=-1, keepdims=True)  6.83 us
  transfers between devices with their start and end apart: 2, of which 1 were waited for; matrix products, arithmetic and copies ran while one was open for 7% of the time, Pallas kernels for 31%

profile of v13, /device:TPU:1, one launch (start us, length us, event | category | flops | bytes accessed | tf_op | source)
XLA Modules:
  0.0 308.5 jit_solution(10374904635983200161)
XLA Ops:
  6.5 0.7 all-gather.2.cloned.1.call-update
  7.3 0.9 convert_element_type.45
  8.2 2.8 convert_reduce_fusion
  11.0 2.6 fusion.2
  13.6 3.4 %fusion.62 = bf16[1024,960]{1,0:T(8,128)(2,1)S(1)} fusion(bf16[1280,960]{0,1:T(8,128)(2,1)S(1)} %bitcast.87, bf16[1024,1280]{1,0:T(8,128)(2,1)S(1)} %copy-done.1, f32[1280]{0:T(1024)S(1)} %convert_element_type.45, f32[1024]{0:T(1024)S(1)} %add_rsqrt_fusion.1, f32[1024]{0:T(1024)S(1)} %broadcast_multiply_fusion.1), kind=kOutput, calls=%fused_computation.75 | convolution fusion | flops 2524119040 | bytes 7058432 | tf_op jit(solution)/shard_map/dot_general | solution.py:357
  17.1 1.8 fusion.111
  18.9 2.2 copy.29
  21.2 2.2 copy.30
  23.4 2.3 copy.28
  25.7 1.0 copy.31.qm_ref
  26.7 60.0 %shard_map.118 = (bf16[4,80,5120]{2,1,0:T(8,128)(2,1)}, bf16[4,5120,80]{2,1,0:T(8,128)(2,1)}, s32[1,5120]{1,0:T(1,128)}) custom-call(bf16[4,80,1024]{2,1,0:T(8,128)(2,1)} %bitcast.76, bf16[4,1024,80]{2,1,0:T(8,128)(2,1)} %bitcast.75, s32[1,1024]{1,0:T(1,128)} %bitcast.81), custom_call_target="tpu_custom_call" | custom-call | tf_op jit(solution)/shard_map/pallas_call | solution.py:152
  86.9 0.8 and_select_fusion.km_ref
  87.7 0.3 select_reduce_fusion.1
  88.0 1.1 copy-done.3
  89.1 1.0 copy-done.4
  90.2 1.9 copy-done.5
  92.1 36.5 %shard_map.119.ctx_ref = bf16[1024,320]{1,0:T(8,128)(2,1)S(1)} custom-call(s32[2,4]{1,0:T(2,128)S(1)} %pad_add_fusion.bounds, bf16[1024,320]{1,0:T(8,128)(2,1)S(1)} %copy-done.3, s32[1024,1]{1,0:T(8,128)S(1)} %copy-done.4, bf16[4,80,5120]{2,1,0:T(8,128)(2,1)S(1)} %copy-done.5, bf16[4,5120,80]{2,1,0:T(8,128)(2,1)} %get-tuple-element.12.v_ref, ...), custom_call_target="tpu_custom_call" | custom-call | flops 2684354560 | bytes 7864320 | tf_op jit(solution)/shard_map/pallas_call | solution.py:312
  128.6 0.9 copy-done.7
  129.5 1.7 copy-done.2
  131.2 1.1 copy-done.8
  132.4 38.1 %shard_map.120 = (f32[1024,1280]{1,0:T(8,128)}, bf16[1024,1280]{1,0:T(8,128)(2,1)S(1)}) custom-call(bf16[1024,320]{1,0:T(8,128)(2,1)S(1)} %copy-done.8, bf16[1280,1280]{1,0:T(8,128)(2,1)} %all-gather.2.cloned.1.call-done.weight_ref, bf16[1024,1280]{1,0:T(8,128)(2,1)S(1)} %copy-done.2, bf16[1,1280]{1,0:T(2,128)(2,1)S(1)} %reshape.237.gain_ref), custom_call_target="tpu_custom_call" | custom-call | flops 3355443200 | bytes 13762560 | tf_op jit(solution)/shard_map/pallas_call | solution.py:223
  170.5 1.6 copy-done.6
  172.1 20.2 %convolution_convert_fusion = bf16[1024,1280]{1,0:T(8,128)(2,1)} fusion(bf16[1280,1280]{1,0:T(8,128)(2,1)S(1)} %copy-done, bf16[1024,1280]{1,0:T(8,128)(2,1)} %copy-done.6, bf16[1280,1280]{1,0:T(8,128)(2,1)} %param.18), kind=kOutput, calls=%fused_computation.32 | convolution fusion | flops 6797393920 | bytes 11796480 | tf_op jit(solution)/shard_map/dot_general | solution.py:378
  192.4 0.8 reduce-window.6
  193.6 72.1 %all-reduce.2.cloned.1.call-done = bf16[1024,1280]{1,0:T(8,128)(2,1)} async-done(((bf16[1024,1280]{1,0:T(8,128)(2,1)}), bf16[1024,1280]{1,0:T(8,128)(2,1)}) %all-reduce.2.cloned.1.call-update) | async-done | bytes 2621456 | tf_op jit(solution)/shard_map/psum | solution.py:379
  265.7 4.0 %fusion.61 = f32[1024]{0:T(1024)S(1)} fusion(f32[1024,1280]{1,0:T(8,128)} %get-tuple-element.13, bf16[1024,1280]{1,0:T(8,128)(2,1)} %all-reduce.2.cloned.1.call-done), kind=kLoop, calls=%fused_computation.74 | loop fusion | flops 3931136 | bytes 7868416 | tf_op jit(solution)/shard_map/reduce_sum | solution.py:254
  269.8 3.7 %multiply_reduce_fusion = f32[1024]{0:T(1024)S(1)} fusion(f32[1024]{0:T(1024)S(1)} %broadcast_multiply_fusion, f32[1024,1280]{1,0:T(8,128)} %get-tuple-element.13, bf16[1024,1280]{1,0:T(8,128)(2,1)S(1)} %copy-done.9), kind=kLoop, calls=%fused_computation.12 | loop fusion | flops 6552576 | bytes 7872512 | tf_op jit(solution)/shard_map/reduce_sum | solution.py:256
  273.5 5.1 %fusion.16 = bf16[256,4,1280]{2,0,1:T(8,128)(2,1)} fusion(f32[1280]{0:T(1024)S(1)} %convert_element_type.51, f32[1024]{0:T(1024)S(1)} %add_rsqrt_fusion, f32[1024]{0:T(1024)S(1)} %broadcast_multiply_fusion, s32[256,4]{0,1:T(4,128)S(1)} %broadcast_subtract_fusion, f32[1024,1280]{1,0:T(8,128)S(1)} %bitcast.74, bf16[1024,1280]{1,0:T(8,128)(2,1)S(1)} %copy-done.9), kind=kOutput, calls=%fused_computation.31 | convolution fusion | flops 2694578176 | bytes 10503168 | tf_op jit(solution)/shard_map/mkt,tc->mkc/dot_general | solution.py:384
  278.7 4.8 %convolution_convert_fusion.1 = bf16[512,320]{0,1:T(8,128)(2,1)} fusion(bf16[256,4,1280]{2,0,1:T(8,128)(2,1)} %fusion.16, bf16[40,4,8,1280]{3,2,1,0:T(8,128)(2,1)} %bitcast.86, s32[256]{0:T(256)S(1)} %bitcast.85), kind=kOutput, calls=%fused_computation.76 | convolution fusion | flops 923123712 | bytes 6226944 | tf_op jit(solution)/shard_map/ms,mc->sc/dot_general | solution.py:402
  283.4 1.9 copy.33
  285.3 14.6 %shard_map.121 = bf16[32,16,320]{2,1,0:T(8,128)(2,1)} custom-call(bf16[32,16,320]{2,1,0:T(8,128)(2,1)} %bitcast.79), custom_call_target="tpu_custom_call" | custom-call | tf_op jit(solution)/shard_map/pallas_call | solution.py:206
  299.9 1.8 copy.50
  (54 shorter events, 0.7 us)
Async XLA Ops:
  6.5 165.6 %copy-start = (bf16[1280,1280]{1,0:T(8,128)(2,1)S(1)}, bf16[1280,1280]{1,0:T(8,128)(2,1)}, u32[]{:S(2)}) copy-start(bf16[1280,1280]{1,0:T(8,128)(2,1)} %param.19) | copy-start | bytes 9830404
  6.5 123.0 %all-gather.2.cloned.1.call-start = ((), (), s32[]{:S(2)}) async-start(), calls=%async_computation | async-start | bytes 4096000 | tf_op jit(solution)/shard_map/all_gather | solution.py:354
  7.3 258.4 %all-reduce.2.cloned.1.call-start = ((), (), s32[]{:S(2)}) async-start(), calls=%async_computation.1 | async-start | bytes 5242880 | tf_op jit(solution)/shard_map/psum | solution.py:379
  7.3 6.3 %copy-start.1 = (bf16[1024,1280]{1,0:T(8,128)(2,1)S(1)}, bf16[1024,1280]{1,0:T(8,128)(2,1)}, u32[]{:S(2)}) copy-start(bf16[1024,1280]{1,0:T(8,128)(2,1)} %tokens_ref.1) | copy-start | bytes 7864324
  7.3 6.3 %copy-start.16 = (bf16[1280,3,320]{0,2,1:T(8,128)(2,1)S(1)}, bf16[1280,3,320]{0,2,1:T(8,128)(2,1)}, u32[]{:S(2)}) copy-start(bf16[1280,3,320]{0,2,1:T(8,128)(2,1)} %param.15) | copy-start | bytes 7372804
  17.1 8.6 %copy-start.13 = (s32[1024]{0:T(1024)S(1)}, s32[1024]{0:T(1024)}, u32[]{:S(2)}) copy-start(s32[1024]{0:T(1024)} %param.13) | copy-start | bytes 12292
  17.1 9.6 %copy-start.14 = (bf16[1280]{0:T(1024)(128)(2,1)S(1)}, bf16[1280]{0:T(1024)(128)(2,1)}, u32[]{:S(2)}) copy-start(bf16[1280]{0:T(1024)(128)(2,1)} %param.17) | copy-start | bytes 7684
  25.7 1.0 copy-start.10
  88.0 1.1 copy-start.3
  89.1 1.0 copy-start.4
  90.2 1.9 copy-start.5
  128.6 0.9 copy-start.7
  129.5 1.7 copy-start.2
  131.2 1.1 copy-start.8
  170.5 1.6 copy-start.6
  172.1 20.3 %copy-start.12 = (bf16[1280]{0:T(1024)(128)(2,1)S(1)}, bf16[1280]{0:T(1024)(128)(2,1)}, u32[]{:S(2)}) copy-start(bf16[1280]{0:T(1024)(128)(2,1)} %param.20) | copy-start | bytes 7684
  172.1 20.3 %copy-start.11 = (s32[256,1]{0,1:T(1,128)S(1)}, s32[256,1]{0,1:T(1,128)}, u32[]{:S(2)}) copy-start(s32[256,1]{0,1:T(1,128)} %param.23) | copy-start | bytes 3076
  172.1 21.4 %copy-start.15 = (s32[256,4]{0,1:T(4,128)S(1)}, s32[256,4]{0,1:T(4,128)}, u32[]{:S(2)}) copy-start(s32[256,4]{0,1:T(4,128)} %param.22) | copy-start | bytes 12292
  265.7 4.0 %copy-start.9 = (bf16[1024,1280]{1,0:T(8,128)(2,1)S(1)}, bf16[1024,1280]{1,0:T(8,128)(2,1)}, u32[]{:S(2)}) copy-start(bf16[1024,1280]{1,0:T(8,128)(2,1)} %all-reduce.2.cloned.1.call-done) | copy-start | bytes 7864324
  265.7 7.8 %slice-start = ((s8[5242880]{0:T(1024)(128)(4,1)}), s8[4194304]{0:T(1024)(128)(4,1)S(1)}, s32[]{:S(2)}) async-start(s8[5242880]{0:T(1024)(128)(4,1)} %bitcast.73), calls=%async_computation.2 | async-start | bytes 8388608
  269.7 3.8 %slice-start.1 = ((s8[5242880]{0:T(1024)(128)(4,1)}), s8[1048576]{0:T(1024)(128)(4,1)S(1)}, s32[]{:S(2)}) async-start(s8[5242880]{0:T(1024)(128)(4,1)} %bitcast.73), calls=%async_computation.3 | async-start | bytes 2097152
Sparse Core Ops, SparseCore 0:
  9.0 43.8 all-gather.1
  192.5 73.1 all-reduce.1

commit v14 on v9

--- a/solution.py
+++ b/solution.py
@@ -311,7 +311,9 @@
         jnp.zeros((heads, rows, width), jnp.float32),
     )
     _, total, weighted = lax.fori_loop(bounds[0, i], bounds[1, i], step, init)
-    o_ref[...] = (weighted / total).astype(o_ref.dtype)
+    result = (weighted / total).astype(o_ref.dtype)
+    for h in range(heads):
+        o_ref[:, h * width : (h + 1) * width] = result[h]
 
 
 def attention(queries, query_marks, keys, values, key_marks):
@@ -327,7 +329,7 @@
     bounds = jnp.stack([first // TILE, last // TILE + 1]).astype(jnp.int32)
     return pl.pallas_call(
         flash_kernel,
-        out_shape=jax.ShapeDtypeStruct(queries.shape, queries.dtype),
+        out_shape=jax.ShapeDtypeStruct((rows, heads * width), queries.dtype),
         grid_spec=pltpu.PrefetchScalarGridSpec(
             num_scalar_prefetch=1,
             grid=(tiles,),
@@ -338,7 +340,7 @@
                 pl.BlockSpec((heads, key_rows, width), lambda i, b: (0, 0, 0)),
                 pl.BlockSpec((1, key_rows), lambda i, b: (0, 0)),
             ],
-            out_specs=pl.BlockSpec((heads, TILE, width), lambda i, b: (0, i, 0)),
+            out_specs=pl.BlockSpec((TILE, heads * width), lambda i, b: (i, 0)),
         ),
         compiler_params=pltpu.CompilerParams(vmem_limit_bytes=48 * 1024 * 1024),
         cost_estimate=pl.CostEstimate(
@@ -368,7 +370,8 @@
     head_width = attend_weight.shape[2]
     head_count = head_width // HD
     full_weight = lax.all_gather(output_weight, "tp", axis=0, tiled=True)
-    attend_in = norm_rows([tokens], attend_gain)
+    stream = tokens.astype(jnp.float32)
+    attend_in = layer_norm(stream, attend_gain).astype(jnp.bfloat16)
     projected = jnp.dot(
         attend_in,
         attend_weight.reshape(attend_weight.shape[0], 3 * head_width),
@@ -386,7 +389,6 @@
         order,
     )
     context = attention(by_head(projected[:, :head_width]), marks, keys_all, values_all, key_marks)
-    context = jnp.transpose(context, (1, 0, 2)).reshape(token_rows, head_width)
     middle, mixer_in = project(context, full_weight, tokens, mixer_gain, order)
     expanded = jax.nn.gelu(
         jnp.dot(mixer_in, expand_weight, preferred_element_type=jnp.float32), approximate=False

time: 311 us -> 304 us (0.977)
  other arithmetic: 1.98 us -> 8.24 us
  local copies, waits for them, and re-layouts: 26.8 us -> 20.8 us
  Pallas kernels: 165 us -> 161 us
    reduce_sum x0 -> x2, other arithmetic: none -> 5.37 us  [the longest x1 2.81 us: layer_norm(): center = jnp.mean(stream, axis=-1, keepdims=True)]
    pallas_call x2 -> x1, Pallas kernels: 10.6 us -> 5.82 us  [norm_rows(): pl.pallas_call(norm_kernel, out_shape=jax.ShapeDtypeStruct((rows, cols),...]
    pallas_call x1, Pallas kernels: 40.3 us -> 45 us  [project(): pl.pallas_call(functools.partial(project_kernel, order), out_shape=(jax.S...]
    pallas_call x1, Pallas kernels: 39.4 us -> 35.4 us  [attention(): pl.pallas_call(flash_kernel, out_shape=jax.ShapeDtypeStruct((rows, heads...]
    unnamed x29 -> x33, local copies, waits for them, and re-layouts: 11.3 us -> 11.2 us
  transfers between devices with their start and end apart: 2 -> 2, of which waited for: 1 -> 1; matrix products, arithmetic and copies ran while one was open for 7% -> 6% of each run, Pallas kernels for 34% -> 31%
where the time goes in v14:
time: 304 us
  Pallas kernels  161 us (53%)
  waiting for transfers between devices  66.4 us (22%)
  matrix products  33.8 us (11%)
  local copies, waits for them, and re-layouts  20.8 us (7%)
  between operations  13.6 us (4%)
  other arithmetic  8.24 us (3%)
    psum x1, waiting for transfers between devices, body(): lax.psum(hidden_terms.astype(jnp.bfloat16), 'tp')  65.6 us
    pallas_call x1, Pallas kernels, exchange(): pl.pallas_call(functools.partial(exchange_kernel, order, n), out_shape=(j...  60 us
    pallas_call x1, Pallas kernels, project(): pl.pallas_call(functools.partial(project_kernel, order), out_shape=(jax.S...  45 us
    pallas_call x1, Pallas kernels, attention(): pl.pallas_call(flash_kernel, out_shape=jax.ShapeDtypeStruct((rows, heads...  35.4 us
    dot_general x1, matrix products, body(): jnp.dot(expanded, reduce_weight, preferred_element_type=jnp.float32)  20.1 us
    pallas_call x1, Pallas kernels, deliver(): pl.pallas_call(functools.partial(deliver_kernel, order, n), out_shape=jax...  14.6 us
    unnamed x33, local copies, waits for them, and re-layouts  11.2 us
  transfers between devices with their start and end apart: 2, of which 1 were waited for; matrix products, arithmetic and copies ran while one was open for 6% of the time, Pallas kernels for 31%

profile of v14, /device:TPU:1, one launch (start us, length us, event | category | flops | bytes accessed | tf_op | source)
XLA Modules:
  0.0 303.7 jit_solution(1473848250550629897)
XLA Ops:
  6.5 0.7 all-gather.2.cloned.1.call-update
  7.3 0.9 convert_element_type.36
  8.2 2.8 convert_reduce_fusion
  11.0 2.6 fusion.2
  13.6 2.9 fusion.57
  16.5 1.3 fusion.106
  17.9 2.2 copy.22
  20.1 2.3 copy.23
  22.4 1.1 copy.24.qm_ref
  23.4 60.0 %shard_map.118 = (bf16[4,80,5120]{2,1,0:T(8,128)(2,1)}, bf16[4,5120,80]{2,1,0:T(8,128)(2,1)}, s32[1,5120]{1,0:T(1,128)}) custom-call(bf16[4,80,1024]{2,1,0:T(8,128)(2,1)} %bitcast.77, bf16[4,1024,80]{2,1,0:T(8,128)(2,1)} %bitcast.76, s32[1,1024]{1,0:T(1,128)} %bitcast.83), custom_call_target="tpu_custom_call" | custom-call | tf_op jit(solution)/shard_map/pallas_call | solution.py:152
  83.6 0.8 and_select_fusion.km_ref
  84.4 0.3 select_reduce_fusion.1
  84.7 1.2 copy-done.3
  86.0 1.0 copy-done.4
  87.0 1.9 copy-done.5
  88.9 35.4 %shard_map.119.ctx_ref = bf16[1024,320]{1,0:T(8,128)(2,1)S(1)} custom-call(s32[2,4]{1,0:T(2,128)S(1)} %pad_add_fusion.bounds, bf16[4,1024,80]{2,1,0:T(8,128)(2,1)S(1)} %bitcast.74, s32[1024,1]{1,0:T(8,128)S(1)} %copy-done.4, bf16[4,80,5120]{2,1,0:T(8,128)(2,1)S(1)} %copy-done.5, bf16[4,5120,80]{2,1,0:T(8,128)(2,1)} %get-tuple-element.12.v_ref, ...), custom_call_target="tpu_custom_call" | custom-call | flops 2684354560 | bytes 7864320 | tf_op jit(solution)/shard_map/pallas_call | solution.py:330
  124.4 0.9 copy-done.7
  125.2 1.7 copy-done.2
  127.0 1.1 copy-done.8
  128.1 45.0 %shard_map.120 = (f32[1024,1280]{1,0:T(8,128)}, bf16[1024,1280]{1,0:T(8,128)(2,1)S(1)}) custom-call(bf16[1024,320]{1,0:T(8,128)(2,1)S(1)} %copy-done.8, bf16[1280,1280]{1,0:T(8,128)(2,1)} %all-gather.2.cloned.1.call-done.weight_ref, bf16[1024,1280]{1,0:T(8,128)(2,1)S(1)} %copy-done.2, bf16[1,1280]{1,0:T(2,128)(2,1)S(1)} %reshape.231.gain_ref), custom_call_target="tpu_custom_call" | custom-call | flops 3355443200 | bytes 13762560 | tf_op jit(solution)/shard_map/pallas_call | solution.py:243
  173.1 1.5 copy-done.6
  174.6 20.1 %convolution_convert_fusion = bf16[1024,1280]{1,0:T(8,128)(2,1)} fusion(bf16[1280,1280]{1,0:T(8,128)(2,1)S(1)} %copy-done, bf16[1024,1280]{1,0:T(8,128)(2,1)} %copy-done.6, bf16[1280,1280]{1,0:T(8,128)(2,1)} %param.18), kind=kOutput, calls=%fused_computation.29 | convolution fusion | flops 6797393920 | bytes 11796480 | tf_op jit(solution)/shard_map/dot_general | solution.py:396
  194.7 0.6 reshape.232.refs_2_
  195.3 0.6 reduce-window.6
  195.9 0.2 slice_reduce_fusion
  196.3 65.6 %all-reduce.2.cloned.1.call-done.refs_1_ = bf16[1024,1280]{1,0:T(8,128)(2,1)} async-done(((bf16[1024,1280]{1,0:T(8,128)(2,1)}), bf16[1024,1280]{1,0:T(8,128)(2,1)}) %all-reduce.2.cloned.1.call-update) | async-done | bytes 2621456 | tf_op jit(solution)/shard_map/psum | solution.py:397
  261.9 5.8 %shard_map.121 = bf16[1024,1280]{1,0:T(8,128)(2,1)} custom-call(f32[1024,1280]{1,0:T(8,128)} %get-tuple-element.13.refs_0_, bf16[1024,1280]{1,0:T(8,128)(2,1)} %all-reduce.2.cloned.1.call-done.refs_1_, bf16[1,1280]{1,0:T(2,128)(2,1)} %reshape.232.refs_2_), custom_call_target="tpu_custom_call" | custom-call | tf_op jit(solution)/shard_map/pallas_call | solution.py:231
  267.8 6.1 %fusion.16 = bf16[256,4,1280]{2,0,1:T(8,128)(2,1)} fusion(bf16[1024,1280]{1,0:T(8,128)(2,1)} %shard_map.121, s32[256,4]{0,1:T(4,128)S(1)} %broadcast_subtract_fusion), kind=kOutput, calls=%fused_computation.28 | convolution fusion | flops 2686713856 | bytes 5246976 | tf_op jit(solution)/shard_map/mkt,tc->mkc/dot_general | solution.py:401
  273.8 4.8 %convolution_convert_fusion.1 = bf16[512,320]{0,1:T(8,128)(2,1)} fusion(bf16[256,4,1280]{2,0,1:T(8,128)(2,1)} %fusion.16, bf16[40,4,8,1280]{3,2,1,0:T(8,128)(2,1)} %bitcast.88, s32[256]{0:T(256)S(1)} %bitcast.87), kind=kOutput, calls=%fused_computation.69 | convolution fusion | flops 923123712 | bytes 6226944 | tf_op jit(solution)/shard_map/ms,mc->sc/dot_general | solution.py:419
  278.6 1.9 copy.26
  280.5 14.6 %shard_map.122 = bf16[32,16,320]{2,1,0:T(8,128)(2,1)} custom-call(bf16[32,16,320]{2,1,0:T(8,128)(2,1)} %bitcast.81), custom_call_target="tpu_custom_call" | custom-call | tf_op jit(solution)/shard_map/pallas_call | solution.py:206
  295.0 1.8 copy.42
  (43 shorter events, 0.5 us)
Async XLA Ops:
  6.5 168.1 %copy-start = (bf16[1280,1280]{1,0:T(8,128)(2,1)S(1)}, bf16[1280,1280]{1,0:T(8,128)(2,1)}, u32[]{:S(2)}) copy-start(bf16[1280,1280]{1,0:T(8,128)(2,1)} %param.19) | copy-start | bytes 9830404
  6.5 118.7 %all-gather.2.cloned.1.call-start = ((), (), s32[]{:S(2)}) async-start(), calls=%async_computation | async-start | bytes 4096000 | tf_op jit(solution)/shard_map/all_gather | solution.py:372
  7.3 254.7 %all-reduce.2.cloned.1.call-start = ((), (), s32[]{:S(2)}) async-start(), calls=%async_computation.1 | async-start | bytes 5242880 | tf_op jit(solution)/shard_map/psum | solution.py:397
  7.3 6.3 %copy-start.1 = (bf16[1024,1280]{1,0:T(8,128)(2,1)S(1)}, bf16[1024,1280]{1,0:T(8,128)(2,1)}, u32[]{:S(2)}) copy-start(bf16[1024,1280]{1,0:T(8,128)(2,1)} %tokens_ref.1) | copy-start | bytes 7864324
  7.3 6.3 %copy-start.15 = (bf16[1280,3,320]{0,2,1:T(8,128)(2,1)S(1)}, bf16[1280,3,320]{0,2,1:T(8,128)(2,1)}, u32[]{:S(2)}) copy-start(bf16[1280,3,320]{0,2,1:T(8,128)(2,1)} %param.15) | copy-start | bytes 7372804
  16.5 3.6 %copy-start.11 = (s32[1024]{0:T(1024)S(1)}, s32[1024]{0:T(1024)}, u32[]{:S(2)}) copy-start(s32[1024]{0:T(1024)} %param.13) | copy-start | bytes 12292
  16.5 6.9 %copy-start.12 = (bf16[1280]{0:T(1024)(128)(2,1)S(1)}, bf16[1280]{0:T(1024)(128)(2,1)}, u32[]{:S(2)}) copy-start(bf16[1280]{0:T(1024)(128)(2,1)} %param.17) | copy-start | bytes 7684
  20.1 3.3 %copy-start.9 = (s32[1024]{0:T(1024)}, s32[1024]{0:T(1024)S(1)}, u32[]{:S(2)}) copy-start(s32[1024]{0:T(1024)S(1)} %broadcast_add_fusion) | copy-start | bytes 12292
  84.7 1.2 copy-start.3
  86.0 1.0 copy-start.4
  87.0 1.9 copy-start.5
  124.4 0.9 copy-start.7
  125.2 1.7 copy-start.2
  127.0 1.1 copy-start.8
  173.1 1.5 copy-start.6
  174.6 20.1 %copy-start.13 = (bf16[1280]{0:T(1024)(128)(2,1)S(1)}, bf16[1280]{0:T(1024)(128)(2,1)}, u32[]{:S(2)}) copy-start(bf16[1280]{0:T(1024)(128)(2,1)} %param.20) | copy-start | bytes 7684
  174.6 20.7 %copy-start.10 = (s32[256,1]{0,1:T(1,128)S(1)}, s32[256,1]{0,1:T(1,128)}, u32[]{:S(2)}) copy-start(s32[256,1]{0,1:T(1,128)} %param.23) | copy-start | bytes 3076
  174.6 21.7 %copy-start.14 = (s32[256,4]{0,1:T(4,128)S(1)}, s32[256,4]{0,1:T(4,128)}, u32[]{:S(2)}) copy-start(s32[256,4]{0,1:T(4,128)} %param.22) | copy-start | bytes 12292
Sparse Core Ops, SparseCore 0:
  9.0 43.8 all-gather.1
  194.8 67.0 all-reduce.1

commit v15 on v14

--- a/solution.py
+++ b/solution.py
@@ -10,6 +10,7 @@
 
 HD = 80
 TILE = 256
+WIDE = 640
 NEAR = (1, -1, 2, -2)
 MESH_IDS = pl.DeviceIdType.MESH
 
@@ -54,9 +55,9 @@
         def _(i):
             r = pl.ds(pl.multiple_of(i * tile, tile), tile)
 
-            @pl.loop(0, cols // tile)
+            @pl.loop(0, cols // WIDE)
             def _(j):
-                c = pl.ds(pl.multiple_of(j * tile, tile), tile)
+                c = pl.ds(pl.multiple_of(j * WIDE, WIDE), WIDE)
                 term = jnp.dot(
                     block[r, :], weight_ref[pl.ds(base, width), c], preferred_element_type=jnp.float32
                 )

time: 304 us -> 298 us (0.980)
  Pallas kernels: 161 us -> 153 us
    pallas_call x1, Pallas kernels: 45 us -> 40 us  [project(): pl.pallas_call(functools.partial(project_kernel, order), out_shape=(jax.S...]
where the time goes in v15:
time: 298 us; the launch traced here: 297 us
  Pallas kernels  153 us (51%)
  waiting for transfers between devices  67.3 us (23%)
  matrix products  33.8 us (11%)
  local copies, waits for them, and re-layouts  20.8 us (7%)
  between operations  13.6 us (5%)
  other arithmetic  8.24 us (3%)
    psum x1, waiting for transfers between devices, body(): lax.psum(hidden_terms.astype(jnp.bfloat16), 'tp')  66.5 us
    pallas_call x1, Pallas kernels, exchange(): pl.pallas_call(functools.partial(exchange_kernel, order, n), out_shape=(j...  60 us
    pallas_call x1, Pallas kernels, project(): pl.pallas_call(functools.partial(project_kernel, order), out_shape=(jax.S...  40 us
    pallas_call x1, Pallas kernels, attention(): pl.pallas_call(flash_kernel, out_shape=jax.ShapeDtypeStruct((rows, heads...  32.8 us
    dot_general x1, matrix products, body(): jnp.dot(expanded, reduce_weight, preferred_element_type=jnp.float32)  20.1 us
    pallas_call x1, Pallas kernels, deliver(): pl.pallas_call(functools.partial(deliver_kernel, order, n), out_shape=jax...  14.6 us
    unnamed x33, local copies, waits for them, and re-layouts  11.2 us
    dot_general x1, matrix products, body(): jnp.einsum('mkt,tc->mkc', picks, final_normed, preferred_element_type=jnp...  6.05 us
  transfers between devices with their start and end apart: 2, of which 1 were waited for; matrix products, arithmetic and copies ran while one was open for 6% of the time, Pallas kernels for 31%

profile of v15, /device:TPU:1, one launch (start us, length us, event | category | flops | bytes accessed | tf_op | source)
XLA Modules:
  0.0 297.0 jit_solution(7832981975369132441)
XLA Ops:
  6.5 0.7 all-gather.2.cloned.1.call-update
  7.3 0.9 convert_element_type.36
  8.2 2.8 convert_reduce_fusion
  11.0 2.6 fusion.2
  13.6 2.9 fusion.57
  16.5 1.3 fusion.106
  17.9 2.2 copy.22
  20.1 2.3 copy.23
  22.4 1.1 copy.24.qm_ref
  23.4 60.0 %shard_map.118 = (bf16[4,80,5120]{2,1,0:T(8,128)(2,1)}, bf16[4,5120,80]{2,1,0:T(8,128)(2,1)}, s32[1,5120]{1,0:T(1,128)}) custom-call(bf16[4,80,1024]{2,1,0:T(8,128)(2,1)} %bitcast.77, bf16[4,1024,80]{2,1,0:T(8,128)(2,1)} %bitcast.76, s32[1,1024]{1,0:T(1,128)} %bitcast.83), custom_call_target="tpu_custom_call" | custom-call | tf_op jit(solution)/shard_map/pallas_call | solution.py:153
  83.6 0.8 and_select_fusion.km_ref
  84.4 0.3 select_reduce_fusion.1
  84.7 1.2 copy-done.3
  86.0 1.0 copy-done.4
  87.0 1.9 copy-done.5
  88.9 32.8 %shard_map.119.ctx_ref = bf16[1024,320]{1,0:T(8,128)(2,1)S(1)} custom-call(s32[2,4]{1,0:T(2,128)S(1)} %pad_add_fusion.bounds, bf16[4,1024,80]{2,1,0:T(8,128)(2,1)S(1)} %bitcast.74, s32[1024,1]{1,0:T(8,128)S(1)} %copy-done.4, bf16[4,80,5120]{2,1,0:T(8,128)(2,1)S(1)} %copy-done.5, bf16[4,5120,80]{2,1,0:T(8,128)(2,1)} %get-tuple-element.12.v_ref, ...), custom_call_target="tpu_custom_call" | custom-call | flops 2684354560 | bytes 7864320 | tf_op jit(solution)/shard_map/pallas_call | solution.py:331
  121.8 0.9 copy-done.7
  122.6 1.7 copy-done.2
  124.4 1.1 copy-done.8
  125.5 40.0 %shard_map.120 = (f32[1024,1280]{1,0:T(8,128)}, bf16[1024,1280]{1,0:T(8,128)(2,1)S(1)}) custom-call(bf16[1024,320]{1,0:T(8,128)(2,1)S(1)} %copy-done.8, bf16[1280,1280]{1,0:T(8,128)(2,1)} %all-gather.2.cloned.1.call-done.weight_ref, bf16[1024,1280]{1,0:T(8,128)(2,1)S(1)} %copy-done.2, bf16[1,1280]{1,0:T(2,128)(2,1)S(1)} %reshape.231.gain_ref), custom_call_target="tpu_custom_call" | custom-call | flops 3355443200 | bytes 13762560 | tf_op jit(solution)/shard_map/pallas_call | solution.py:244
  165.5 1.5 copy-done.6
  167.0 20.1 %convolution_convert_fusion = bf16[1024,1280]{1,0:T(8,128)(2,1)} fusion(bf16[1280,1280]{1,0:T(8,128)(2,1)S(1)} %copy-done, bf16[1024,1280]{1,0:T(8,128)(2,1)} %copy-done.6, bf16[1280,1280]{1,0:T(8,128)(2,1)} %param.18), kind=kOutput, calls=%fused_computation.29 | convolution fusion | flops 6797393920 | bytes 11796480 | tf_op jit(solution)/shard_map/dot_general | solution.py:397
  187.2 0.6 reshape.232.refs_2_
  187.8 0.6 reduce-window.6
  188.4 0.2 slice_reduce_fusion
  188.7 66.5 %all-reduce.2.cloned.1.call-done.refs_1_ = bf16[1024,1280]{1,0:T(8,128)(2,1)} async-done(((bf16[1024,1280]{1,0:T(8,128)(2,1)}), bf16[1024,1280]{1,0:T(8,128)(2,1)}) %all-reduce.2.cloned.1.call-update) | async-done | bytes 2621456 | tf_op jit(solution)/shard_map/psum | solution.py:398
  255.3 5.8 %shard_map.121 = bf16[1024,1280]{1,0:T(8,128)(2,1)} custom-call(f32[1024,1280]{1,0:T(8,128)} %get-tuple-element.13.refs_0_, bf16[1024,1280]{1,0:T(8,128)(2,1)} %all-reduce.2.cloned.1.call-done.refs_1_, bf16[1,1280]{1,0:T(2,128)(2,1)} %reshape.232.refs_2_), custom_call_target="tpu_custom_call" | custom-call | tf_op jit(solution)/shard_map/pallas_call | solution.py:232
  261.1 6.1 %fusion.16 = bf16[256,4,1280]{2,0,1:T(8,128)(2,1)} fusion(bf16[1024,1280]{1,0:T(8,128)(2,1)} %shard_map.121, s32[256,4]{0,1:T(4,128)S(1)} %broadcast_subtract_fusion), kind=kOutput, calls=%fused_computation.28 | convolution fusion | flops 2686713856 | bytes 5246976 | tf_op jit(solution)/shard_map/mkt,tc->mkc/dot_general | solution.py:402
  267.1 4.8 %convolution_convert_fusion.1 = bf16[512,320]{0,1:T(8,128)(2,1)} fusion(bf16[256,4,1280]{2,0,1:T(8,128)(2,1)} %fusion.16, bf16[40,4,8,1280]{3,2,1,0:T(8,128)(2,1)} %bitcast.88, s32[256]{0:T(256)S(1)} %bitcast.87), kind=kOutput, calls=%fused_computation.69 | convolution fusion | flops 923123712 | bytes 6226944 | tf_op jit(solution)/shard_map/ms,mc->sc/dot_general | solution.py:420
  271.9 1.9 copy.26
  273.8 14.6 %shard_map.122 = bf16[32,16,320]{2,1,0:T(8,128)(2,1)} custom-call(bf16[32,16,320]{2,1,0:T(8,128)(2,1)} %bitcast.81), custom_call_target="tpu_custom_call" | custom-call | tf_op jit(solution)/shard_map/pallas_call | solution.py:207
  288.4 1.8 copy.42
  (43 shorter events, 0.5 us)
Async XLA Ops:
  6.5 160.5 %copy-start = (bf16[1280,1280]{1,0:T(8,128)(2,1)S(1)}, bf16[1280,1280]{1,0:T(8,128)(2,1)}, u32[]{:S(2)}) copy-start(bf16[1280,1280]{1,0:T(8,128)(2,1)} %param.19) | copy-start | bytes 9830404
  6.5 116.1 %all-gather.2.cloned.1.call-start = ((), (), s32[]{:S(2)}) async-start(), calls=%async_computation | async-start | bytes 4096000 | tf_op jit(solution)/shard_map/all_gather | solution.py:373
  7.3 248.0 %all-reduce.2.cloned.1.call-start = ((), (), s32[]{:S(2)}) async-start(), calls=%async_computation.1 | async-start | bytes 5242880 | tf_op jit(solution)/shard_map/psum | solution.py:398
  7.3 6.3 %copy-start.1 = (bf16[1024,1280]{1,0:T(8,128)(2,1)S(1)}, bf16[1024,1280]{1,0:T(8,128)(2,1)}, u32[]{:S(2)}) copy-start(bf16[1024,1280]{1,0:T(8,128)(2,1)} %tokens_ref.1) | copy-start | bytes 7864324
  7.3 6.3 %copy-start.15 = (bf16[1280,3,320]{0,2,1:T(8,128)(2,1)S(1)}, bf16[1280,3,320]{0,2,1:T(8,128)(2,1)}, u32[]{:S(2)}) copy-start(bf16[1280,3,320]{0,2,1:T(8,128)(2,1)} %param.15) | copy-start | bytes 7372804
  16.5 3.6 %copy-start.11 = (s32[1024]{0:T(1024)S(1)}, s32[1024]{0:T(1024)}, u32[]{:S(2)}) copy-start(s32[1024]{0:T(1024)} %param.13) | copy-start | bytes 12292
  16.5 6.9 %copy-start.12 = (bf16[1280]{0:T(1024)(128)(2,1)S(1)}, bf16[1280]{0:T(1024)(128)(2,1)}, u32[]{:S(2)}) copy-start(bf16[1280]{0:T(1024)(128)(2,1)} %param.17) | copy-start | bytes 7684
  20.1 3.3 %copy-start.9 = (s32[1024]{0:T(1024)}, s32[1024]{0:T(1024)S(1)}, u32[]{:S(2)}) copy-start(s32[1024]{0:T(1024)S(1)} %broadcast_add_fusion) | copy-start | bytes 12292
  84.7 1.2 copy-start.3
  86.0 1.0 copy-start.4
  87.0 1.9 copy-start.5
  121.8 0.9 copy-start.7
  122.6 1.7 copy-start.2
  124.4 1.1 copy-start.8
  165.5 1.5 copy-start.6
  167.0 20.1 %copy-start.13 = (bf16[1280]{0:T(1024)(128)(2,1)S(1)}, bf16[1280]{0:T(1024)(128)(2,1)}, u32[]{:S(2)}) copy-start(bf16[1280]{0:T(1024)(128)(2,1)} %param.20) | copy-start | bytes 7684
  167.0 20.7 %copy-start.10 = (s32[256,1]{0,1:T(1,128)S(1)}, s32[256,1]{0,1:T(1,128)}, u32[]{:S(2)}) copy-start(s32[256,1]{0,1:T(1,128)} %param.23) | copy-start | bytes 3076
  167.0 21.7 %copy-start.14 = (s32[256,4]{0,1:T(4,128)S(1)}, s32[256,4]{0,1:T(4,128)}, u32[]{:S(2)}) copy-start(s32[256,4]{0,1:T(4,128)} %param.22) | copy-start | bytes 12292
Sparse Core Ops, SparseCore 0:
  9.0 43.8 all-gather.1
  187.3 67.9 all-reduce.1

commit v16 on v15

--- a/solution.py
+++ b/solution.py
@@ -10,7 +10,7 @@
 
 HD = 80
 TILE = 256
-WIDE = 640
+WIDE = 1280
 NEAR = (1, -1, 2, -2)
 MESH_IDS = pl.DeviceIdType.MESH
 

time: 298 us -> 297 us (level)
    pallas_call x1, Pallas kernels: 40 us -> 34.1 us  [project(): pl.pallas_call(functools.partial(project_kernel, order), out_shape=(jax.S...]
    pallas_call x1, Pallas kernels: 32.8 us -> 36.3 us  [attention(): pl.pallas_call(flash_kernel, out_shape=jax.ShapeDtypeStruct((rows, heads...]
  transfers between devices with their start and end apart: 2 -> 2, of which waited for: 1 -> 1; matrix products, arithmetic and copies ran while one was open for 6% -> 6% of each run, Pallas kernels for 31% -> 33%
where the time goes in v16:
time: 297 us; the launch traced here: 296 us
  Pallas kernels  151 us (51%)
  waiting for transfers between devices  68.1 us (23%)
  matrix products  33.9 us (11%)
  local copies, waits for them, and re-layouts  20.8 us (7%)
  between operations  13.6 us (5%)
  other arithmetic  8.24 us (3%)
    psum x1, waiting for transfers between devices, body(): lax.psum(hidden_terms.astype(jnp.bfloat16), 'tp')  67.4 us
    pallas_call x1, Pallas kernels, exchange(): pl.pallas_call(functools.partial(exchange_kernel, order, n), out_shape=(j...  60 us
    pallas_call x1, Pallas kernels, attention(): pl.pallas_call(flash_kernel, out_shape=jax.ShapeDtypeStruct((rows, heads...  36.3 us
    pallas_call x1, Pallas kernels, project(): pl.pallas_call(functools.partial(project_kernel, order), out_shape=(jax.S...  34.1 us
    dot_general x1, matrix products, body(): jnp.dot(expanded, reduce_weight, preferred_element_type=jnp.float32)  20.2 us
    pallas_call x1, Pallas kernels, deliver(): pl.pallas_call(functools.partial(deliver_kernel, order, n), out_shape=jax...  14.6 us
    unnamed x33, local copies, waits for them, and re-layouts  11.2 us
    dot_general x1, matrix products, body(): jnp.einsum('mkt,tc->mkc', picks, final_normed, preferred_element_type=jnp...  6.05 us
  transfers between devices with their start and end apart: 2, of which 1 were waited for; matrix products, arithmetic and copies ran while one was open for 6% of the time, Pallas kernels for 33%

profile of v16, /device:TPU:1, one launch (start us, length us, event | category | flops | bytes accessed | tf_op | source)
XLA Modules:
  0.0 295.5 jit_solution(5626076575811710255)
XLA Ops:
  6.5 0.7 all-gather.2.cloned.1.call-update
  7.3 0.9 convert_element_type.36
  8.2 2.8 convert_reduce_fusion
  11.0 2.6 fusion.2
  13.6 2.9 fusion.57
  16.5 1.3 fusion.106
  17.9 2.2 copy.22
  20.1 2.3 copy.23
  22.4 1.1 copy.24.qm_ref
  23.4 60.0 %shard_map.118 = (bf16[4,80,5120]{2,1,0:T(8,128)(2,1)}, bf16[4,5120,80]{2,1,0:T(8,128)(2,1)}, s32[1,5120]{1,0:T(1,128)}) custom-call(bf16[4,80,1024]{2,1,0:T(8,128)(2,1)} %bitcast.77, bf16[4,1024,80]{2,1,0:T(8,128)(2,1)} %bitcast.76, s32[1,1024]{1,0:T(1,128)} %bitcast.83), custom_call_target="tpu_custom_call" | custom-call | tf_op jit(solution)/shard_map/pallas_call | solution.py:153
  83.6 0.8 and_select_fusion.km_ref
  84.4 0.3 select_reduce_fusion.1
  84.7 1.2 copy-done.3
  86.0 1.0 copy-done.4
  87.0 1.9 copy-done.5
  88.9 36.3 %shard_map.119.ctx_ref = bf16[1024,320]{1,0:T(8,128)(2,1)S(1)} custom-call(s32[2,4]{1,0:T(2,128)S(1)} %pad_add_fusion.bounds, bf16[4,1024,80]{2,1,0:T(8,128)(2,1)S(1)} %bitcast.74, s32[1024,1]{1,0:T(8,128)S(1)} %copy-done.4, bf16[4,80,5120]{2,1,0:T(8,128)(2,1)S(1)} %copy-done.5, bf16[4,5120,80]{2,1,0:T(8,128)(2,1)} %get-tuple-element.12.v_ref, ...), custom_call_target="tpu_custom_call" | custom-call | flops 2684354560 | bytes 7864320 | tf_op jit(solution)/shard_map/pallas_call | solution.py:331
  125.2 0.9 copy-done.7
  126.1 1.7 copy-done.2
  127.8 1.1 copy-done.8
  129.0 34.1 %shard_map.120 = (f32[1024,1280]{1,0:T(8,128)}, bf16[1024,1280]{1,0:T(8,128)(2,1)S(1)}) custom-call(bf16[1024,320]{1,0:T(8,128)(2,1)S(1)} %copy-done.8, bf16[1280,1280]{1,0:T(8,128)(2,1)} %all-gather.2.cloned.1.call-done.weight_ref, bf16[1024,1280]{1,0:T(8,128)(2,1)S(1)} %copy-done.2, bf16[1,1280]{1,0:T(2,128)(2,1)S(1)} %reshape.231.gain_ref), custom_call_target="tpu_custom_call" | custom-call | flops 3355443200 | bytes 13762560 | tf_op jit(solution)/shard_map/pallas_call | solution.py:244
  163.1 1.5 copy-done.6
  164.6 20.2 %convolution_convert_fusion = bf16[1024,1280]{1,0:T(8,128)(2,1)} fusion(bf16[1280,1280]{1,0:T(8,128)(2,1)S(1)} %copy-done, bf16[1024,1280]{1,0:T(8,128)(2,1)} %copy-done.6, bf16[1280,1280]{1,0:T(8,128)(2,1)} %param.18), kind=kOutput, calls=%fused_computation.29 | convolution fusion | flops 6797393920 | bytes 11796480 | tf_op jit(solution)/shard_map/dot_general | solution.py:397
  184.9 0.6 reshape.232.refs_2_
  185.5 0.6 reduce-window.6
  186.1 0.2 slice_reduce_fusion
  186.4 67.4 %all-reduce.2.cloned.1.call-done.refs_1_ = bf16[1024,1280]{1,0:T(8,128)(2,1)} async-done(((bf16[1024,1280]{1,0:T(8,128)(2,1)}), bf16[1024,1280]{1,0:T(8,128)(2,1)}) %all-reduce.2.cloned.1.call-update) | async-done | bytes 2621456 | tf_op jit(solution)/shard_map/psum | solution.py:398
  253.8 5.8 %shard_map.121 = bf16[1024,1280]{1,0:T(8,128)(2,1)} custom-call(f32[1024,1280]{1,0:T(8,128)} %get-tuple-element.13.refs_0_, bf16[1024,1280]{1,0:T(8,128)(2,1)} %all-reduce.2.cloned.1.call-done.refs_1_, bf16[1,1280]{1,0:T(2,128)(2,1)} %reshape.232.refs_2_), custom_call_target="tpu_custom_call" | custom-call | tf_op jit(solution)/shard_map/pallas_call | solution.py:232
  259.6 6.1 %fusion.16 = bf16[256,4,1280]{2,0,1:T(8,128)(2,1)} fusion(bf16[1024,1280]{1,0:T(8,128)(2,1)} %shard_map.121, s32[256,4]{0,1:T(4,128)S(1)} %broadcast_subtract_fusion), kind=kOutput, calls=%fused_computation.28 | convolution fusion | flops 2686713856 | bytes 5246976 | tf_op jit(solution)/shard_map/mkt,tc->mkc/dot_general | solution.py:402
  265.7 4.8 %convolution_convert_fusion.1 = bf16[512,320]{0,1:T(8,128)(2,1)} fusion(bf16[256,4,1280]{2,0,1:T(8,128)(2,1)} %fusion.16, bf16[40,4,8,1280]{3,2,1,0:T(8,128)(2,1)} %bitcast.88, s32[256]{0:T(256)S(1)} %bitcast.87), kind=kOutput, calls=%fused_computation.69 | convolution fusion | flops 923123712 | bytes 6226944 | tf_op jit(solution)/shard_map/ms,mc->sc/dot_general | solution.py:420
  270.4 1.9 copy.26
  272.3 14.6 %shard_map.122 = bf16[32,16,320]{2,1,0:T(8,128)(2,1)} custom-call(bf16[32,16,320]{2,1,0:T(8,128)(2,1)} %bitcast.81), custom_call_target="tpu_custom_call" | custom-call | tf_op jit(solution)/shard_map/pallas_call | solution.py:207
  286.9 1.8 copy.42
  (43 shorter events, 0.5 us)
Async XLA Ops:
  6.5 158.1 %copy-start = (bf16[1280,1280]{1,0:T(8,128)(2,1)S(1)}, bf16[1280,1280]{1,0:T(8,128)(2,1)}, u32[]{:S(2)}) copy-start(bf16[1280,1280]{1,0:T(8,128)(2,1)} %param.19) | copy-start | bytes 9830404
  6.5 119.5 %all-gather.2.cloned.1.call-start = ((), (), s32[]{:S(2)}) async-start(), calls=%async_computation | async-start | bytes 4096000 | tf_op jit(solution)/shard_map/all_gather | solution.py:373
  7.3 246.5 %all-reduce.2.cloned.1.call-start = ((), (), s32[]{:S(2)}) async-start(), calls=%async_computation.1 | async-start | bytes 5242880 | tf_op jit(solution)/shard_map/psum | solution.py:398
  7.3 6.3 %copy-start.1 = (bf16[1024,1280]{1,0:T(8,128)(2,1)S(1)}, bf16[1024,1280]{1,0:T(8,128)(2,1)}, u32[]{:S(2)}) copy-start(bf16[1024,1280]{1,0:T(8,128)(2,1)} %tokens_ref.1) | copy-start | bytes 7864324
  7.3 6.3 %copy-start.15 = (bf16[1280,3,320]{0,2,1:T(8,128)(2,1)S(1)}, bf16[1280,3,320]{0,2,1:T(8,128)(2,1)}, u32[]{:S(2)}) copy-start(bf16[1280,3,320]{0,2,1:T(8,128)(2,1)} %param.15) | copy-start | bytes 7372804
  16.5 3.6 %copy-start.11 = (s32[1024]{0:T(1024)S(1)}, s32[1024]{0:T(1024)}, u32[]{:S(2)}) copy-start(s32[1024]{0:T(1024)} %param.13) | copy-start | bytes 12292
  16.5 6.9 %copy-start.12 = (bf16[1280]{0:T(1024)(128)(2,1)S(1)}, bf16[1280]{0:T(1024)(128)(2,1)}, u32[]{:S(2)}) copy-start(bf16[1280]{0:T(1024)(128)(2,1)} %param.17) | copy-start | bytes 7684
  20.1 3.3 %copy-start.9 = (s32[1024]{0:T(1024)}, s32[1024]{0:T(1024)S(1)}, u32[]{:S(2)}) copy-start(s32[1024]{0:T(1024)S(1)} %broadcast_add_fusion) | copy-start | bytes 12292
  84.7 1.2 copy-start.3
  86.0 1.0 copy-start.4
  87.0 1.9 copy-start.5
  125.2 0.9 copy-start.7
  126.1 1.7 copy-start.2
  127.8 1.1 copy-start.8
  163.1 1.5 copy-start.6
  164.6 20.3 %copy-start.13 = (bf16[1280]{0:T(1024)(128)(2,1)S(1)}, bf16[1280]{0:T(1024)(128)(2,1)}, u32[]{:S(2)}) copy-start(bf16[1280]{0:T(1024)(128)(2,1)} %param.20) | copy-start | bytes 7684
  164.6 20.9 %copy-start.10 = (s32[256,1]{0,1:T(1,128)S(1)}, s32[256,1]{0,1:T(1,128)}, u32[]{:S(2)}) copy-start(s32[256,1]{0,1:T(1,128)} %param.23) | copy-start | bytes 3076
  164.6 21.8 %copy-start.14 = (s32[256,4]{0,1:T(4,128)S(1)}, s32[256,4]{0,1:T(4,128)}, u32[]{:S(2)}) copy-start(s32[256,4]{0,1:T(4,128)} %param.22) | copy-start | bytes 12292
Sparse Core Ops, SparseCore 0:
  9.0 43.8 all-gather.1
  185.0 68.7 all-reduce.1

commit v17 on v16

--- a/solution.py
+++ b/solution.py
@@ -46,7 +46,7 @@
     pl.semaphore_wait(barrier, 2)
     right = send(ctx_ref, slots.at[1], 1, 1)
     left = send(ctx_ref, slots.at[3], 3, n - 1)
-    tile = 256
+    tile = 512
 
     def add_term(block, source, first):
         base = pl.multiple_of(source * width, 8)

time: 297 us -> 297 us (level)
  waiting for transfers between devices: 68.1 us -> 71.6 us
  Pallas kernels: 151 us -> 148 us
    pallas_call x1, Pallas kernels: 36.3 us -> 29.3 us  [attention(): pl.pallas_call(flash_kernel, out_shape=jax.ShapeDtypeStruct((rows, heads...]
    pallas_call x1, Pallas kernels: 34.1 us -> 37.7 us  [project(): pl.pallas_call(functools.partial(project_kernel, order), out_shape=(jax.S...]
    psum x1, waiting for transfers between devices: 67.4 us -> 70.9 us  [body(): lax.psum(hidden_terms.astype(jnp.bfloat16), 'tp')]
  transfers between devices with their start and end apart: 2 -> 2, of which waited for: 1 -> 1; matrix products, arithmetic and copies ran while one was open for 6% -> 6% of each run, Pallas kernels for 33% -> 30%
where the time goes in v17:
time: 297 us; the launch traced here: 296 us
  Pallas kernels  148 us (50%)
  waiting for transfers between devices  71.6 us (24%)
  matrix products  34 us (11%)
  local copies, waits for them, and re-layouts  20.8 us (7%)
  between operations  13.6 us (5%)
  other arithmetic  8.24 us (3%)
    psum x1, waiting for transfers between devices, body(): lax.psum(hidden_terms.astype(jnp.bfloat16), 'tp')  70.9 us
    pallas_call x1, Pallas kernels, exchange(): pl.pallas_call(functools.partial(exchange_kernel, order, n), out_shape=(j...  60 us
    pallas_call x1, Pallas kernels, project(): pl.pallas_call(functools.partial(project_kernel, order), out_shape=(jax.S...  37.7 us
    pallas_call x1, Pallas kernels, attention(): pl.pallas_call(flash_kernel, out_shape=jax.ShapeDtypeStruct((rows, heads...  29.3 us
    dot_general x1, matrix products, body(): jnp.dot(expanded, reduce_weight, preferred_element_type=jnp.float32)  20.2 us
    pallas_call x1, Pallas kernels, deliver(): pl.pallas_call(functools.partial(deliver_kernel, order, n), out_shape=jax...  14.6 us
    unnamed x33, local copies, waits for them, and re-layouts  11.2 us
    dot_general x1, matrix products, body(): jnp.einsum('mkt,tc->mkc', picks, final_normed, preferred_element_type=jnp...  6.05 us
  transfers between devices with their start and end apart: 2, of which 1 were waited for; matrix products, arithmetic and copies ran while one was open for 6% of the time, Pallas kernels for 30%

profile of v17, /device:TPU:1, one launch (start us, length us, event | category | flops | bytes accessed | tf_op | source)
XLA Modules:
  0.0 295.8 jit_solution(10179528972632626067)
XLA Ops:
  6.5 0.7 all-gather.2.cloned.1.call-update
  7.3 0.9 convert_element_type.36
  8.2 2.8 convert_reduce_fusion
  11.0 2.6 fusion.2
  13.6 2.9 fusion.57
  16.5 1.3 fusion.106
  17.9 2.2 copy.22
  20.1 2.3 copy.23
  22.4 1.1 copy.24.qm_ref
  23.4 60.0 %shard_map.118 = (bf16[4,80,5120]{2,1,0:T(8,128)(2,1)}, bf16[4,5120,80]{2,1,0:T(8,128)(2,1)}, s32[1,5120]{1,0:T(1,128)}) custom-call(bf16[4,80,1024]{2,1,0:T(8,128)(2,1)} %bitcast.77, bf16[4,1024,80]{2,1,0:T(8,128)(2,1)} %bitcast.76, s32[1,1024]{1,0:T(1,128)} %bitcast.83), custom_call_target="tpu_custom_call" | custom-call | tf_op jit(solution)/shard_map/pallas_call | solution.py:153
  83.6 0.8 and_select_fusion.km_ref
  84.4 0.3 select_reduce_fusion.1
  84.7 1.2 copy-done.3
  86.0 1.0 copy-done.4
  87.0 1.9 copy-done.5
  88.9 29.3 %shard_map.119.ctx_ref = bf16[1024,320]{1,0:T(8,128)(2,1)S(1)} custom-call(s32[2,4]{1,0:T(2,128)S(1)} %pad_add_fusion.bounds, bf16[4,1024,80]{2,1,0:T(8,128)(2,1)S(1)} %bitcast.74, s32[1024,1]{1,0:T(8,128)S(1)} %copy-done.4, bf16[4,80,5120]{2,1,0:T(8,128)(2,1)S(1)} %copy-done.5, bf16[4,5120,80]{2,1,0:T(8,128)(2,1)} %get-tuple-element.12.v_ref, ...), custom_call_target="tpu_custom_call" | custom-call | flops 2684354560 | bytes 7864320 | tf_op jit(solution)/shard_map/pallas_call | solution.py:331
  118.3 0.9 copy-done.7
  119.2 1.7 copy-done.2
  120.9 1.1 copy-done.8
  122.0 37.7 %shard_map.120 = (f32[1024,1280]{1,0:T(8,128)}, bf16[1024,1280]{1,0:T(8,128)(2,1)S(1)}) custom-call(bf16[1024,320]{1,0:T(8,128)(2,1)S(1)} %copy-done.8, bf16[1280,1280]{1,0:T(8,128)(2,1)} %all-gather.2.cloned.1.call-done.weight_ref, bf16[1024,1280]{1,0:T(8,128)(2,1)S(1)} %copy-done.2, bf16[1,1280]{1,0:T(2,128)(2,1)S(1)} %reshape.231.gain_ref), custom_call_target="tpu_custom_call" | custom-call | flops 3355443200 | bytes 13762560 | tf_op jit(solution)/shard_map/pallas_call | solution.py:244
  159.8 1.5 copy-done.6
  161.3 20.2 %convolution_convert_fusion = bf16[1024,1280]{1,0:T(8,128)(2,1)} fusion(bf16[1280,1280]{1,0:T(8,128)(2,1)S(1)} %copy-done, bf16[1024,1280]{1,0:T(8,128)(2,1)} %copy-done.6, bf16[1280,1280]{1,0:T(8,128)(2,1)} %param.18), kind=kOutput, calls=%fused_computation.29 | convolution fusion | flops 6797393920 | bytes 11796480 | tf_op jit(solution)/shard_map/dot_general | solution.py:397
  181.6 0.6 reshape.232.refs_2_
  182.2 0.6 reduce-window.6
  182.8 0.2 slice_reduce_fusion
  183.2 70.9 %all-reduce.2.cloned.1.call-done.refs_1_ = bf16[1024,1280]{1,0:T(8,128)(2,1)} async-done(((bf16[1024,1280]{1,0:T(8,128)(2,1)}), bf16[1024,1280]{1,0:T(8,128)(2,1)}) %all-reduce.2.cloned.1.call-update) | async-done | bytes 2621456 | tf_op jit(solution)/shard_map/psum | solution.py:398
  254.1 5.8 %shard_map.121 = bf16[1024,1280]{1,0:T(8,128)(2,1)} custom-call(f32[1024,1280]{1,0:T(8,128)} %get-tuple-element.13.refs_0_, bf16[1024,1280]{1,0:T(8,128)(2,1)} %all-reduce.2.cloned.1.call-done.refs_1_, bf16[1,1280]{1,0:T(2,128)(2,1)} %reshape.232.refs_2_), custom_call_target="tpu_custom_call" | custom-call | tf_op jit(solution)/shard_map/pallas_call | solution.py:232
  259.9 6.1 %fusion.16 = bf16[256,4,1280]{2,0,1:T(8,128)(2,1)} fusion(bf16[1024,1280]{1,0:T(8,128)(2,1)} %shard_map.121, s32[256,4]{0,1:T(4,128)S(1)} %broadcast_subtract_fusion), kind=kOutput, calls=%fused_computation.28 | convolution fusion | flops 2686713856 | bytes 5246976 | tf_op jit(solution)/shard_map/mkt,tc->mkc/dot_general | solution.py:402
  265.9 4.8 %convolution_convert_fusion.1 = bf16[512,320]{0,1:T(8,128)(2,1)} fusion(bf16[256,4,1280]{2,0,1:T(8,128)(2,1)} %fusion.16, bf16[40,4,8,1280]{3,2,1,0:T(8,128)(2,1)} %bitcast.88, s32[256]{0:T(256)S(1)} %bitcast.87), kind=kOutput, calls=%fused_computation.69 | convolution fusion | flops 923123712 | bytes 6226944 | tf_op jit(solution)/shard_map/ms,mc->sc/dot_general | solution.py:420
  270.7 1.9 copy.26
  272.6 14.6 %shard_map.122 = bf16[32,16,320]{2,1,0:T(8,128)(2,1)} custom-call(bf16[32,16,320]{2,1,0:T(8,128)(2,1)} %bitcast.81), custom_call_target="tpu_custom_call" | custom-call | tf_op jit(solution)/shard_map/pallas_call | solution.py:207
  287.2 1.8 copy.42
  (43 shorter events, 0.5 us)
Async XLA Ops:
  6.5 154.8 %copy-start = (bf16[1280,1280]{1,0:T(8,128)(2,1)S(1)}, bf16[1280,1280]{1,0:T(8,128)(2,1)}, u32[]{:S(2)}) copy-start(bf16[1280,1280]{1,0:T(8,128)(2,1)} %param.19) | copy-start | bytes 9830404
  6.5 112.6 %all-gather.2.cloned.1.call-start = ((), (), s32[]{:S(2)}) async-start(), calls=%async_computation | async-start | bytes 4096000 | tf_op jit(solution)/shard_map/all_gather | solution.py:373
  7.3 246.8 %all-reduce.2.cloned.1.call-start = ((), (), s32[]{:S(2)}) async-start(), calls=%async_computation.1 | async-start | bytes 5242880 | tf_op jit(solution)/shard_map/psum | solution.py:398
  7.3 6.3 %copy-start.1 = (bf16[1024,1280]{1,0:T(8,128)(2,1)S(1)}, bf16[1024,1280]{1,0:T(8,128)(2,1)}, u32[]{:S(2)}) copy-start(bf16[1024,1280]{1,0:T(8,128)(2,1)} %tokens_ref.1) | copy-start | bytes 7864324
  7.3 6.3 %copy-start.15 = (bf16[1280,3,320]{0,2,1:T(8,128)(2,1)S(1)}, bf16[1280,3,320]{0,2,1:T(8,128)(2,1)}, u32[]{:S(2)}) copy-start(bf16[1280,3,320]{0,2,1:T(8,128)(2,1)} %param.15) | copy-start | bytes 7372804
  16.5 3.6 %copy-start.11 = (s32[1024]{0:T(1024)S(1)}, s32[1024]{0:T(1024)}, u32[]{:S(2)}) copy-start(s32[1024]{0:T(1024)} %param.13) | copy-start | bytes 12292
  16.5 6.9 %copy-start.12 = (bf16[1280]{0:T(1024)(128)(2,1)S(1)}, bf16[1280]{0:T(1024)(128)(2,1)}, u32[]{:S(2)}) copy-start(bf16[1280]{0:T(1024)(128)(2,1)} %param.17) | copy-start | bytes 7684
  20.1 3.3 %copy-start.9 = (s32[1024]{0:T(1024)}, s32[1024]{0:T(1024)S(1)}, u32[]{:S(2)}) copy-start(s32[1024]{0:T(1024)S(1)} %broadcast_add_fusion) | copy-start | bytes 12292
  84.7 1.2 copy-start.3
  86.0 1.0 copy-start.4
  87.0 1.9 copy-start.5
  118.3 0.9 copy-start.7
  119.2 1.7 copy-start.2
  120.9 1.1 copy-start.8
  159.8 1.5 copy-start.6
  161.3 20.3 %copy-start.13 = (bf16[1280]{0:T(1024)(128)(2,1)S(1)}, bf16[1280]{0:T(1024)(128)(2,1)}, u32[]{:S(2)}) copy-start(bf16[1280]{0:T(1024)(128)(2,1)} %param.20) | copy-start | bytes 7684
  161.3 20.9 %copy-start.10 = (s32[256,1]{0,1:T(1,128)S(1)}, s32[256,1]{0,1:T(1,128)}, u32[]{:S(2)}) copy-start(s32[256,1]{0,1:T(1,128)} %param.23) | copy-start | bytes 3076
  161.3 21.8 %copy-start.14 = (s32[256,4]{0,1:T(4,128)S(1)}, s32[256,4]{0,1:T(4,128)}, u32[]{:S(2)}) copy-start(s32[256,4]{0,1:T(4,128)} %param.22) | copy-start | bytes 12292
Sparse Core Ops, SparseCore 0:
  9.0 43.8 all-gather.1
  181.7 72.3 all-reduce.1
